TPU v7x, 256 devices: a whole 4x4x8 slice. The times are simulated.
256 devices in a mesh: gx: 4 (over x), gy: 16 (over z_lo, y), gz: 4 (over z_hi, core).
Axes of the slice: x: 4, y: 4, z: 8 (z_hi: 2, z_lo: 4; z = z_hi * 4 + z_lo), core: 2. Of those that a mesh axis runs over, the one named last changes fastest.
Arguments:
- species: int32 [4, 16, 4, 256], P('gx', 'gy', 'gz'), may hold values from 0 to 7
- neighbour_index: int32 [4, 16, 4, 32, 256], P('gx', 'gy', 'gz'), may hold values from 0 to 639
- neighbour_count: int32 [4, 16, 4, 256], P('gx', 'gy', 'gz'), may hold values from 16 to 32, as said below
- edge_vectors: float32 [4, 16, 4, 3, 32, 256], P('gx', 'gy', 'gz'), as said below
- ghost_send: int32 [4, 16, 4, 3, 128], P('gx', 'gy', 'gz'), may hold values from 0 to 511, as said below
- brick_send: int32 [4, 16, 4, 512], P('gx', 'gy', 'gz'), may hold values from 0 to 639
- probe_index: int32 [4, 16, 4, 32, 512], P('gx', 'gy', 'gz'), may hold values from 0 to 511, as said below
- probe_count: int32 [4, 16, 4, 512], P('gx', 'gy', 'gz'), may hold values from 8 to 32, as said below
- probe_vectors: float32 [4, 16, 4, 3, 32, 512], P('gx', 'gy', 'gz'), as said below
- embedding: bfloat16 [8, 128], replicated, may hold values from -4 to 4
- message_one: bfloat16 [128, 128], replicated, may hold values from -0.5 to 0.5
- radial_in_one: bfloat16 [8, 64], replicated, may hold values from -2 to 2
- radial_out_one: bfloat16 [64, 512], replicated, may hold values from -0.75 to 0.75
- self_mix: bfloat16 [128, 128], replicated, may hold values from -0.5 to 0.5
- basis_mix: bfloat16 [512, 128], replicated, may hold values from -0.25 to 0.25
- message_two: bfloat16 [128, 128], replicated, may hold values from -0.5 to 0.5
- radial_in_two: bfloat16 [8, 64], replicated, may hold values from -2 to 2
- radial_out_two: bfloat16 [64, 512], replicated, may hold values from -0.75 to 0.75
- decoder: bfloat16 [4, 128, 8], replicated, may hold values from -0.5 to 0.5
Outputs:
- density: float32 [4, 16, 4, 512], P('gx', 'gy', 'gz')
Inputs may be any that keep to these rules, and one draw needn't show every extreme that they name: `neighbour_count`: each domain has an atom with all 32 slots live. `edge_vectors`: lengths lie between 0.8 and 5. `ghost_send`: section s entries index the first 256 + 2 s * 64 rows of the table. `probe_index`: an entry s * 32 + t refers to source s of the gy column, which lies at most 2 domains from the brick along gy (periodically); for each source and brick only t below a fixed live count (at least 16, all 32 from the brick's own domain) occurs. `probe_count`: each brick has a probe with all 32 slots live. `probe_vectors`: lengths lie between 0.5 and 4.
All inputs are finite; a program needn't handle non-finite values.
Results may differ from a plain program's by a relative error of at most 0.0064.
Values may be sent and summed in bfloat16 or wider, within the bound.
No kernel may reach another device: no remote copies, remote signals or barrier semaphores. Data moves between devices by JAX's collectives and lax.ppermute only.
A program may use at most 128 MiB of HBM per device.

v0:
```python
import math

import jax
import jax.numpy as jnp
from jax import lax
from jax.sharding import PartitionSpec as P

BASIS = 8


def padded(block, sides, width):
    for axis, dim in sides:
        count = lax.axis_size(axis)
        forward = [(i, i + 1) for i in range(count - 1)]
        forward.append((count - 1, 0))
        backward = [(target, source) for source, target in forward]
        low = lax.ppermute(
            lax.slice_in_dim(block, block.shape[dim] - width, None, axis=dim), axis, forward
        )
        high = lax.ppermute(lax.slice_in_dim(block, 0, width, axis=dim), axis, backward)
        block = jnp.concatenate([low, block, high], axis=dim)
    return block


def from_behind(block, axis, distance):
    devices = range(lax.axis_size(axis))
    route = [((i - distance) % len(devices), i) for i in devices]
    return lax.ppermute(block, axis, route)


def harmonics(vectors):
    radius = jnp.sqrt(vectors[0] * vectors[0] + vectors[1] * vectors[1] + vectors[2] * vectors[2])
    along_x = vectors[0] / radius
    along_y = vectors[1] / radius
    along_z = vectors[2] / radius
    ones_row = jnp.ones_like(radius)
    root_three = math.sqrt(3.0)
    root_fifteen = math.sqrt(15.0)
    root_five = math.sqrt(5.0)
    root_hundred = math.sqrt(105.0)
    root_seven = math.sqrt(7.0)
    outer_coef = math.sqrt(35.0 / 8.0)
    inner_coef = math.sqrt(21.0 / 8.0)
    rows_list = [
        ones_row,
        root_three * along_x,
        root_three * along_y,
        root_three * along_z,
        root_fifteen * along_x * along_y,
        root_fifteen * along_y * along_z,
        0.5 * root_five * (3.0 * along_z * along_z - 1.0),
        root_fifteen * along_x * along_z,
        0.5 * root_fifteen * (along_x * along_x - along_y * along_y),
        outer_coef * along_y * (3.0 * along_x * along_x - along_y * along_y),
        root_hundred * along_x * along_y * along_z,
        inner_coef * along_y * (5.0 * along_z * along_z - 1.0),
        0.5 * root_seven * along_z * (5.0 * along_z * along_z - 3.0),
        inner_coef * along_x * (5.0 * along_z * along_z - 1.0),
        0.5 * root_hundred * along_z * (along_x * along_x - along_y * along_y),
        outer_coef * along_x * (along_x * along_x - 3.0 * along_y * along_y),
    ]
    return (jnp.stack(rows_list), radius)


def radial_basis(radius, cutoff):
    scaled = radius / cutoff
    envelope = 1.0 - 28.0 * scaled**6 + 48.0 * scaled**7 - 21.0 * scaled**8
    order_grid = jnp.arange(1, BASIS + 1).astype(jnp.float32).reshape((BASIS,) + (1,) * radius.ndim)
    return (
        math.sqrt(2.0 / cutoff)
        * jnp.sin(order_grid * (math.pi / cutoff) * radius[None])
        / radius[None]
        * envelope[None]
    )


def layer_sums(ghost_table, slot_index, slot_count, vector_set, radial_in, radial_out):
    neigh_slots, atom_rows = slot_index.shape
    channels = ghost_table.shape[1]
    block_rows = 128 if atom_rows % 128 == 0 else atom_rows
    slot_ids = lax.iota(jnp.int32, neigh_slots)

    def layer_one_block(first_row):
        index_block = lax.dynamic_slice_in_dim(slot_index, first_row, block_rows, 1)
        count_block = lax.dynamic_slice_in_dim(slot_count, first_row, block_rows, 0)
        vector_block = lax.dynamic_slice_in_dim(vector_set, first_row, block_rows, 2)
        angular, radius = harmonics(vector_block)
        radial_values = radial_basis(radius, 5.0).astype(jnp.bfloat16)
        hidden = jax.nn.silu(
            jnp.einsum("nkb,nh->kbh", radial_values, radial_in, preferred_element_type=jnp.float32)
        ).astype(jnp.bfloat16)
        radial = jnp.einsum("kbh,hf->kbf", hidden, radial_out, preferred_element_type=jnp.float32)
        live_mask = (slot_ids[:, None] < count_block[None, :]).astype(jnp.float32)
        picked = (
            jnp.take(ghost_table, index_block, axis=0).astype(jnp.float32) * live_mask[:, :, None]
        )
        pieces = []
        for degree in range(4):
            weighted = radial[:, :, degree * channels : (degree + 1) * channels] * picked
            pieces.append(
                jnp.einsum(
                    "mkb,kbc->bmc",
                    angular[degree * degree : (degree + 1) * (degree + 1)],
                    weighted,
                    precision=lax.Precision.HIGHEST,
                )
            )
        return 0.25 * jnp.concatenate(pieces, axis=1)

    starts = (jnp.arange(atom_rows // block_rows) * block_rows).astype(jnp.int32)
    return lax.map(layer_one_block, starts).reshape(atom_rows, 16, channels)


def node_update(previous, sums, self_mix, basis_mix):
    pieces = [sums[:, 0, :]]
    for degree in (1, 2, 3):
        pieces.append(
            jnp.sum(sums[:, degree * degree : (degree + 1) * (degree + 1), :] ** 2, axis=1)
        )
    mixed_in = jnp.concatenate(pieces, axis=1).astype(jnp.bfloat16)
    summed = jnp.dot(previous, self_mix, preferred_element_type=jnp.float32) + jnp.dot(
        mixed_in, basis_mix, preferred_element_type=jnp.float32
    )
    return jax.nn.silu(summed).astype(jnp.bfloat16)


def coefficients(features, decoder):
    row_count = features.shape[0]
    pieces = []
    for degree in range(4):
        part_rows = features[:, degree * degree : (degree + 1) * (degree + 1), :]
        pieces.append(
            jnp.einsum(
                "rmc,cn->rmn", part_rows, decoder[degree], preferred_element_type=jnp.float32
            )
        )
    return jnp.concatenate(pieces, axis=1).astype(jnp.bfloat16).reshape(row_count, -1)


def density_of(received, slot_index, slot_count, vector_set):
    probe_slots, probe_rows = slot_index.shape
    block_rows = 512 if probe_rows % 512 == 0 else probe_rows
    slot_ids = lax.iota(jnp.int32, probe_slots)

    def density_one_block(first_row):
        index_block = lax.dynamic_slice_in_dim(slot_index, first_row, block_rows, 1)
        count_block = lax.dynamic_slice_in_dim(slot_count, first_row, block_rows, 0)
        vector_block = lax.dynamic_slice_in_dim(vector_set, first_row, block_rows, 2)
        angular, radius = harmonics(vector_block)
        radial_values = radial_basis(radius, 4.0)
        outer_basis = (
            angular.transpose(1, 2, 0)[:, :, :, None]
            * radial_values.transpose(1, 2, 0)[:, :, None, :]
        ).reshape(probe_slots, block_rows, -1)
        picked = jnp.take(received, index_block, axis=0).astype(jnp.float32)
        live_mask = (slot_ids[:, None] < count_block[None, :]).astype(jnp.float32)
        return 0.125 * jnp.sum(jnp.sum(outer_basis * picked, axis=2) * live_mask, axis=0)

    starts = (jnp.arange(probe_rows // block_rows) * block_rows).astype(jnp.int32)
    return lax.map(density_one_block, starts).reshape(probe_rows)


def extend(row_block, send_lists):
    ghost_rows = send_lists.shape[1] // 2
    ghost_table = row_block
    arrived = padded(jnp.take(ghost_table, send_lists[0], axis=0), (("gx", 0),), ghost_rows)
    ghost_table = jnp.concatenate(
        [ghost_table, arrived[:ghost_rows], arrived[3 * ghost_rows :]], axis=0
    )
    arrived = padded(jnp.take(ghost_table, send_lists[1], axis=0), (("gy", 0),), ghost_rows)
    ghost_table = jnp.concatenate(
        [ghost_table, arrived[:ghost_rows], arrived[3 * ghost_rows :]], axis=0
    )
    arrived = padded(jnp.take(ghost_table, send_lists[2], axis=0), (("gz", 0),), ghost_rows)
    return jnp.concatenate([ghost_table, arrived[:ghost_rows], arrived[3 * ghost_rows :]], axis=0)


def carry_table(row_block, send_lists):
    ghost_rows = send_lists.shape[1] // 2
    ghost_table = row_block
    arrived = padded(jnp.take(ghost_table, send_lists[0], axis=0), (("gx", 0),), ghost_rows)
    ghost_table = jnp.concatenate(
        [ghost_table, arrived[:ghost_rows], arrived[3 * ghost_rows :]], axis=0
    )
    arrived = padded(jnp.take(ghost_table, send_lists[1], axis=0), (("gy", 0),), ghost_rows)
    ghost_table = jnp.concatenate(
        [ghost_table, arrived[:ghost_rows], arrived[3 * ghost_rows :]], axis=0
    )
    arrived = padded(jnp.take(ghost_table, send_lists[2], axis=0), (("gz", 0),), ghost_rows)
    return jnp.concatenate([ghost_table, arrived[:ghost_rows], arrived[3 * ghost_rows :]], axis=0)


def shards(
    species,
    neighbour_index,
    neighbour_count,
    edge_vectors,
    ghost_send,
    brick_send,
    probe_index,
    probe_count,
    probe_vectors,
    embedding,
    message_one,
    radial_in_one,
    radial_out_one,
    self_mix,
    basis_mix,
    message_two,
    radial_in_two,
    radial_out_two,
    decoder,
):
    atom_species = species.reshape(-1)
    slot_index = neighbour_index.reshape(neighbour_index.shape[3:])
    slot_count = neighbour_count.reshape(-1)
    vector_set = edge_vectors.reshape(edge_vectors.shape[3:])
    send_lists = ghost_send.reshape(ghost_send.shape[3:])
    brick_list = brick_send.reshape(-1)
    probe_slots = probe_index.reshape(probe_index.shape[3:])
    probe_live = probe_count.reshape(-1)
    probe_set = probe_vectors.reshape(probe_vectors.shape[3:])
    onehot = (atom_species[:, None] == lax.iota(jnp.int32, embedding.shape[0])[None, :]).astype(
        jnp.bfloat16
    )
    start_h = jnp.dot(onehot, embedding, preferred_element_type=jnp.float32).astype(jnp.bfloat16)
    first_msg = jnp.dot(start_h, message_one, preferred_element_type=jnp.float32).astype(
        jnp.bfloat16
    )
    sums_one = layer_sums(
        extend(first_msg, send_lists),
        slot_index,
        slot_count,
        vector_set,
        radial_in_one,
        radial_out_one,
    )
    next_h = node_update(start_h, sums_one, self_mix, basis_mix)
    second_msg = jnp.dot(next_h, message_two, preferred_element_type=jnp.float32).astype(
        jnp.bfloat16
    )
    features = layer_sums(
        extend(second_msg, send_lists),
        slot_index,
        slot_count,
        vector_set,
        radial_in_two,
        radial_out_two,
    ).astype(jnp.bfloat16)
    coeff_table = carry_table(coefficients(features, decoder), send_lists)
    column_size = lax.axis_size("gy")
    here = lax.axis_index("gy")
    capacity = brick_list.shape[0] // column_size
    width = coeff_table.shape[1]

    def rows_for(step):
        target = (here + step + 4 * column_size) % column_size
        chosen = lax.dynamic_slice_in_dim(brick_list, target * capacity, capacity, 0)
        return jnp.take(coeff_table, chosen, axis=0)

    def place(received, piece, step):
        source = (here - step + 4 * column_size) % column_size
        return lax.dynamic_update_slice_in_dim(received, piece, source * capacity, 0)

    received = jnp.zeros((column_size * capacity, width), jnp.bfloat16)
    received = place(received, rows_for(0), 0)
    offsets = sorted(set((step % column_size for step in range(-2, 3))) - {0})
    for step in offsets:
        arrived = from_behind(rows_for(step), "gy", step)
        received = place(received, arrived, step)
    return density_of(received, probe_slots, probe_live, probe_set).reshape(1, 1, 1, -1)


def solution(mesh):
    placed = (
        P("gx", "gy", "gz", None),
        P("gx", "gy", "gz", None, None),
        P("gx", "gy", "gz", None),
        P("gx", "gy", "gz", None, None, None),
        P("gx", "gy", "gz", None, None),
        P("gx", "gy", "gz", None),
        P("gx", "gy", "gz", None, None),
        P("gx", "gy", "gz", None),
        P("gx", "gy", "gz", None, None, None),
        P(),
        P(),
        P(),
        P(),
        P(),
        P(),
        P(),
        P(),
        P(),
        P(),
    )
    return jax.shard_map(
        shards, mesh=mesh, in_specs=placed, out_specs=P("gx", "gy", "gz", None), check_vma=False
    )
```

profile of v0, /device:TPU:1, one launch (start us, length us, event | category | flops | bytes accessed | tf_op | source)
XLA Modules:
  0.0 399.8 jit_solution(6342340217267798942)
XLA Ops:
  3.5 2.1 collective-permute-start
  5.6 1.4 collective-permute-start.1
  7.8 1.5 compare_and_fusion.2
  15.4 2.6 divide_multiply_fusion
  19.5 1.5 collective-permute-start.2
  20.9 5.6 %collective-permute-start.3 = (bf16[64,128]{1,0:T(8,128)(2,1)S(1)}, bf16[64,128]{1,0:T(8,128)(2,1)S(1)}, u32[]{:S(2)}, u32[]{:S(2)}) collective-permute-start(bf16[64,128]{1,0:T(8,128)(2,1)S(1)} %get-tuple-element.520), channel_id=1, source_target_pairs={{4,0},{8,4},{12,8},{16,12},{20,16},{24,20},{28,24},{32,28},{36,32}... | collective-permute-start | bytes 49160 | tf_op jit(solution)/shard_map/ppermute | solution.py:20
  28.4 7.8 %collective-permute-start.4 = (bf16[64,128]{1,0:T(8,128)(2,1)S(1)}, bf16[64,128]{1,0:T(8,128)(2,1)S(1)}, u32[]{:S(2)}, u32[]{:S(2)}) collective-permute-start(bf16[64,128]{1,0:T(8,128)(2,1)S(1)} %get-tuple-element.519), channel_id=1, source_target_pairs={{0,1},{1,2},{2,3},{3,0},{4,5},{5,6},{6,7},{7,4},{8,9},{9,10},{10,1... | collective-permute-start | bytes 49160 | tf_op jit(solution)/shard_map/ppermute | solution.py:17
  37.1 6.2 %collective-permute-done.5 = bf16[64,128]{1,0:T(8,128)(2,1)S(1)} collective-permute-done((bf16[64,128]{1,0:T(8,128)(2,1)S(1)}, bf16[64,128]{1,0:T(8,128)(2,1)S(1)}, u32[]{:S(2)}, u32[]{:S(2)}) %collective-permute-start.5) | collective-permute-done | bytes 16416 | tf_op jit(solution)/shard_map/ppermute | solution.py:20
  43.4 109.0 %while.32 = (s32[]{:T(128)}, f32[2,128,16,128]{3,1,0,2:T(8,128)}, s32[2]{0:T(128)S(1)}, f32[3,32,256]{2,1,0:T(8,128)S(1)}, bf16[8,64]{1,0:T(8,128)(2,1)S(1)}, /*...) while((s32[]{:T(128)}, f32[2,128,16,128]{3,1,0,2:T(8,128)}, ...), condition=%wide.region_1.6_spmd.clone, body=%wide.region_0.5_spmd.clone.sunk | while | flops 379867168 | bytes 46235312 | solution.py:111
  48.1 5.2 %fusion.242 = f32[32,128,512]{2,1,0:T(8,128)} fusion(bf16[64,512]{1,0:T(8,128)(2,1)S(1)} %get-tuple-element.805, f32[32,128]{1,0:T(8,128)S(1)} %get-tuple-element.726, f32[32,128]{1,0:T(8,128)S(1)} %get-tuple-element.727, f32[8]{0:T(128)S(1)} %convert_multiply_fusion.7, bf16[8,64]{1,0:T(8,128)(2,1)S(1)} %get-tuple-element.804), kind=kOutput, calls=%fused_computation.39.clone.1 | convolution fusion | flops 274104320 | bytes 8487968 | tf_op jit(solution)/shard_map/while/body/eval_jaxpr/kbh,hf->kbf/dot_general | solution.py:92
  54.3 12.1 %gather_fusion = bf16[4096,128]{1,0:T(8,128)(2,1)S(1)} fusion(bf16[640,128]{1,0:T(8,128)(2,1)S(1)} %get-tuple-element.807, s32[4096]{0:T(1024)S(1)} %bitcast_clamp_fusion.4), kind=kCustom, calls=%fused_computation.3.clone.clone.1 | custom fusion | bytes 2113536 | tf_op jit(solution)/shard_map/while/body/eval_jaxpr/jit(_take)/gather | solution.py:95
  66.4 7.0 %slice_multiply_fusion.13 = (f32[32,128,128]{2,1,0:T(8,128)S(1)}, f32[32,128,128]{2,1,0:T(8,128)}, f32[32,128,128]{2,1,0:T(8,128)}, f32[32,128,128]{2,1,0:T(8,128)}) fusion(f32[32,128,512]{2,1,0:T(8,128)} %fusion.242, f32[32,128]{1,0:T(8,128)S(1)} %get-tuple-element.728, bf16[32,128,128]{2,1,0:T(8,128)(2,1)S(1)} %bitcast.241, ...), kind=kLoop, calls=%fused_computation.22.clone.1 | loop fusion | flops 3670016 | bytes 17846272 | tf_op jit(solution)/shard_map/while/body/eval_jaxpr/mul | solution.py:99
  75.9 1.2 copy.164
  77.0 4.4 %fusion.245 = f32[1,128,5,128]{3,2,1,0:T(8,128)S(1)} fusion(f32[5,32,128]{1,0,2:T(8,128)S(1)} %copy.164, f32[32,128,128]{2,1,0:T(8,128)} %get-tuple-element.732), kind=kOutput, calls=%fused_computation.32.clone.1 | convolution fusion | flops 31457280 | bytes 2506752 | tf_op jit(solution)/shard_map/while/body/eval_jaxpr/mkb,kbc->bmc/dot_general | solution.py:101
  82.5 4.6 %fusion.244 = f32[1,128,7,128]{3,2,1,0:T(8,128)S(1)} fusion(f32[7,32,128]{1,0,2:T(8,128)} %copy.163, f32[32,128,128]{2,1,0:T(8,128)} %get-tuple-element.730), kind=kOutput, calls=%fused_computation.33.clone.1 | convolution fusion | flops 44040192 | bytes 2670592 | tf_op jit(solution)/shard_map/while/body/eval_jaxpr/mkb,kbc->bmc/dot_general | solution.py:101
  88.7 4.5 %fusion.246 = f32[1,128,3,128]{3,2,1,0:T(4,128)S(1)} fusion(f32[3,32,128]{1,0,2:T(4,128)} %copy.165, f32[32,128,128]{2,1,0:T(8,128)} %get-tuple-element.736), kind=kOutput, calls=%fused_computation.34.clone.1 | convolution fusion | flops 18874368 | bytes 2342912 | tf_op jit(solution)/shard_map/while/body/eval_jaxpr/mkb,kbc->bmc/dot_general | solution.py:101
  93.3 2.8 fusion.247
  96.5 1.3 copy_dynamic-update-slice_fusion.2
  102.4 5.2 %fusion.242 = f32[32,128,512]{2,1,0:T(8,128)} fusion(bf16[64,512]{1,0:T(8,128)(2,1)S(1)} %get-tuple-element.805, f32[32,128]{1,0:T(8,128)S(1)} %get-tuple-element.726, f32[32,128]{1,0:T(8,128)S(1)} %get-tuple-element.727, f32[8]{0:T(128)S(1)} %convert_multiply_fusion.7, bf16[8,64]{1,0:T(8,128)(2,1)S(1)} %get-tuple-element.804), kind=kOutput, calls=%fused_computation.39.clone.1 | convolution fusion | flops 274104320 | bytes 8487968 | tf_op jit(solution)/shard_map/while/body/eval_jaxpr/kbh,hf->kbf/dot_general | solution.py:92
  108.5 12.1 %gather_fusion = bf16[4096,128]{1,0:T(8,128)(2,1)S(1)} fusion(bf16[640,128]{1,0:T(8,128)(2,1)S(1)} %get-tuple-element.807, s32[4096]{0:T(1024)S(1)} %bitcast_clamp_fusion.4), kind=kCustom, calls=%fused_computation.3.clone.clone.1 | custom fusion | bytes 2113536 | tf_op jit(solution)/shard_map/while/body/eval_jaxpr/jit(_take)/gather | solution.py:95
  120.7 7.0 %slice_multiply_fusion.13 = (f32[32,128,128]{2,1,0:T(8,128)S(1)}, f32[32,128,128]{2,1,0:T(8,128)}, f32[32,128,128]{2,1,0:T(8,128)}, f32[32,128,128]{2,1,0:T(8,128)}) fusion(f32[32,128,512]{2,1,0:T(8,128)} %fusion.242, f32[32,128]{1,0:T(8,128)S(1)} %get-tuple-element.728, bf16[32,128,128]{2,1,0:T(8,128)(2,1)S(1)} %bitcast.241, ...), kind=kLoop, calls=%fused_computation.22.clone.1 | loop fusion | flops 3670016 | bytes 17846272 | tf_op jit(solution)/shard_map/while/body/eval_jaxpr/mul | solution.py:99
  130.1 1.2 copy.164
  131.3 4.4 %fusion.245 = f32[1,128,5,128]{3,2,1,0:T(8,128)S(1)} fusion(f32[5,32,128]{1,0,2:T(8,128)S(1)} %copy.164, f32[32,128,128]{2,1,0:T(8,128)} %get-tuple-element.732), kind=kOutput, calls=%fused_computation.32.clone.1 | convolution fusion | flops 31457280 | bytes 2506752 | tf_op jit(solution)/shard_map/while/body/eval_jaxpr/mkb,kbc->bmc/dot_general | solution.py:101
  136.7 4.6 %fusion.244 = f32[1,128,7,128]{3,2,1,0:T(8,128)S(1)} fusion(f32[7,32,128]{1,0,2:T(8,128)} %copy.163, f32[32,128,128]{2,1,0:T(8,128)} %get-tuple-element.730), kind=kOutput, calls=%fused_computation.33.clone.1 | convolution fusion | flops 44040192 | bytes 2670592 | tf_op jit(solution)/shard_map/while/body/eval_jaxpr/mkb,kbc->bmc/dot_general | solution.py:101
  143.0 4.5 %fusion.246 = f32[1,128,3,128]{3,2,1,0:T(4,128)S(1)} fusion(f32[3,32,128]{1,0,2:T(4,128)} %copy.165, f32[32,128,128]{2,1,0:T(8,128)} %get-tuple-element.736), kind=kOutput, calls=%fused_computation.34.clone.1 | convolution fusion | flops 18874368 | bytes 2342912 | tf_op jit(solution)/shard_map/while/body/eval_jaxpr/mkb,kbc->bmc/dot_general | solution.py:101
  147.5 2.8 fusion.247
  150.7 1.3 copy_dynamic-update-slice_fusion.2
  152.5 1.3 fusion.117
  153.8 1.1 fusion.118
  155.0 1.0 fusion.119
  158.4 2.7 collective-permute-start.7
  163.2 5.8 %collective-permute-start.9 = (bf16[64,128]{1,0:T(8,128)(2,1)S(1)}, bf16[64,128]{1,0:T(8,128)(2,1)S(1)}, u32[]{:S(2)}, u32[]{:S(2)}) collective-permute-start(bf16[64,128]{1,0:T(8,128)(2,1)S(1)} %get-tuple-element.514), channel_id=1, source_target_pairs={{4,0},{8,4},{12,8},{16,12},{20,16},{24,20},{28,24},{32,28},{36,32}... | collective-permute-start | bytes 49160 | tf_op jit(solution)/shard_map/ppermute | solution.py:20
  171.0 2.1 collective-permute-start.10
  174.0 6.8 %collective-permute-done.11 = bf16[64,128]{1,0:T(8,128)(2,1)S(1)} collective-permute-done((bf16[64,128]{1,0:T(8,128)(2,1)S(1)}, bf16[64,128]{1,0:T(8,128)(2,1)S(1)}, u32[]{:S(2)}, u32[]{:S(2)}) %collective-permute-start.11) | collective-permute-done | bytes 16416 | tf_op jit(solution)/shard_map/ppermute | solution.py:20
  180.9 106.2 %while.33 = (s32[]{:T(128)}, bf16[2,128,16,128]{3,2,1,0:T(8,128)(2,1)}, s32[2]{0:T(128)S(1)}, f32[3,32,256]{2,1,0:T(8,128)S(1)}, bf16[8,64]{1,0:T(8,128)(2,1)S(1...) while((s32[]{:T(128)}, ...), condition=%wide.region_6.11_spmd.clone, body=%wide.region_5.10_spmd.clone.sunk | while | flops 379867168 | bytes 46694164 | solution.py:111
  185.5 5.2 %fusion.258 = f32[32,128,512]{2,1,0:T(8,128)} fusion(bf16[64,512]{1,0:T(8,128)(2,1)S(1)} %get-tuple-element.847, f32[32,128]{1,0:T(8,128)S(1)} %get-tuple-element.760, f32[32,128]{1,0:T(8,128)S(1)} %get-tuple-element.761, f32[8]{0:T(128)S(1)} %convert_multiply_fusion.8, bf16[8,64]{1,0:T(8,128)(2,1)S(1)} %get-tuple-element.846), kind=kOutput, calls=%fused_computation.127.clone.1 | convolution fusion | flops 274104320 | bytes 8487968 | tf_op jit(solution)/shard_map/while/body/eval_jaxpr/kbh,hf->kbf/dot_general | solution.py:92
  191.7 12.1 %gather_fusion.1 = bf16[4096,128]{1,0:T(8,128)(2,1)S(1)} fusion(bf16[640,128]{1,0:T(8,128)(2,1)S(1)} %get-tuple-element.849, s32[4096]{0:T(1024)S(1)} %bitcast_clamp_fusion.5), kind=kCustom, calls=%fused_computation.11.clone.clone.1 | custom fusion | bytes 2113536 | tf_op jit(solution)/shard_map/while/body/eval_jaxpr/jit(_take)/gather | solution.py:95
  203.9 7.0 %slice_multiply_fusion.14 = (f32[32,128,128]{2,1,0:T(8,128)S(1)}, f32[32,128,128]{2,1,0:T(8,128)}, f32[32,128,128]{2,1,0:T(8,128)}, f32[32,128,128]{2,1,0:T(8,128)}) fusion(f32[32,128,512]{2,1,0:T(8,128)} %fusion.258, f32[32,128]{1,0:T(8,128)S(1)} %get-tuple-element.762, bf16[32,128,128]{2,1,0:T(8,128)(2,1)S(1)} %bitcast.242, ...), kind=kLoop, calls=%fused_computation.110.clone.1 | loop fusion | flops 3670016 | bytes 17846272 | tf_op jit(solution)/shard_map/while/body/eval_jaxpr/mul | solution.py:99
  213.3 1.2 copy.171
  214.5 4.4 %fusion.261 = f32[1,128,5,128]{3,2,1,0:T(8,128)S(1)} fusion(f32[5,32,128]{1,0,2:T(8,128)S(1)} %copy.171, f32[32,128,128]{2,1,0:T(8,128)} %get-tuple-element.766), kind=kOutput, calls=%fused_computation.120.clone.1 | convolution fusion | flops 31457280 | bytes 2506752 | tf_op jit(solution)/shard_map/while/body/eval_jaxpr/mkb,kbc->bmc/dot_general | solution.py:101
  219.2 5.3 %fusion.260 = f32[1,128,7,128]{3,2,1,0:T(8,128)} fusion(f32[7,32,128]{1,0,2:T(8,128)S(1)} %copy.170, f32[32,128,128]{2,1,0:T(8,128)} %get-tuple-element.764), kind=kOutput, calls=%fused_computation.121.clone.1 | convolution fusion | flops 44040192 | bytes 2670592 | tf_op jit(solution)/shard_map/while/body/eval_jaxpr/mkb,kbc->bmc/dot_general | solution.py:101
  225.3 4.6 %fusion.262 = f32[1,128,3,128]{3,2,1,0:T(4,128)S(1)} fusion(f32[3,32,128]{1,0,2:T(4,128)} %copy.172, f32[32,128,128]{2,1,0:T(8,128)} %get-tuple-element.770), kind=kOutput, calls=%fused_computation.122.clone.1 | convolution fusion | flops 18874368 | bytes 2342912 | tf_op jit(solution)/shard_map/while/body/eval_jaxpr/mkb,kbc->bmc/dot_general | solution.py:101
  229.9 2.8 fusion.263
  232.7 1.2 fusion.264
  238.4 5.2 %fusion.258 = f32[32,128,512]{2,1,0:T(8,128)} fusion(bf16[64,512]{1,0:T(8,128)(2,1)S(1)} %get-tuple-element.847, f32[32,128]{1,0:T(8,128)S(1)} %get-tuple-element.760, f32[32,128]{1,0:T(8,128)S(1)} %get-tuple-element.761, f32[8]{0:T(128)S(1)} %convert_multiply_fusion.8, bf16[8,64]{1,0:T(8,128)(2,1)S(1)} %get-tuple-element.846), kind=kOutput, calls=%fused_computation.127.clone.1 | convolution fusion | flops 274104320 | bytes 8487968 | tf_op jit(solution)/shard_map/while/body/eval_jaxpr/kbh,hf->kbf/dot_general | solution.py:92
  244.6 12.1 %gather_fusion.1 = bf16[4096,128]{1,0:T(8,128)(2,1)S(1)} fusion(bf16[640,128]{1,0:T(8,128)(2,1)S(1)} %get-tuple-element.849, s32[4096]{0:T(1024)S(1)} %bitcast_clamp_fusion.5), kind=kCustom, calls=%fused_computation.11.clone.clone.1 | custom fusion | bytes 2113536 | tf_op jit(solution)/shard_map/while/body/eval_jaxpr/jit(_take)/gather | solution.py:95
  256.8 7.0 %slice_multiply_fusion.14 = (f32[32,128,128]{2,1,0:T(8,128)S(1)}, f32[32,128,128]{2,1,0:T(8,128)}, f32[32,128,128]{2,1,0:T(8,128)}, f32[32,128,128]{2,1,0:T(8,128)}) fusion(f32[32,128,512]{2,1,0:T(8,128)} %fusion.258, f32[32,128]{1,0:T(8,128)S(1)} %get-tuple-element.762, bf16[32,128,128]{2,1,0:T(8,128)(2,1)S(1)} %bitcast.242, ...), kind=kLoop, calls=%fused_computation.110.clone.1 | loop fusion | flops 3670016 | bytes 17846272 | tf_op jit(solution)/shard_map/while/body/eval_jaxpr/mul | solution.py:99
  266.2 1.2 copy.171
  267.4 4.4 %fusion.261 = f32[1,128,5,128]{3,2,1,0:T(8,128)S(1)} fusion(f32[5,32,128]{1,0,2:T(8,128)S(1)} %copy.171, f32[32,128,128]{2,1,0:T(8,128)} %get-tuple-element.766), kind=kOutput, calls=%fused_computation.120.clone.1 | convolution fusion | flops 31457280 | bytes 2506752 | tf_op jit(solution)/shard_map/while/body/eval_jaxpr/mkb,kbc->bmc/dot_general | solution.py:101
  272.1 5.3 %fusion.260 = f32[1,128,7,128]{3,2,1,0:T(8,128)} fusion(f32[7,32,128]{1,0,2:T(8,128)S(1)} %copy.170, f32[32,128,128]{2,1,0:T(8,128)} %get-tuple-element.764), kind=kOutput, calls=%fused_computation.121.clone.1 | convolution fusion | flops 44040192 | bytes 2670592 | tf_op jit(solution)/shard_map/while/body/eval_jaxpr/mkb,kbc->bmc/dot_general | solution.py:101
  278.2 4.6 %fusion.262 = f32[1,128,3,128]{3,2,1,0:T(4,128)S(1)} fusion(f32[3,32,128]{1,0,2:T(4,128)} %copy.172, f32[32,128,128]{2,1,0:T(8,128)} %get-tuple-element.770), kind=kOutput, calls=%fused_computation.122.clone.1 | convolution fusion | flops 18874368 | bytes 2342912 | tf_op jit(solution)/shard_map/while/body/eval_jaxpr/mkb,kbc->bmc/dot_general | solution.py:101
  282.8 2.8 fusion.263
  285.7 1.2 fusion.264
  287.1 1.5 copy.90
  290.9 2.8 collective-permute-start.13
  295.8 5.8 %collective-permute-start.15 = (bf16[64,128]{1,0:T(8,128)(2,1)S(1)}, bf16[64,128]{1,0:T(8,128)(2,1)S(1)}, u32[]{:S(2)}, u32[]{:S(2)}) collective-permute-start(bf16[64,128]{1,0:T(8,128)(2,1)S(1)} %get-tuple-element.508), channel_id=1, source_target_pairs={{4,0},{8,4},{12,8},{16,12},{20,16},{24,20},{28,24},{32,28},{36,32}... | collective-permute-start | bytes 49160 | tf_op jit(solution)/shard_map/ppermute | solution.py:20
  303.6 1.8 collective-permute-start.16
  306.3 7.0 %collective-permute-done.17 = bf16[64,128]{1,0:T(8,128)(2,1)S(1)} collective-permute-done((bf16[64,128]{1,0:T(8,128)(2,1)S(1)}, bf16[64,128]{1,0:T(8,128)(2,1)S(1)}, u32[]{:S(2)}, u32[]{:S(2)}) %collective-permute-start.17) | collective-permute-done | bytes 16416 | tf_op jit(solution)/shard_map/ppermute | solution.py:20
  314.1 5.7 %collective-permute-start.21 = (bf16[32,128]{1,0:T(8,128)(2,1)S(1)}, bf16[32,128]{1,0:T(8,128)(2,1)S(1)}, u32[]{:S(2)}, u32[]{:S(2)}) collective-permute-start(bf16[32,128]{1,0:T(8,128)(2,1)S(1)} %broadcast_select_fusion.11), channel_id=1, source_target_pairs={{4,0},{8,4},{12,8},{16,12},{20,16},{24,20},{28,24},{32,28},{36,32}... | collective-permute-start | bytes 24584 | tf_op jit(solution)/shard_map/ppermute | solution.py:28
  321.5 3.0 collective-permute-start.19
  326.0 5.7 %collective-permute-done.18 = bf16[32,128]{1,0:T(8,128)(2,1)S(1)} collective-permute-done((bf16[32,128]{1,0:T(8,128)(2,1)S(1)}, bf16[32,128]{1,0:T(8,128)(2,1)S(1)}, u32[]{:S(2)}, u32[]{:S(2)}) %collective-permute-start.18) | collective-permute-done | bytes 8224 | tf_op jit(solution)/shard_map/ppermute | solution.py:28
  331.7 57.4 %gather_fusion.2 = bf16[16384,128]{1,0:T(8,128)(2,1)} fusion(bf16[512,128]{1,0:T(8,128)(2,1)S(1)} %constant_dynamic-update-slice_fusion.76, s32[16384]{0:T(1024)S(1)} %copy-done.29), kind=kCustom, calls=%fused_computation.16 | custom fusion | bytes 8454144 | tf_op jit(solution)/shard_map/while/body/eval_jaxpr/jit(_take)/gather | solution.py:155
  389.1 6.6 %copy.95 = bf16[32,512,128]{1,2,0:T(8,128)(2,1)} copy(bf16[32,512,128]{2,1,0:T(8,128)(2,1)} %bitcast.243) | data formatting | bytes 8388608 | tf_op jit(solution)/shard_map/while/body/eval_jaxpr/jit(_take)/gather | solution.py:155
  395.7 3.3 fusion.115
  (391 shorter events, 65.7 us)
Async XLA Ops:
  0.0 156.9 %copy-start = (bf16[512,128]{1,0:T(8,128)(2,1)S(1)}, bf16[512,128]{1,0:T(8,128)(2,1)}, u32[]{:S(2)}) copy-start(bf16[512,128]{1,0:T(8,128)(2,1)} %param.47) | copy-start | bytes 393220
  0.0 12.0 %copy-start.12 = (f32[1,1,1,3,32,512]{5,4,3,2,1,0:T(8,128)S(1)}, f32[1,1,1,3,32,512]{5,4,3,2,1,0:T(8,128)}, u32[]{:S(2)}) copy-start(f32[1,1,1,3,32,512]{5,4,3,2,1,0:T(8,128)} %param.41) | copy-start | bytes 589828
  0.7 11.4 %copy-start.43 = (pred[128]{0:T(512)(128)(4,1)}, pred[128]{0:T(512)(128)(4,1)S(1)}, u32[]{:S(2)}) copy-start(pred[128]{0:T(512)(128)(4,1)S(1)} %get-tuple-element.556) | copy-start | bytes 388
  0.8 18.6 %copy-start.40 = (pred[128]{0:T(512)(128)(4,1)}, pred[128]{0:T(512)(128)(4,1)S(1)}, u32[]{:S(2)}) copy-start(pred[128]{0:T(512)(128)(4,1)S(1)} %get-tuple-element.558) | copy-start | bytes 388
  0.8 27.6 %copy-start.37 = (pred[128]{0:T(512)(128)(4,1)}, pred[128]{0:T(512)(128)(4,1)S(1)}, u32[]{:S(2)}) copy-start(pred[128]{0:T(512)(128)(4,1)S(1)} %get-tuple-element.454) | copy-start | bytes 388
  3.5 15.2 %collective-permute-start = (bf16[64,128]{1,0:T(8,128)(2,1)S(1)}, bf16[64,128]{1,0:T(8,128)(2,1)S(1)}, u32[]{:S(2)}, u32[]{:S(2)}) collective-permute-start(bf16[64,128]{1,0:T(8,128)(2,1)S(1)} %get-tuple-element.523), channel_id=1, source_target_pairs={{0,64},{64,128},{128,192},{192,0},{1,65},{65,129},{129,193},{193,1... | collective-permute-start | bytes 49160 | tf_op jit(solution)/shard_map/ppermute | solution.py:17
  5.6 13.1 %collective-permute-start.1 = (bf16[64,128]{1,0:T(8,128)(2,1)S(1)}, bf16[64,128]{1,0:T(8,128)(2,1)S(1)}, u32[]{:S(2)}, u32[]{:S(2)}) collective-permute-start(bf16[64,128]{1,0:T(8,128)(2,1)S(1)} %get-tuple-element.522), channel_id=1, source_target_pairs={{64,0},{128,64},{192,128},{0,192},{65,1},{129,65},{193,129},{1,193... | collective-permute-start | bytes 49160 | tf_op jit(solution)/shard_map/ppermute | solution.py:20
  12.2 31.1 %copy-start.2 = (f32[1,1,1,3,32,256]{5,4,3,2,1,0:T(8,128)S(1)}, f32[1,1,1,3,32,256]{5,4,3,2,1,0:T(8,128)}, u32[]{:S(2)}) copy-start(f32[1,1,1,3,32,256]{5,4,3,2,1,0:T(8,128)} %param.36) | copy-start | bytes 294916
  12.2 31.1 %copy-start.13 = (s32[1,1,1,32,256]{4,3,2,1,0:T(8,128)S(1)}, s32[1,1,1,32,256]{4,3,2,1,0:T(8,128)}, u32[]{:S(2)}) copy-start(s32[1,1,1,32,256]{4,3,2,1,0:T(8,128)} %param.34) | copy-start | bytes 98308
  12.2 31.1 %copy-start.20 = (bf16[64,512]{1,0:T(8,128)(2,1)S(1)}, bf16[64,512]{1,0:T(8,128)(2,1)}, u32[]{:S(2)}) copy-start(bf16[64,512]{1,0:T(8,128)(2,1)} %param.45) | copy-start | bytes 196612
  12.3 31.1 %copy-start.32 = (bf16[8,64]{1,0:T(8,128)(2,1)S(1)}, bf16[8,64]{1,0:T(8,128)(2,1)}, u32[]{:S(2)}) copy-start(bf16[8,64]{1,0:T(8,128)(2,1)} %param.44) | copy-start | bytes 3076
  12.5 30.9 %copy-start.27 = (f32[16,32,512]{2,1,0:T(8,128)}, f32[16,32,512]{2,1,0:T(8,128)S(1)}, u32[]{:S(2)}) copy-start(f32[16,32,512]{2,1,0:T(8,128)S(1)} %constant_dynamic-update-slice_fusion.24) | copy-start | bytes 3145732
  12.5 30.9 %copy-start.48 = (s32[1024]{0:T(1024)}, s32[1024]{0:T(1024)S(1)}, u32[]{:S(2)}) copy-start(s32[1024]{0:T(1024)S(1)} %pad_clamp_fusion.6) | copy-start | bytes 12292
  12.5 30.9 %copy-start.47 = (s32[1024]{0:T(1024)}, s32[1024]{0:T(1024)S(1)}, u32[]{:S(2)}) copy-start(s32[1024]{0:T(1024)S(1)} %pad_clamp_fusion.5) | copy-start | bytes 12292
  19.5 8.1 %collective-permute-start.2 = (bf16[64,128]{1,0:T(8,128)(2,1)S(1)}, bf16[64,128]{1,0:T(8,128)(2,1)S(1)}, u32[]{:S(2)}, u32[]{:S(2)}) collective-permute-start(bf16[64,128]{1,0:T(8,128)(2,1)S(1)} %get-tuple-element.521), channel_id=1, source_target_pairs={{0,4},{4,8},{8,12},{12,16},{16,20},{20,24},{24,28},{28,32},{32,36}... | collective-permute-start | bytes 49160 | tf_op jit(solution)/shard_map/ppermute | solution.py:17
  20.9 6.6 %collective-permute-start.3 = (bf16[64,128]{1,0:T(8,128)(2,1)S(1)}, bf16[64,128]{1,0:T(8,128)(2,1)S(1)}, u32[]{:S(2)}, u32[]{:S(2)}) collective-permute-start(bf16[64,128]{1,0:T(8,128)(2,1)S(1)} %get-tuple-element.520), channel_id=1, source_target_pairs={{4,0},{8,4},{12,8},{16,12},{20,16},{24,20},{28,24},{32,28},{36,32}... | collective-permute-start | bytes 49160 | tf_op jit(solution)/shard_map/ppermute | solution.py:20
  28.4 8.7 %collective-permute-start.4 = (bf16[64,128]{1,0:T(8,128)(2,1)S(1)}, bf16[64,128]{1,0:T(8,128)(2,1)S(1)}, u32[]{:S(2)}, u32[]{:S(2)}) collective-permute-start(bf16[64,128]{1,0:T(8,128)(2,1)S(1)} %get-tuple-element.519), channel_id=1, source_target_pairs={{0,1},{1,2},{2,3},{3,0},{4,5},{5,6},{6,7},{7,4},{8,9},{9,10},{10,1... | collective-permute-start | bytes 49160 | tf_op jit(solution)/shard_map/ppermute | solution.py:17
  36.3 7.1 %collective-permute-start.5 = (bf16[64,128]{1,0:T(8,128)(2,1)S(1)}, bf16[64,128]{1,0:T(8,128)(2,1)S(1)}, u32[]{:S(2)}, u32[]{:S(2)}) collective-permute-start(bf16[64,128]{1,0:T(8,128)(2,1)S(1)} %get-tuple-element.518), channel_id=1, source_target_pairs={{1,0},{2,1},{3,2},{0,3},{5,4},{6,5},{7,6},{4,7},{9,8},{10,9},{11,1... | collective-permute-start | bytes 49160 | tf_op jit(solution)/shard_map/ppermute | solution.py:20
  48.1 18.3 %copy-start.17 = (f32[5,32,128]{2,1,0:T(8,128)}, f32[5,32,128]{2,1,0:T(8,128)S(1)}, u32[]{:S(2)}) copy-start(f32[5,32,128]{2,1,0:T(8,128)S(1)} %get-tuple-element.717) | copy-start | bytes 245764 | tf_op jit(solution)/shard_map/while
  66.4 7.0 %copy-start.6 = (f32[7,32,128]{2,1,0:T(8,128)S(1)}, f32[7,32,128]{2,1,0:T(8,128)}, u32[]{:S(2)}) copy-start(f32[7,32,128]{2,1,0:T(8,128)} %get-tuple-element.719) | copy-start | bytes 344068 | tf_op jit(solution)/shard_map/while
  102.3 18.3 %copy-start.17 = (f32[5,32,128]{2,1,0:T(8,128)}, f32[5,32,128]{2,1,0:T(8,128)S(1)}, u32[]{:S(2)}) copy-start(f32[5,32,128]{2,1,0:T(8,128)S(1)} %get-tuple-element.717) | copy-start | bytes 245764 | tf_op jit(solution)/shard_map/while
  152.5 8.6 %copy-start.59 = (s32[32]{0:T(128)S(1)}, s32[32]{0:T(128)}, u32[]{:S(2)}) copy-start(s32[32]{0:T(128)} %get-tuple-element.549) | copy-start | bytes 388
  153.8 9.2 %copy-start.41 = (pred[128]{0:T(512)(128)(4,1)S(1)}, pred[128]{0:T(512)(128)(4,1)}, u32[]{:S(2)}) copy-start(pred[128]{0:T(512)(128)(4,1)} %copy-done.40) | copy-start | bytes 388
  154.9 16.0 %copy-start.38 = (pred[128]{0:T(512)(128)(4,1)S(1)}, pred[128]{0:T(512)(128)(4,1)}, u32[]{:S(2)}) copy-start(pred[128]{0:T(512)(128)(4,1)} %copy-done.37) | copy-start | bytes 388
  154.9 18.2 %copy-start.58 = (s32[32]{0:T(128)S(1)}, s32[32]{0:T(128)}, u32[]{:S(2)}) copy-start(s32[32]{0:T(128)} %get-tuple-element.551) | copy-start | bytes 388
  155.0 25.9 %copy-start.22 = (bf16[64,512]{1,0:T(8,128)(2,1)S(1)}, bf16[64,512]{1,0:T(8,128)(2,1)}, u32[]{:S(2)}) copy-start(bf16[64,512]{1,0:T(8,128)(2,1)} %param.50) | copy-start | bytes 196612
  155.0 25.9 %copy-start.34 = (bf16[8,64]{1,0:T(8,128)(2,1)S(1)}, bf16[8,64]{1,0:T(8,128)(2,1)}, u32[]{:S(2)}) copy-start(bf16[8,64]{1,0:T(8,128)(2,1)} %param.49) | copy-start | bytes 3076
  155.0 25.9 %copy-start.64 = (s32[2]{0:T(128)S(1)}, s32[2]{0:T(128)}, u32[]{:S(2)}) copy-start(s32[2]{0:T(128)} %copy-done.63) | copy-start | bytes 28
  158.3 3.9 collective-permute-start.6
  158.4 3.8 collective-permute-start.7
  163.1 7.0 %collective-permute-start.8 = (bf16[64,128]{1,0:T(8,128)(2,1)S(1)}, bf16[64,128]{1,0:T(8,128)(2,1)S(1)}, u32[]{:S(2)}, u32[]{:S(2)}) collective-permute-start(bf16[64,128]{1,0:T(8,128)(2,1)S(1)} %get-tuple-element.515), channel_id=1, source_target_pairs={{0,4},{4,8},{8,12},{12,16},{16,20},{20,24},{24,28},{28,32},{32,36}... | collective-permute-start | bytes 49160 | tf_op jit(solution)/shard_map/ppermute | solution.py:17
  163.2 6.9 %collective-permute-start.9 = (bf16[64,128]{1,0:T(8,128)(2,1)S(1)}, bf16[64,128]{1,0:T(8,128)(2,1)S(1)}, u32[]{:S(2)}, u32[]{:S(2)}) collective-permute-start(bf16[64,128]{1,0:T(8,128)(2,1)S(1)} %get-tuple-element.514), channel_id=1, source_target_pairs={{4,0},{8,4},{12,8},{16,12},{20,16},{24,20},{28,24},{32,28},{36,32}... | collective-permute-start | bytes 49160 | tf_op jit(solution)/shard_map/ppermute | solution.py:20
  171.0 3.0 collective-permute-start.10
  173.8 7.1 %collective-permute-start.11 = (bf16[64,128]{1,0:T(8,128)(2,1)S(1)}, bf16[64,128]{1,0:T(8,128)(2,1)S(1)}, u32[]{:S(2)}, u32[]{:S(2)}) collective-permute-start(bf16[64,128]{1,0:T(8,128)(2,1)S(1)} %get-tuple-element.512), channel_id=1, source_target_pairs={{1,0},{2,1},{3,2},{0,3},{5,4},{6,5},{7,6},{4,7},{9,8},{10,9},{11,1... | collective-permute-start | bytes 49160 | tf_op jit(solution)/shard_map/ppermute | solution.py:20
  181.0 9.7 %copy-start.4 = (f32[3,32,256]{2,1,0:T(8,128)}, f32[3,32,256]{2,1,0:T(8,128)S(1)}, u32[]{:S(2)}) copy-start(f32[3,32,256]{2,1,0:T(8,128)S(1)} %get-tuple-element.845) | copy-start | bytes 294916 | tf_op jit(solution)/shard_map/while
  181.0 10.6 %copy-start.15 = (s32[32,256]{1,0:T(8,128)}, s32[32,256]{1,0:T(8,128)S(1)}, u32[]{:S(2)}) copy-start(s32[32,256]{1,0:T(8,128)S(1)} %get-tuple-element.848) | copy-start | bytes 98308 | tf_op jit(solution)/shard_map/while
  185.5 18.3 %copy-start.18 = (f32[5,32,128]{2,1,0:T(8,128)}, f32[5,32,128]{2,1,0:T(8,128)S(1)}, u32[]{:S(2)}) copy-start(f32[5,32,128]{2,1,0:T(8,128)S(1)} %get-tuple-element.751) | copy-start | bytes 245764 | tf_op jit(solution)/shard_map/while
  203.8 7.0 %copy-start.9 = (f32[7,32,128]{2,1,0:T(8,128)S(1)}, f32[7,32,128]{2,1,0:T(8,128)}, u32[]{:S(2)}) copy-start(f32[7,32,128]{2,1,0:T(8,128)} %get-tuple-element.753) | copy-start | bytes 344068 | tf_op jit(solution)/shard_map/while
  225.3 7.4 %copy-start.1 = (f32[1,128,7,128]{3,2,1,0:T(8,128)S(1)}, f32[1,128,7,128]{3,2,1,0:T(8,128)}, u32[]{:S(2)}) copy-start(f32[1,128,7,128]{3,2,1,0:T(8,128)} %fusion.260) | copy-start | bytes 1376260 | tf_op jit(solution)/shard_map/while
  234.0 9.7 %copy-start.4 = (f32[3,32,256]{2,1,0:T(8,128)}, f32[3,32,256]{2,1,0:T(8,128)S(1)}, u32[]{:S(2)}) copy-start(f32[3,32,256]{2,1,0:T(8,128)S(1)} %get-tuple-element.845) | copy-start | bytes 294916 | tf_op jit(solution)/shard_map/while
  234.0 10.6 %copy-start.15 = (s32[32,256]{1,0:T(8,128)}, s32[32,256]{1,0:T(8,128)S(1)}, u32[]{:S(2)}) copy-start(s32[32,256]{1,0:T(8,128)S(1)} %get-tuple-element.848) | copy-start | bytes 98308 | tf_op jit(solution)/shard_map/while
  238.4 18.3 %copy-start.18 = (f32[5,32,128]{2,1,0:T(8,128)}, f32[5,32,128]{2,1,0:T(8,128)S(1)}, u32[]{:S(2)}) copy-start(f32[5,32,128]{2,1,0:T(8,128)S(1)} %get-tuple-element.751) | copy-start | bytes 245764 | tf_op jit(solution)/shard_map/while
  256.8 7.0 %copy-start.9 = (f32[7,32,128]{2,1,0:T(8,128)S(1)}, f32[7,32,128]{2,1,0:T(8,128)}, u32[]{:S(2)}) copy-start(f32[7,32,128]{2,1,0:T(8,128)} %get-tuple-element.753) | copy-start | bytes 344068 | tf_op jit(solution)/shard_map/while
  278.2 7.4 %copy-start.1 = (f32[1,128,7,128]{3,2,1,0:T(8,128)S(1)}, f32[1,128,7,128]{3,2,1,0:T(8,128)}, u32[]{:S(2)}) copy-start(f32[1,128,7,128]{3,2,1,0:T(8,128)} %fusion.260) | copy-start | bytes 1376260 | tf_op jit(solution)/shard_map/while
  287.1 8.5 %copy-start.42 = (pred[128]{0:T(512)(128)(4,1)S(1)}, pred[128]{0:T(512)(128)(4,1)}, u32[]{:S(2)}) copy-start(pred[128]{0:T(512)(128)(4,1)} %copy-done.40) | copy-start | bytes 388
  288.6 14.9 %copy-start.39 = (pred[128]{0:T(512)(128)(4,1)S(1)}, pred[128]{0:T(512)(128)(4,1)}, u32[]{:S(2)}) copy-start(pred[128]{0:T(512)(128)(4,1)} %copy-done.37) | copy-start | bytes 388
  288.6 16.8 %copy-start.57 = (s32[32]{0:T(128)S(1)}, s32[32]{0:T(128)}, u32[]{:S(2)}) copy-start(s32[32]{0:T(128)} %get-tuple-element.553) | copy-start | bytes 388
  288.7 16.9 %copy-start.28 = (f32[16,32,512]{2,1,0:T(8,128)S(1)}, f32[16,32,512]{2,1,0:T(8,128)}, u32[]{:S(2)}) copy-start(f32[16,32,512]{2,1,0:T(8,128)} %copy-done.27) | copy-start | bytes 3145732
  289.6 24.4 %copy-start.56 = (pred[32]{0:T(512)(128)(4,1)S(1)}, pred[32]{0:T(512)(128)(4,1)}, u32[]{:S(2)}) copy-start(pred[32]{0:T(512)(128)(4,1)} %get-tuple-element.444) | copy-start | bytes 100
  290.5 30.1 %copy-start.55 = (pred[32]{0:T(512)(128)(4,1)S(1)}, pred[32]{0:T(512)(128)(4,1)}, u32[]{:S(2)}) copy-start(pred[32]{0:T(512)(128)(4,1)} %get-tuple-element.554) | copy-start | bytes 100
  290.5 30.9 %copy-start.54 = (pred[32]{0:T(512)(128)(4,1)S(1)}, pred[32]{0:T(512)(128)(4,1)}, u32[]{:S(2)}) copy-start(pred[32]{0:T(512)(128)(4,1)} %get-tuple-element.548) | copy-start | bytes 100
  290.6 34.6 %copy-start.53 = (pred[32]{0:T(512)(128)(4,1)S(1)}, pred[32]{0:T(512)(128)(4,1)}, u32[]{:S(2)}) copy-start(pred[32]{0:T(512)(128)(4,1)} %get-tuple-element.550) | copy-start | bytes 100
  290.6 4.2 %collective-permute-start.12 = (bf16[64,128]{1,0:T(8,128)(2,1)S(1)}, bf16[64,128]{1,0:T(8,128)(2,1)S(1)}, u32[]{:S(2)}, u32[]{:S(2)}) collective-permute-start(bf16[64,128]{1,0:T(8,128)(2,1)S(1)} %get-tuple-element.511), channel_id=1, source_target_pairs={{0,64},{64,128},{128,192},{192,0},{1,65},{65,129},{129,193},{193,1... | collective-permute-start | bytes 49160 | tf_op jit(solution)/shard_map/ppermute | solution.py:17
  290.9 3.8 collective-permute-start.13
  293.7 32.2 %copy-start.52 = (pred[32]{0:T(512)(128)(4,1)S(1)}, pred[32]{0:T(512)(128)(4,1)}, u32[]{:S(2)}) copy-start(pred[32]{0:T(512)(128)(4,1)} %get-tuple-element.552) | copy-start | bytes 100
  293.7 38.0 %copy-start.29 = (s32[16384]{0:T(1024)S(1)}, s32[16384]{0:T(1024)}, u32[]{:S(2)}) copy-start(s32[16384]{0:T(1024)} %broadcast_clamp_fusion) | copy-start | bytes 196612
  295.7 6.9 %collective-permute-start.14 = (bf16[64,128]{1,0:T(8,128)(2,1)S(1)}, bf16[64,128]{1,0:T(8,128)(2,1)S(1)}, u32[]{:S(2)}, u32[]{:S(2)}) collective-permute-start(bf16[64,128]{1,0:T(8,128)(2,1)S(1)} %get-tuple-element.509), channel_id=1, source_target_pairs={{0,4},{4,8},{8,12},{12,16},{16,20},{20,24},{24,28},{28,32},{32,36}... | collective-permute-start | bytes 49160 | tf_op jit(solution)/shard_map/ppermute | solution.py:17
  295.8 6.8 %collective-permute-start.15 = (bf16[64,128]{1,0:T(8,128)(2,1)S(1)}, bf16[64,128]{1,0:T(8,128)(2,1)S(1)}, u32[]{:S(2)}, u32[]{:S(2)}) collective-permute-start(bf16[64,128]{1,0:T(8,128)(2,1)S(1)} %get-tuple-element.508), channel_id=1, source_target_pairs={{4,0},{8,4},{12,8},{16,12},{20,16},{24,20},{28,24},{32,28},{36,32}... | collective-permute-start | bytes 49160 | tf_op jit(solution)/shard_map/ppermute | solution.py:20
  303.6 2.7 collective-permute-start.16
  306.2 7.1 %collective-permute-start.17 = (bf16[64,128]{1,0:T(8,128)(2,1)S(1)}, bf16[64,128]{1,0:T(8,128)(2,1)S(1)}, u32[]{:S(2)}, u32[]{:S(2)}) collective-permute-start(bf16[64,128]{1,0:T(8,128)(2,1)S(1)} %get-tuple-element.506), channel_id=1, source_target_pairs={{1,0},{2,1},{3,2},{0,3},{5,4},{6,5},{7,6},{4,7},{9,8},{10,9},{11,1... | collective-permute-start | bytes 49160 | tf_op jit(solution)/shard_map/ppermute | solution.py:20
  314.1 17.6 %collective-permute-start.21 = (bf16[32,128]{1,0:T(8,128)(2,1)S(1)}, bf16[32,128]{1,0:T(8,128)(2,1)S(1)}, u32[]{:S(2)}, u32[]{:S(2)}) collective-permute-start(bf16[32,128]{1,0:T(8,128)(2,1)S(1)} %broadcast_select_fusion.11), channel_id=1, source_target_pairs={{4,0},{8,4},{12,8},{16,12},{20,16},{24,20},{28,24},{32,28},{36,32}... | collective-permute-start | bytes 24584 | tf_op jit(solution)/shard_map/ppermute | solution.py:28
  320.6 11.0 %collective-permute-start.20 = (bf16[32,128]{1,0:T(8,128)(2,1)S(1)}, bf16[32,128]{1,0:T(8,128)(2,1)S(1)}, u32[]{:S(2)}, u32[]{:S(2)}) collective-permute-start(bf16[32,128]{1,0:T(8,128)(2,1)S(1)} %broadcast_select_fusion.12), channel_id=1, source_target_pairs={{8,0},{12,4},{16,8},{20,12},{24,16},{28,20},{32,24},{36,28},{40,32... | collective-permute-start | bytes 24584 | tf_op jit(solution)/shard_map/ppermute | solution.py:28
  321.5 10.2 %collective-permute-start.19 = (bf16[32,128]{1,0:T(8,128)(2,1)S(1)}, bf16[32,128]{1,0:T(8,128)(2,1)S(1)}, u32[]{:S(2)}, u32[]{:S(2)}) collective-permute-start(bf16[32,128]{1,0:T(8,128)(2,1)S(1)} %broadcast_select_fusion.13), channel_id=1, source_target_pairs={{56,0},{60,4},{0,8},{4,12},{8,16},{12,20},{16,24},{20,28},{24,32},... | collective-permute-start | bytes 24584 | tf_op jit(solution)/shard_map/ppermute | solution.py:28
  325.2 6.4 %collective-permute-start.18 = (bf16[32,128]{1,0:T(8,128)(2,1)S(1)}, bf16[32,128]{1,0:T(8,128)(2,1)S(1)}, u32[]{:S(2)}, u32[]{:S(2)}) collective-permute-start(bf16[32,128]{1,0:T(8,128)(2,1)S(1)} %broadcast_select_fusion.14), channel_id=1, source_target_pairs={{60,0},{0,4},{4,8},{8,12},{12,16},{16,20},{20,24},{24,28},{28,32},... | collective-permute-start | bytes 24584 | tf_op jit(solution)/shard_map/ppermute | solution.py:28
  (49 other events, 153.7 us)
where the time goes:
time: 407 us; the launch traced here: 400 us
  local copies, waits for them, and re-layouts  148 us (36%)
  matrix products  91.7 us (23%)
  other arithmetic  69.5 us (17%)
  starting transfers between devices  48.8 us (12%)
  waiting for transfers between devices  31.5 us (8%)
  loops' own time  9.15 us (2%)
    dot_general x16, matrix products, layer_one_block(): jnp.einsum('mkb,kbc->bmc', angular[degree * degree:(degree + 1) * (degree...  66.8 us
    gather x2, local copies, waits for them, and re-layouts, density_one_block(): picked = jnp.take(received, index_block, axis=0).astype(jnp.float32)  64 us
    gather x4, local copies, waits for them, and re-layouts, layer_one_block(): jnp.take(ghost_table, index_block, axis=0).astype(jnp.float32)  48.5 us
    mul x4, other arithmetic, layer_one_block(): weighted = radial[:, :, degree * channels:(degree + 1) * channels] * picked  27.8 us
    ppermute x9, starting transfers between devices, padded(): lax.ppermute(lax.slice_in_dim(block, 0, width, axis=dim), axis, backward)  24.1 us
    dot_general x4, matrix products, layer_one_block(): jnp.einsum('kbh,hf->kbf', hidden, radial_out, preferred_element_type=jnp....  21 us
    ppermute x9, waiting for transfers between devices, padded(): lax.ppermute(lax.slice_in_dim(block, 0, width, axis=dim), axis, backward)  20 us
    ppermute x9, starting transfers between devices, padded(): lax.ppermute(lax.slice_in_dim(block, block.shape[dim] - width, None, axis...  16 us
  transfers between devices with their start and end apart: 22, of which 12 were waited for; matrix products, arithmetic and copies ran while one was open for 4% of the time, Pallas kernels for 0%

commit v1 on v0

v1 whole, which is shorter than its diff:
```python
import math

import jax
import jax.numpy as jnp
from jax import lax
from jax.experimental import pallas as pl
from jax.experimental.pallas import tpu as pltpu
from jax.sharding import PartitionSpec as P

BASIS = 8
F32 = jnp.float32
BF16 = jnp.bfloat16
VMEM = pl.BlockSpec(memory_space=pltpu.VMEM)
SMEM = pl.BlockSpec(memory_space=pltpu.SMEM)


def call(kernel, out_shape, operands, scratch=(), flops=0, moved=1 << 20, specs=None):
    many = isinstance(out_shape, (list, tuple))
    return pl.pallas_call(
        kernel,
        out_shape=out_shape,
        in_specs=specs or [VMEM] * len(operands),
        out_specs=[VMEM] * len(out_shape) if many else VMEM,
        scratch_shapes=list(scratch),
        cost_estimate=pl.CostEstimate(flops=flops, bytes_accessed=moved, transcendentals=0),
    )(*operands)


def dot(a, b):
    return jnp.dot(a, b, preferred_element_type=F32)


def dot_first(a, b):
    return lax.dot_general(a, b, (((0,), (0,)), ((), ())), preferred_element_type=F32)


def harmonics(vx, vy, vz, weight):
    radius = jnp.sqrt(vx * vx + vy * vy + vz * vz)
    inverse = 1.0 / radius
    x, y, z = vx * inverse, vy * inverse, vz * inverse
    xx, yy, zz = x * x, y * y, z * z
    r3, r15, r5, r105, r7 = (math.sqrt(v) for v in (3.0, 15.0, 5.0, 105.0, 7.0))
    outer, inner = math.sqrt(35.0 / 8.0), math.sqrt(21.0 / 8.0)
    rows = [
        jnp.ones_like(x),
        r3 * x,
        r3 * y,
        r3 * z,
        r15 * x * y,
        r15 * y * z,
        0.5 * r5 * (3.0 * zz - 1.0),
        r15 * x * z,
        0.5 * r15 * (xx - yy),
        outer * y * (3.0 * xx - yy),
        r105 * x * y * z,
        inner * y * (5.0 * zz - 1.0),
        0.5 * r7 * z * (5.0 * zz - 3.0),
        inner * x * (5.0 * zz - 1.0),
        0.5 * r105 * z * (xx - yy),
        outer * x * (xx - 3.0 * yy),
    ]
    return [row * weight for row in rows], radius, inverse


def radial_basis(radius, inverse, cutoff):
    u = radius * (1.0 / cutoff)
    u2 = u * u
    envelope = 1.0 + u2 * u2 * u2 * (-28.0 + u * (48.0 - 21.0 * u))
    scale = math.sqrt(2.0 / cutoff) * inverse * envelope
    angle = radius * (math.pi / cutoff)
    before, now = jnp.zeros_like(angle), jnp.sin(angle)
    twice = 2.0 * jnp.cos(angle)
    rows = []
    for _ in range(BASIS):
        rows.append(now * scale)
        before, now = now, twice * now - before
    return rows


def sections(arrays):
    return jnp.where(lax.broadcasted_iota(jnp.int32, (8, 128), 1) < 64, arrays[1], arrays[0])


def swapped(index):
    return jnp.where(index >= 256, index ^ 64, index)


def species_rows(species_ref, pieces):
    parts = [jnp.broadcast_to(species_ref[...].astype(F32), (8, 256))]
    for first in range(0, len(pieces), 2):
        parts.append(sections((pieces[first][...], pieces[first + 1][...])))
    return jnp.concatenate(parts, axis=1)


def pick_species(section):
    def kernel(species_ref, lists_ref, *rest):
        out_ref = rest[-1]
        table = species_rows(species_ref, rest[:-1]).astype(BF16)
        rows = table.shape[1]
        chosen = swapped(lists_ref[section : section + 1, :])
        onehot = lax.broadcasted_iota(jnp.int32, (rows, 128), 0) == chosen
        out_ref[...] = dot(table, jnp.where(onehot, 1.0, 0.0).astype(BF16))

    return kernel


def store_rows(ref, rows):
    for n, row in enumerate(rows):
        size = row.shape[0]
        for tile in range(ref.shape[0]):
            ref[tile, n * size : (n + 1) * size, :] = row[:, tile * 128 : (tile + 1) * 128]


def spread(ref, row):
    parts = [ref[tile, pl.ds(row, 8, stride=0), :] for tile in range(ref.shape[0])]
    return jnp.concatenate(parts, axis=1)


def basis_rows(ref, slot, slots):
    parts = [ref[tile, pl.ds(slot, BASIS, stride=slots), :] for tile in range(ref.shape[0])]
    return jnp.concatenate(parts, axis=1)


def geometry_kernel(vec_ref, count_ref, in1_ref, in2_ref, y_ref, hid1_ref, hid2_ref, phi):
    slots, atoms = vec_ref.shape[1:]
    live = lax.broadcasted_iota(jnp.int32, (slots, atoms), 0) < count_ref[...]
    weight = jnp.where(live, 0.25, 0.0)
    rows, radius, inverse = harmonics(vec_ref[0], vec_ref[1], vec_ref[2], weight)
    store_rows(y_ref, rows)
    store_rows(phi, radial_basis(radius, inverse, 5.0))
    into1 = in1_ref[...].astype(F32).T.astype(BF16)
    into2 = in2_ref[...].astype(F32).T.astype(BF16)
    for k in range(slots):
        basis = basis_rows(phi, k, slots).astype(BF16)
        for into, out in ((into1, hid1_ref), (into2, hid2_ref)):
            value = dot(into, basis)
            out[k] = (value / (1.0 + jnp.exp(-value))).astype(BF16)


def slot_sums(weighted, y_ref, finish):
    slots, _, atoms = weighted.shape
    tiles = atoms // 128

    def block(j, carry):
        first = pl.multiple_of((j // tiles) * 16, 16)
        tile = j % tiles
        lane = pl.multiple_of(tile * 128, 128)
        sums = [[jnp.zeros((8, 128), F32) for _ in range(16)] for _ in range(2)]
        for k in range(slots):
            for degree in range(4):
                w = [
                    weighted[k, pl.ds(degree * 128 + first + 8 * h, 8), pl.ds(lane, 128)]
                    for h in range(2)
                ]
                for m in range(degree * degree, (degree + 1) * (degree + 1)):
                    y = y_ref[tile, pl.ds(m * slots + k, 8, stride=0), :]
                    for h in range(2):
                        sums[h][m] = sums[h][m] + y * w[h]
        finish(first, lane, [jnp.concatenate([sums[0][m], sums[1][m]], axis=0) for m in range(16)])
        return carry

    lax.fori_loop(0, 8 * tiles, block, 0)


def layer_one_kernel(
    species_ref, xl, xh, yl, yh, zl, zh, index_ref, y_ref, hid_ref, out_ref, emb_ref, msg1_ref,
    self_ref, mix_ref, msg2_ref, next_ref, weighted, kinds, feats,
):
    slots, atoms = index_ref.shape
    table = species_rows(species_ref, (xl, xh, yl, yh, zl, zh))
    for row in range(0, slots, 8):
        for lane in range(0, atoms, 128):
            where = swapped(index_ref[row : row + 8, lane : lane + 128])
            found = jnp.zeros((8, 128), F32)
            for b in range(5):
                part = jnp.take_along_axis(table[:, b * 128 : (b + 1) * 128], where & 127, axis=1)
                found = jnp.where((where >> 7) == b, part, found)
            kinds[lane // 128, row : row + 8, :] = found
    rows = dot(emb_ref[...], msg1_ref[...]).astype(BF16).astype(F32)
    rows_t = rows.T.astype(BF16)
    out_t = out_ref[...].astype(F32).T.astype(BF16)
    kind_ids = lax.broadcasted_iota(jnp.int32, (8, atoms), 0).astype(F32)

    def fill(k, carry):
        radial = dot(out_t, hid_ref[k])
        onehot = jnp.where(spread(kinds, k) == kind_ids, 1.0, 0.0).astype(BF16)
        picked = dot(rows_t, onehot)
        for degree in range(4):
            weighted[k, degree * 128 : (degree + 1) * 128, :] = (
                radial[degree * 128 : (degree + 1) * 128] * picked
            )
        return carry

    lax.fori_loop(0, slots, fill, 0)

    def finish(first, lane, sums):
        feats[pl.ds(first, 16), pl.ds(lane, 128)] = sums[0].astype(BF16)
        for degree in (1, 2, 3):
            total = sums[degree * degree] * sums[degree * degree]
            for m in range(degree * degree + 1, (degree + 1) * (degree + 1)):
                total = total + sums[m] * sums[m]
            feats[pl.ds(degree * 128 + first, 16), pl.ds(lane, 128)] = total.astype(BF16)

    slot_sums(weighted, y_ref, finish)
    own = jnp.where(table[:, :atoms] == kind_ids, 1.0, 0.0).astype(BF16)
    start = dot_first(emb_ref[...].astype(F32), own.astype(F32)).astype(BF16)
    mixed = dot_first(self_ref[...], start) + dot_first(mix_ref[...], feats[...])
    hidden = (mixed / (1.0 + jnp.exp(-mixed))).astype(BF16)
    next_ref[...] = dot_first(hidden, msg2_ref[...]).astype(BF16)


def layer_two_kernel(
    own_ref, xl, xh, yl, yh, zl, zh, index_ref, y_ref, hid_ref, out_ref, dec_ref, coeff_ref,
    weighted, feats, table,
):
    slots, atoms = index_ref.shape
    table[:atoms, :] = own_ref[...].astype(F32)
    for n, piece in enumerate((xl, xh, yl, yh, zl, zh)):
        table[atoms + 64 * n : atoms + 64 * (n + 1), :] = piece[...].astype(F32)
    rows = table.shape[0]
    rows_t = table[...].T.astype(BF16)
    out_t = out_ref[...].astype(F32).T.astype(BF16)
    row_ids = lax.broadcasted_iota(jnp.int32, (rows, atoms), 0)

    def fill(k, carry):
        radial = dot(out_t, hid_ref[k])
        onehot = jnp.where(index_ref[pl.ds(k, 1), :] == row_ids, 1.0, 0.0).astype(BF16)
        picked = dot(rows_t, onehot)
        for degree in range(4):
            weighted[k, degree * 128 : (degree + 1) * 128, :] = (
                radial[degree * 128 : (degree + 1) * 128] * picked
            )
        return carry

    lax.fori_loop(0, slots, fill, 0)

    def finish(first, lane, sums):
        for m in range(16):
            feats[pl.ds(m * 128 + first, 16), pl.ds(lane, 128)] = sums[m].astype(BF16)

    slot_sums(weighted, y_ref, finish)
    group = lax.broadcasted_iota(jnp.int32, (128, 128), 0) >> 3
    total = jnp.zeros((128, atoms), F32)
    for degree in range(4):
        tall = jnp.concatenate([dec_ref[degree].astype(F32).T] * 16, axis=0)
        for m in range(degree * degree, (degree + 1) * (degree + 1)):
            part = jnp.where(group == m, tall, 0.0).astype(BF16)
            total = total + dot(part, feats[m * 128 : (m + 1) * 128, :])
    coeff_ref[...] = total.T.astype(BF16)


def density_kernel(
    here_ref, p0, p1, p2, p3, p4, index_ref, count_ref, vec_ref, out_ref, y, phi, table
):
    slots, probes = index_ref.shape
    live = lax.broadcasted_iota(jnp.int32, (slots, probes), 0) < count_ref[...]
    weight = jnp.where(live, 0.125, 0.0)
    rows, radius, inverse = harmonics(vec_ref[0], vec_ref[1], vec_ref[2], weight)
    store_rows(y, rows)
    store_rows(phi, radial_basis(radius, inverse, 4.0))
    table[...] = jnp.zeros_like(table)
    for n, piece in enumerate((p0, p1, p2, p3, p4)):
        table[32 * n : 32 * (n + 1), :] = piece[...].astype(F32)
    rows_t = table[...].T.astype(BF16)
    row_ids = lax.broadcasted_iota(jnp.int32, (table.shape[0], probes), 0)
    column, here = here_ref[1], here_ref[0]

    def slot(k, total):
        index = index_ref[pl.ds(k, 1), :]
        source = (index >> 5) - here + 2
        source = jnp.where(source < 0, source + column, source)
        source = jnp.where(source >= column, source - column, source)
        where = source * 32 + (index & 31)
        onehot = jnp.where(where == row_ids, 1.0, 0.0).astype(BF16)
        picked = dot(rows_t, onehot)
        part = jnp.zeros((8, probes), F32)
        for m in range(16):
            part = part + spread(y, m * slots + k) * picked[m * 8 : (m + 1) * 8]
        return total + part * basis_rows(phi, k, slots)

    total = lax.fori_loop(0, slots, slot, jnp.zeros((8, probes), F32))
    out_ref[...] = jnp.sum(total, axis=0, keepdims=True)


def shifted(block, axis, step):
    size = lax.axis_size(axis)
    return lax.ppermute(block, axis, [(i, (i + step) % size) for i in range(size)])


def extend(rows, lists):
    table = rows
    pieces = []
    for section, axis in enumerate(("gx", "gy", "gz")):
        chosen = jnp.take(table, lists[section], axis=0)
        low = shifted(chosen[64:], axis, 1)
        high = shifted(chosen[:64], axis, -1)
        pieces += [low, high]
        if section < 2:
            table = jnp.concatenate([table, low, high], axis=0)
    return pieces


def shards(
    species, neighbour_index, neighbour_count, edge_vectors, ghost_send, brick_send, probe_index,
    probe_count, probe_vectors, embedding, message_one, radial_in_one, radial_out_one, self_mix,
    basis_mix, message_two, radial_in_two, radial_out_two, decoder,
):
    slots, atoms = neighbour_index.shape[3:]
    probes = probe_index.shape[-1]
    kinds = species.reshape(1, atoms)
    index = neighbour_index.reshape(slots, atoms)
    vectors = edge_vectors.reshape(3, slots, atoms)
    lists = ghost_send.reshape(3, 128)
    shape = jax.ShapeDtypeStruct

    ghosts = []
    for section, axis in enumerate(("gx", "gy", "gz")):
        chosen = call(pick_species(section), shape((8, 128), F32), (kinds, lists, *ghosts))
        ghosts += [shifted(chosen, axis, 1), shifted(chosen, axis, -1)]
    angular, hidden_one, hidden_two = call(
        geometry_kernel,
        (
            shape((atoms // 128, 16 * slots, 128), F32),
            shape((slots, 64, atoms), BF16),
            shape((slots, 64, atoms), BF16),
        ),
        (vectors, neighbour_count.reshape(1, atoms), radial_in_one, radial_in_two),
        [pltpu.VMEM((atoms // 128, BASIS * slots, 128), F32)],
    )
    second = call(
        layer_one_kernel,
        shape((atoms, 128), BF16),
        (kinds, *ghosts, index, angular, hidden_one, radial_out_one, embedding, message_one,
         self_mix, basis_mix, message_two),
        [
            pltpu.VMEM((slots, 512, atoms), F32),
            pltpu.VMEM((atoms // 128, slots, 128), F32),
            pltpu.VMEM((512, atoms), BF16),
        ],
    )
    coeffs = call(
        layer_two_kernel,
        shape((atoms, 128), BF16),
        (second, *extend(second, lists), index, angular, hidden_two, radial_out_two, decoder),
        [
            pltpu.VMEM((slots, 512, atoms), F32),
            pltpu.VMEM((2048, atoms), BF16),
            pltpu.VMEM((640, 128), F32),
        ],
    )
    table = jnp.concatenate([coeffs, *extend(coeffs, lists)], axis=0)
    column = lax.axis_size("gy")
    here = lax.axis_index("gy")
    bricks = brick_send.reshape(-1)
    bricks = jnp.concatenate([bricks, bricks])
    nearby = lax.dynamic_slice_in_dim(bricks, ((here + column - 2) % column) * 32, 160, 0)
    chosen = jnp.take(table, nearby, axis=0)
    pieces = []
    for n in range(5):
        step = 2 - n
        sent = chosen[32 * (step + 2) : 32 * (step + 3)]
        pieces.append(shifted(sent, "gy", step) if step else sent)
    density = call(
        density_kernel,
        shape((1, probes), F32),
        (jnp.stack([here, column]).astype(jnp.int32), *pieces, probe_index.reshape(slots, probes),
         probe_count.reshape(1, probes), probe_vectors.reshape(3, slots, probes)),
        [
            pltpu.VMEM((probes // 128, 16 * slots, 128), F32),
            pltpu.VMEM((probes // 128, BASIS * slots, 128), F32),
            pltpu.VMEM((256, 128), F32),
        ],
        specs=[SMEM] + [VMEM] * 8,
    )
    return density.reshape(1, 1, 1, probes)


def solution(mesh):
    domain = ("gx", "gy", "gz")
    placed = tuple(P(*domain) for _ in range(9)) + tuple(P() for _ in range(10))
    return jax.shard_map(
        shards, mesh=mesh, in_specs=placed, out_specs=P(*domain), check_vma=False
    )
```

time: 407 us -> 142 us (0.35); the launches traced: 400 us -> 141 us
  local copies, waits for them, and re-layouts: 148 us -> 14.5 us
  matrix products: 91.7 us -> 0 us
  other arithmetic: 69.5 us -> 1.4 us
  Pallas kernels: 0 us -> 50.5 us
  loops' own time: 9.15 us -> 0 us
  waiting for transfers between devices: 31.5 us -> 24.3 us
    gather x20 -> x7, local copies, waits for them, and re-layouts: 123 us -> 6.58 us  [the longest x6 5.83 us: extend(): chosen = jnp.take(table, lists[section], axis=0)]
    dot_general x28 -> x0, matrix products: 91.7 us -> none  [the longest x16 66.8 us: layer_one_block(): jnp.einsum('mkb,kbc->bmc', angular[degree * degree:(degree + 1) * (degree...]
    pallas_call x0 -> x7, Pallas kernels: none -> 50.5 us  [call(): pl.pallas_call(kernel, out_shape=out_shape, in_specs=specs or [VMEM] * le...]
    mul x22 -> x0, other arithmetic: 37.4 us -> none  [the longest x4 27.8 us: layer_one_block(): weighted = radial[:, :, degree * channels:(degree + 1) * channels] * picked]
    another operation x12 -> x0, local copies, waits for them, and re-layouts: 10.5 us -> none  [harmonics(): return (jnp.stack(rows_list), radius)]
    another operation x2 -> x0, loops' own time: 9.15 us -> none  [layer_sums(): return lax.map(layer_one_block, starts).reshape(atom_rows, 16, channels)]
    while x24 -> x0, other arithmetic: 7.36 us -> none
    ppermute x22, waiting for transfers between devices: 31.5 us -> 24.3 us  [shifted(): lax.ppermute(block, axis, [(i, (i + step) % size) for i in range(size)])]
  transfers between devices with their start and end apart: 22 -> 22, of which waited for: 12 -> 12; matrix products, arithmetic and copies ran while one was open for 4% -> 1% of each run, Pallas kernels for 0% -> 3%
where the time goes in v1:
time: 142 us; the launch traced here: 141 us
  Pallas kernels  50.5 us (36%)
  starting transfers between devices  50.4 us (35%)
  waiting for transfers between devices  24.3 us (17%)
  local copies, waits for them, and re-layouts  14.5 us (10%)
    pallas_call x7, Pallas kernels, call(): pl.pallas_call(kernel, out_shape=out_shape, in_specs=specs or [VMEM] * le...  50.5 us
    ppermute x22, starting transfers between devices, shifted(): lax.ppermute(block, axis, [(i, (i + step) % size) for i in range(size)])  50.4 us
    ppermute x22, waiting for transfers between devices, shifted(): lax.ppermute(block, axis, [(i, (i + step) % size) for i in range(size)])  24.3 us
    unnamed x53, local copies, waits for them, and re-layouts  7.28 us
    gather x6, local copies, waits for them, and re-layouts, extend(): chosen = jnp.take(table, lists[section], axis=0)  5.83 us
  transfers between devices with their start and end apart: 22, of which 12 were waited for; matrix products, arithmetic and copies ran while one was open for 1% of the time, Pallas kernels for 3%

profile of v1, /device:TPU:1, one launch (start us, length us, event | category | flops | bytes accessed | tf_op | source)
XLA Modules:
  0.0 141.4 jit_solution(18160933927170093651)
XLA Ops:
  0.0 1.3 copy.23
  1.3 1.4 %shard_map.181 = f32[8,128]{1,0:T(8,128)} custom-call(s32[1,256]{1,0:T(1,128)} %bitcast.30, s32[3,128]{1,0:T(4,128)} %bitcast.27), custom_call_target="tpu_custom_call" | custom-call | bytes 1048576 | tf_op jit(solution)/shard_map/pallas_call | solution.py:19
  2.7 2.0 %collective-permute-start = (f32[8,128]{1,0:T(8,128)}, f32[8,128]{1,0:T(8,128)S(1)}, u32[]{:S(2)}, u32[]{:S(2)}) collective-permute-start(f32[8,128]{1,0:T(8,128)} %shard_map.181), channel_id=1, source_target_pairs={{0,64},{64,128},{128,192},{192,0},{1,65},{65,129},{129,193},{193,1... | collective-permute-start | bytes 12296 | tf_op jit(solution)/shard_map/ppermute | solution.py:287
  4.7 1.3 collective-permute-start.1
  6.0 1.2 collective-permute-done.rest_0_.xl
  7.2 0.2 collective-permute-done.1.rest_1_.xh
  7.4 0.4 copy-done.6
  7.8 0.6 copy-done.7
  8.4 1.4 %shard_map.182 = f32[8,128]{1,0:T(8,128)} custom-call(s32[1,256]{1,0:T(1,128)} %bitcast.31, s32[3,128]{1,0:T(4,128)} %bitcast.28, f32[8,128]{1,0:T(8,128)} %copy-done.6, f32[8,128]{1,0:T(8,128)} %copy-done.7), custom_call_target="tpu_custom_call" | custom-call | bytes 1048576 | tf_op jit(solution)/shard_map/pallas_call | solution.py:19
  9.8 1.5 %collective-permute-start.2 = (f32[8,128]{1,0:T(8,128)}, f32[8,128]{1,0:T(8,128)S(1)}, u32[]{:S(2)}, u32[]{:S(2)}) collective-permute-start(f32[8,128]{1,0:T(8,128)} %shard_map.182), channel_id=1, source_target_pairs={{0,4},{4,8},{8,12},{12,16},{16,20},{20,24},{24,28},{28,32},{32,36}... | collective-permute-start | bytes 12296 | tf_op jit(solution)/shard_map/ppermute | solution.py:287
  11.3 5.5 %collective-permute-start.3 = (f32[8,128]{1,0:T(8,128)}, f32[8,128]{1,0:T(8,128)S(1)}, u32[]{:S(2)}, u32[]{:S(2)}) collective-permute-start(f32[8,128]{1,0:T(8,128)} %shard_map.182), channel_id=1, source_target_pairs={{0,60},{4,0},{8,4},{12,8},{16,12},{20,16},{24,20},{28,24},{32,28},... | collective-permute-start | bytes 12296 | tf_op jit(solution)/shard_map/ppermute | solution.py:287
  16.8 1.2 collective-permute-done.2.rest_2_.yl
  18.0 0.6 copy-done.10
  18.6 0.6 copy-done.11
  19.2 1.5 %shard_map.183 = f32[8,128]{1,0:T(8,128)} custom-call(s32[1,256]{1,0:T(1,128)} %bitcast.32, s32[3,128]{1,0:T(4,128)} %bitcast.29, f32[8,128]{1,0:T(8,128)} %copy-done.6, f32[8,128]{1,0:T(8,128)} %copy-done.7, f32[8,128]{1,0:T(8,128)} %copy-done.10, f32[8,128]{1,0:T(8,128)} %copy-done.11), custom_call_target="tpu_custom_call" | custom-call | bytes 1048576 | tf_op jit(solution)/shard_map/pallas_call | solution.py:19
  20.7 8.3 %collective-permute-start.4 = (f32[8,128]{1,0:T(8,128)}, f32[8,128]{1,0:T(8,128)S(1)}, u32[]{:S(2)}, u32[]{:S(2)}) collective-permute-start(f32[8,128]{1,0:T(8,128)} %shard_map.183), channel_id=1, source_target_pairs={{0,1},{1,2},{2,3},{3,0},{4,5},{5,6},{6,7},{7,4},{8,9},{9,10},{10,1... | collective-permute-start | bytes 12296 | tf_op jit(solution)/shard_map/ppermute | solution.py:287
  29.0 3.9 %shard_map.184 = (f32[2,512,128]{2,1,0:T(8,128)}, bf16[32,64,256]{2,1,0:T(8,128)(2,1)}, bf16[32,64,256]{2,1,0:T(8,128)(2,1)}) custom-call(f32[3,32,256]{2,1,0:T(8,128)} %bitcast.25, s32[1,256]{1,0:T(1,128)} %bitcast.36, bf16[8,64]{1,0:T(8,128)(2,1)} %in1_ref.1, bf16[8,64]{1,0:T(8,128)(2,1)} %in2_ref.1), custom_call_target="tpu_custom_call" | custom-call | bytes 1048576 | tf_op jit(solution)/shard_map/pallas_call | solution.py:19
  33.0 3.2 %collective-permute-done.5.zh = f32[8,128]{1,0:T(8,128)S(1)} collective-permute-done((f32[8,128]{1,0:T(8,128)}, f32[8,128]{1,0:T(8,128)S(1)}, u32[]{:S(2)}, u32[]{:S(2)}) %collective-permute-start.5) | collective-permute-done | bytes 4128 | tf_op jit(solution)/shard_map/ppermute | solution.py:287
  36.2 0.6 copy-done.19
  36.8 16.0 %shard_map.185.own_ref = bf16[256,128]{1,0:T(8,128)(2,1)} custom-call(s32[1,256]{1,0:T(1,128)} %bitcast.33, f32[8,128]{1,0:T(8,128)} %copy-done.6, f32[8,128]{1,0:T(8,128)} %copy-done.7, f32[8,128]{1,0:T(8,128)} %copy-done.10, f32[8,128]{1,0:T(8,128)} %copy-done.11, f32[8,128]{1,0:T(8,128)} %copy-done.18, f32[8,128]{1,0:T(8,128)} %copy-done.19, ...), custom_call_target="tpu_custom_call" | custom-call | bytes 1048576 | tf_op jit(solution)/shard_map/pallas_call | solution.py:19
  52.7 1.5 %gather_fusion.1 = bf16[128,128]{1,0:T(8,128)(2,1)S(1)} fusion(bf16[256,128]{1,0:T(8,128)(2,1)} %shard_map.185.own_ref, s32[1024]{0:T(1024)S(1)} %pad_clamp_fusion.3), kind=kCustom, calls=%fused_computation.clone | custom fusion | bytes 66048 | tf_op jit(solution)/shard_map/jit(_take)/gather | solution.py:294
  54.2 0.1 broadcast_select_fusion.6
  54.3 1.0 collective-permute-start.6
  55.3 1.8 %collective-permute-start.7 = (bf16[64,128]{1,0:T(8,128)(2,1)S(1)}, bf16[64,128]{1,0:T(8,128)(2,1)S(1)}, u32[]{:S(2)}, u32[]{:S(2)}) collective-permute-start(bf16[64,128]{1,0:T(8,128)(2,1)S(1)} %get-tuple-element.39), channel_id=1, source_target_pairs={{0,192},{64,0},{128,64},{192,128},{1,193},{65,1},{129,65},{193,129... | collective-permute-start | bytes 49160 | tf_op jit(solution)/shard_map/ppermute | solution.py:287
  57.1 1.1 collective-permute-done.6.xl
  58.2 0.7 gather_fusion.2
  59.0 0.1 broadcast_select_fusion.4
  59.1 0.1 collective-permute-start.8
  59.2 5.4 %collective-permute-start.9 = (bf16[64,128]{1,0:T(8,128)(2,1)S(1)}, bf16[64,128]{1,0:T(8,128)(2,1)S(1)}, u32[]{:S(2)}, u32[]{:S(2)}) collective-permute-start(bf16[64,128]{1,0:T(8,128)(2,1)S(1)} %get-tuple-element.37), channel_id=1, source_target_pairs={{0,60},{4,0},{8,4},{12,8},{16,12},{20,16},{24,20},{28,24},{32,28},... | collective-permute-start | bytes 49160 | tf_op jit(solution)/shard_map/ppermute | solution.py:287
  64.5 1.1 collective-permute-done.8.yl
  65.7 0.6 copy-done.4
  66.2 0.6 copy-done.5
  66.8 0.7 gather_fusion.3
  67.5 0.1 broadcast_select_fusion.2
  67.7 4.9 %collective-permute-start.10 = (bf16[64,128]{1,0:T(8,128)(2,1)S(1)}, bf16[64,128]{1,0:T(8,128)(2,1)S(1)}, u32[]{:S(2)}, u32[]{:S(2)}) collective-permute-start(bf16[64,128]{1,0:T(8,128)(2,1)S(1)} %get-tuple-element.36), channel_id=1, source_target_pairs={{0,1},{1,2},{2,3},{3,0},{4,5},{5,6},{6,7},{7,4},{8,9},{9,10},{10,1... | collective-permute-start | bytes 49160 | tf_op jit(solution)/shard_map/ppermute | solution.py:287
  72.5 0.1 compare_and_fusion.3
  72.6 0.8 copy.20.dec_ref
  73.4 6.2 %collective-permute-done.11.zh = bf16[64,128]{1,0:T(8,128)(2,1)S(1)} collective-permute-done((bf16[64,128]{1,0:T(8,128)(2,1)S(1)}, bf16[64,128]{1,0:T(8,128)(2,1)S(1)}, u32[]{:S(2)}, u32[]{:S(2)}) %collective-permute-start.11) | collective-permute-done | bytes 16416 | tf_op jit(solution)/shard_map/ppermute | solution.py:287
  79.6 0.6 copy-done.9
  80.2 17.0 %shard_map.186 = bf16[256,128]{1,0:T(8,128)(2,1)} custom-call(bf16[256,128]{1,0:T(8,128)(2,1)} %shard_map.185.own_ref, bf16[64,128]{1,0:T(8,128)(2,1)} %copy-done.2, bf16[64,128]{1,0:T(8,128)(2,1)} %copy-done.3, bf16[64,128]{1,0:T(8,128)(2,1)} %copy-done.4, bf16[64,128]{1,0:T(8,128)(2,1)} %copy-done.5, bf16[64,128]{1,0:T(8,128)(2,1)} %copy-done.8, ...), custom_call_target="tpu_custom_call" | custom-call | bytes 1048576 | tf_op jit(solution)/shard_map/pallas_call | solution.py:19
  97.3 1.5 %gather_fusion.4 = bf16[128,128]{1,0:T(8,128)(2,1)S(1)} fusion(bf16[256,128]{1,0:T(8,128)(2,1)} %shard_map.186, s32[1024]{0:T(1024)S(1)} %pad_clamp_fusion.3), kind=kCustom, calls=%fused_computation.3.clone | custom fusion | bytes 66048 | tf_op jit(solution)/shard_map/jit(_take)/gather | solution.py:294
  98.7 0.1 broadcast_select_fusion.5
  98.9 1.0 collective-permute-start.12
  99.8 2.1 %collective-permute-start.13 = (bf16[64,128]{1,0:T(8,128)(2,1)S(1)}, bf16[64,128]{1,0:T(8,128)(2,1)S(1)}, u32[]{:S(2)}, u32[]{:S(2)}) collective-permute-start(bf16[64,128]{1,0:T(8,128)(2,1)S(1)} %get-tuple-element.33), channel_id=1, source_target_pairs={{0,192},{64,0},{128,64},{192,128},{1,193},{65,1},{129,65},{193,129... | collective-permute-start | bytes 49160 | tf_op jit(solution)/shard_map/ppermute | solution.py:287
  102.0 1.0 collective-permute-done.12
  103.0 0.7 gather_fusion.5
  103.7 0.1 broadcast_select_fusion.3
  103.8 0.1 collective-permute-start.14
  103.9 5.4 %collective-permute-start.15 = (bf16[64,128]{1,0:T(8,128)(2,1)S(1)}, bf16[64,128]{1,0:T(8,128)(2,1)S(1)}, u32[]{:S(2)}, u32[]{:S(2)}) collective-permute-start(bf16[64,128]{1,0:T(8,128)(2,1)S(1)} %get-tuple-element.31), channel_id=1, source_target_pairs={{0,60},{4,0},{8,4},{12,8},{16,12},{20,16},{24,20},{28,24},{32,28},... | collective-permute-start | bytes 49160 | tf_op jit(solution)/shard_map/ppermute | solution.py:287
  109.3 1.1 collective-permute-done.14
  110.5 0.7 gather_fusion.6
  111.2 0.1 broadcast_select_fusion.1
  111.3 2.1 %collective-permute-start.16 = (bf16[64,128]{1,0:T(8,128)(2,1)S(1)}, bf16[64,128]{1,0:T(8,128)(2,1)S(1)}, u32[]{:S(2)}, u32[]{:S(2)}) collective-permute-start(bf16[64,128]{1,0:T(8,128)(2,1)S(1)} %get-tuple-element.30), channel_id=1, source_target_pairs={{0,1},{1,2},{2,3},{3,0},{4,5},{5,6},{6,7},{7,4},{8,9},{9,10},{10,1... | collective-permute-start | bytes 49160 | tf_op jit(solution)/shard_map/ppermute | solution.py:287
  113.4 0.9 collective-permute-done.16
  114.3 6.2 %collective-permute-done.17 = bf16[64,128]{1,0:T(8,128)(2,1)S(1)} collective-permute-done((bf16[64,128]{1,0:T(8,128)(2,1)S(1)}, bf16[64,128]{1,0:T(8,128)(2,1)S(1)}, u32[]{:S(2)}, u32[]{:S(2)}) %collective-permute-start.17) | collective-permute-done | bytes 16416 | tf_op jit(solution)/shard_map/ppermute | solution.py:287
  120.5 0.8 gather_fusion
  121.2 0.1 broadcast_select_fusion
  121.3 0.6 fusion
  122.0 5.6 %collective-permute-start.20 = (bf16[32,128]{1,0:T(8,128)(2,1)S(1)}, bf16[32,128]{1,0:T(8,128)(2,1)S(1)}, u32[]{:S(2)}, u32[]{:S(2)}) collective-permute-start(bf16[32,128]{1,0:T(8,128)(2,1)S(1)} %get-tuple-element.25), channel_id=1, source_target_pairs={{0,60},{4,0},{8,4},{12,8},{16,12},{20,16},{24,20},{28,24},{32,28},... | collective-permute-start | bytes 24584 | tf_op jit(solution)/shard_map/ppermute | solution.py:287
  127.6 2.4 %collective-permute-start.21 = (bf16[32,128]{1,0:T(8,128)(2,1)S(1)}, bf16[32,128]{1,0:T(8,128)(2,1)S(1)}, u32[]{:S(2)}, u32[]{:S(2)}) collective-permute-start(bf16[32,128]{1,0:T(8,128)(2,1)S(1)} %get-tuple-element.24), channel_id=1, source_target_pairs={{0,56},{4,60},{8,0},{12,4},{16,8},{20,12},{24,16},{28,20},{32,24},... | collective-permute-start | bytes 24584 | tf_op jit(solution)/shard_map/ppermute | solution.py:287
  129.9 0.7 pad_add_fusion.1.here_ref
  130.6 0.9 collective-permute-done.21.p4
  131.6 0.6 copy-done.16
  132.2 9.2 %shard_map.187 = f32[1,512]{1,0:T(1,128)} custom-call(s32[2]{0:T(128)} %pad_add_fusion.1.here_ref, bf16[32,128]{1,0:T(8,128)(2,1)} %copy-done.13, bf16[32,128]{1,0:T(8,128)(2,1)} %copy-done.14, bf16[32,128]{1,0:T(8,128)(2,1)} %get-tuple-element.26.p2, bf16[32,128]{1,0:T(8,128)(2,1)} %copy-done.15, bf16[32,128]{1,0:T(8,128)(2,1)} %copy-done.16, ...), custom_call_target="tpu_custom_call" | custom-call | bytes 1048576 | tf_op jit(solution)/shard_map/pallas_call | solution.py:19
  (74 shorter events, 0.3 us)
Async XLA Ops:
  1.3 4.7 %copy-start.17 = (s32[1,1,1,3,128]{4,2,3,1,0:T(1,128)S(1)}, s32[1,1,1,3,128]{4,2,3,1,0:T(1,128)}, u32[]{:S(2)}) copy-start(s32[1,1,1,3,128]{4,2,3,1,0:T(1,128)} %param.29) | copy-start | bytes 4612
  2.7 4.5 %collective-permute-start = (f32[8,128]{1,0:T(8,128)}, f32[8,128]{1,0:T(8,128)S(1)}, u32[]{:S(2)}, u32[]{:S(2)}) collective-permute-start(f32[8,128]{1,0:T(8,128)} %shard_map.181), channel_id=1, source_target_pairs={{0,64},{64,128},{128,192},{192,0},{1,65},{65,129},{129,193},{193,1... | collective-permute-start | bytes 12296 | tf_op jit(solution)/shard_map/ppermute | solution.py:287
  4.7 2.7 %collective-permute-start.1 = (f32[8,128]{1,0:T(8,128)}, f32[8,128]{1,0:T(8,128)S(1)}, u32[]{:S(2)}, u32[]{:S(2)}) collective-permute-start(f32[8,128]{1,0:T(8,128)} %shard_map.181), channel_id=1, source_target_pairs={{0,192},{64,0},{128,64},{192,128},{1,193},{65,1},{129,65},{193,129... | collective-permute-start | bytes 12296 | tf_op jit(solution)/shard_map/ppermute | solution.py:287
  7.2 0.6 copy-start.6
  7.8 0.6 copy-start.7
  9.8 8.2 %collective-permute-start.2 = (f32[8,128]{1,0:T(8,128)}, f32[8,128]{1,0:T(8,128)S(1)}, u32[]{:S(2)}, u32[]{:S(2)}) collective-permute-start(f32[8,128]{1,0:T(8,128)} %shard_map.182), channel_id=1, source_target_pairs={{0,4},{4,8},{8,12},{12,16},{16,20},{20,24},{24,28},{28,32},{32,36}... | collective-permute-start | bytes 12296 | tf_op jit(solution)/shard_map/ppermute | solution.py:287
  11.3 6.7 %collective-permute-start.3 = (f32[8,128]{1,0:T(8,128)}, f32[8,128]{1,0:T(8,128)S(1)}, u32[]{:S(2)}, u32[]{:S(2)}) collective-permute-start(f32[8,128]{1,0:T(8,128)} %shard_map.182), channel_id=1, source_target_pairs={{0,60},{4,0},{8,4},{12,8},{16,12},{20,16},{24,20},{28,24},{32,28},... | collective-permute-start | bytes 12296 | tf_op jit(solution)/shard_map/ppermute | solution.py:287
  18.0 0.6 copy-start.10
  18.6 0.6 copy-start.11
  19.2 9.8 %copy-start.20 = (s32[1,1,1,512]{3,2,1,0:T(1,128)S(1)}, s32[1,1,1,512]{3,2,1,0:T(1,128)}, u32[]{:S(2)}) copy-start(s32[1,1,1,512]{3,2,1,0:T(1,128)} %param.30) | copy-start | bytes 6148
  20.7 12.3 %collective-permute-start.4 = (f32[8,128]{1,0:T(8,128)}, f32[8,128]{1,0:T(8,128)S(1)}, u32[]{:S(2)}, u32[]{:S(2)}) collective-permute-start(f32[8,128]{1,0:T(8,128)} %shard_map.183), channel_id=1, source_target_pairs={{0,1},{1,2},{2,3},{3,0},{4,5},{5,6},{6,7},{7,4},{8,9},{9,10},{10,1... | collective-permute-start | bytes 12296 | tf_op jit(solution)/shard_map/ppermute | solution.py:287
  29.0 7.2 %collective-permute-start.5 = (f32[8,128]{1,0:T(8,128)}, f32[8,128]{1,0:T(8,128)S(1)}, u32[]{:S(2)}, u32[]{:S(2)}) collective-permute-start(f32[8,128]{1,0:T(8,128)} %shard_map.183), channel_id=1, source_target_pairs={{0,3},{1,0},{2,1},{3,2},{4,7},{5,4},{6,5},{7,6},{8,11},{9,8},{10,9... | collective-permute-start | bytes 12296 | tf_op jit(solution)/shard_map/ppermute | solution.py:287
  33.0 3.2 %copy-start.18 = (f32[8,128]{1,0:T(8,128)}, f32[8,128]{1,0:T(8,128)S(1)}, u32[]{:S(2)}) copy-start(f32[8,128]{1,0:T(8,128)S(1)} %collective-permute-done.4.zl) | copy-start | bytes 12292
  36.2 0.6 copy-start.19
  54.2 2.9 %copy-start = (bf16[256,128]{1,0:T(8,128)(2,1)S(1)}, bf16[256,128]{1,0:T(8,128)(2,1)}, u32[]{:S(2)}) copy-start(bf16[256,128]{1,0:T(8,128)(2,1)} %shard_map.185.own_ref) | copy-start | bytes 196612
  54.3 3.9 %collective-permute-start.6 = (bf16[64,128]{1,0:T(8,128)(2,1)S(1)}, bf16[64,128]{1,0:T(8,128)(2,1)S(1)}, u32[]{:S(2)}, u32[]{:S(2)}) collective-permute-start(bf16[64,128]{1,0:T(8,128)(2,1)S(1)} %get-tuple-element.40), channel_id=1, source_target_pairs={{0,64},{64,128},{128,192},{192,0},{1,65},{65,129},{129,193},{193,1... | collective-permute-start | bytes 49160 | tf_op jit(solution)/shard_map/ppermute | solution.py:287
  55.3 2.9 %collective-permute-start.7 = (bf16[64,128]{1,0:T(8,128)(2,1)S(1)}, bf16[64,128]{1,0:T(8,128)(2,1)S(1)}, u32[]{:S(2)}, u32[]{:S(2)}) collective-permute-start(bf16[64,128]{1,0:T(8,128)(2,1)S(1)} %get-tuple-element.39), channel_id=1, source_target_pairs={{0,192},{64,0},{128,64},{192,128},{1,193},{65,1},{129,65},{193,129... | collective-permute-start | bytes 49160 | tf_op jit(solution)/shard_map/ppermute | solution.py:287
  58.2 6.3 %copy-start.2 = (bf16[64,128]{1,0:T(8,128)(2,1)}, bf16[64,128]{1,0:T(8,128)(2,1)S(1)}, u32[]{:S(2)}) copy-start(bf16[64,128]{1,0:T(8,128)(2,1)S(1)} %collective-permute-done.6.xl) | copy-start | bytes 49156
  58.2 6.3 %copy-start.3 = (bf16[64,128]{1,0:T(8,128)(2,1)}, bf16[64,128]{1,0:T(8,128)(2,1)S(1)}, u32[]{:S(2)}) copy-start(bf16[64,128]{1,0:T(8,128)(2,1)S(1)} %collective-permute-done.7.xh) | copy-start | bytes 49156
  59.1 6.6 %collective-permute-start.8 = (bf16[64,128]{1,0:T(8,128)(2,1)S(1)}, bf16[64,128]{1,0:T(8,128)(2,1)S(1)}, u32[]{:S(2)}, u32[]{:S(2)}) collective-permute-start(bf16[64,128]{1,0:T(8,128)(2,1)S(1)} %get-tuple-element.38), channel_id=1, source_target_pairs={{0,4},{4,8},{8,12},{12,16},{16,20},{20,24},{24,28},{28,32},{32,36}... | collective-permute-start | bytes 49160 | tf_op jit(solution)/shard_map/ppermute | solution.py:287
  59.2 7.1 %collective-permute-start.9 = (bf16[64,128]{1,0:T(8,128)(2,1)S(1)}, bf16[64,128]{1,0:T(8,128)(2,1)S(1)}, u32[]{:S(2)}, u32[]{:S(2)}) collective-permute-start(bf16[64,128]{1,0:T(8,128)(2,1)S(1)} %get-tuple-element.37), channel_id=1, source_target_pairs={{0,60},{4,0},{8,4},{12,8},{16,12},{20,16},{24,20},{28,24},{32,28},... | collective-permute-start | bytes 49160 | tf_op jit(solution)/shard_map/ppermute | solution.py:287
  65.6 0.6 copy-start.4
  66.2 0.6 copy-start.5
  67.6 5.0 %copy-start.12 = (bf16[4,128,8]{1,2,0:T(8,128)(2,1)S(1)}, bf16[4,128,8]{1,2,0:T(8,128)(2,1)}, u32[]{:S(2)}) copy-start(bf16[4,128,8]{1,2,0:T(8,128)(2,1)} %param.43) | copy-start | bytes 24580
  67.7 5.7 %collective-permute-start.10 = (bf16[64,128]{1,0:T(8,128)(2,1)S(1)}, bf16[64,128]{1,0:T(8,128)(2,1)S(1)}, u32[]{:S(2)}, u32[]{:S(2)}) collective-permute-start(bf16[64,128]{1,0:T(8,128)(2,1)S(1)} %get-tuple-element.36), channel_id=1, source_target_pairs={{0,1},{1,2},{2,3},{3,0},{4,5},{5,6},{6,7},{7,4},{8,9},{9,10},{10,1... | collective-permute-start | bytes 49160 | tf_op jit(solution)/shard_map/ppermute | solution.py:287
  72.5 7.1 %collective-permute-start.11 = (bf16[64,128]{1,0:T(8,128)(2,1)S(1)}, bf16[64,128]{1,0:T(8,128)(2,1)S(1)}, u32[]{:S(2)}, u32[]{:S(2)}) collective-permute-start(bf16[64,128]{1,0:T(8,128)(2,1)S(1)} %get-tuple-element.35), channel_id=1, source_target_pairs={{0,3},{1,0},{2,1},{3,2},{4,7},{5,4},{6,5},{7,6},{8,11},{9,8},{10,9... | collective-permute-start | bytes 49160 | tf_op jit(solution)/shard_map/ppermute | solution.py:287
  73.4 6.2 %copy-start.8 = (bf16[64,128]{1,0:T(8,128)(2,1)}, bf16[64,128]{1,0:T(8,128)(2,1)S(1)}, u32[]{:S(2)}) copy-start(bf16[64,128]{1,0:T(8,128)(2,1)S(1)} %collective-permute-done.10.zl) | copy-start | bytes 49156
  79.6 0.6 copy-start.9
  98.7 3.2 %copy-start.1 = (bf16[256,128]{1,0:T(8,128)(2,1)S(1)}, bf16[256,128]{1,0:T(8,128)(2,1)}, u32[]{:S(2)}) copy-start(bf16[256,128]{1,0:T(8,128)(2,1)} %shard_map.186) | copy-start | bytes 196612
  98.9 4.2 %collective-permute-start.12 = (bf16[64,128]{1,0:T(8,128)(2,1)S(1)}, bf16[64,128]{1,0:T(8,128)(2,1)S(1)}, u32[]{:S(2)}, u32[]{:S(2)}) collective-permute-start(bf16[64,128]{1,0:T(8,128)(2,1)S(1)} %get-tuple-element.34), channel_id=1, source_target_pairs={{0,64},{64,128},{128,192},{192,0},{1,65},{65,129},{129,193},{193,1... | collective-permute-start | bytes 49160 | tf_op jit(solution)/shard_map/ppermute | solution.py:287
  99.8 3.2 %collective-permute-start.13 = (bf16[64,128]{1,0:T(8,128)(2,1)S(1)}, bf16[64,128]{1,0:T(8,128)(2,1)S(1)}, u32[]{:S(2)}, u32[]{:S(2)}) collective-permute-start(bf16[64,128]{1,0:T(8,128)(2,1)S(1)} %get-tuple-element.33), channel_id=1, source_target_pairs={{0,192},{64,0},{128,64},{192,128},{1,193},{65,1},{129,65},{193,129... | collective-permute-start | bytes 49160 | tf_op jit(solution)/shard_map/ppermute | solution.py:287
  103.8 6.6 %collective-permute-start.14 = (bf16[64,128]{1,0:T(8,128)(2,1)S(1)}, bf16[64,128]{1,0:T(8,128)(2,1)S(1)}, u32[]{:S(2)}, u32[]{:S(2)}) collective-permute-start(bf16[64,128]{1,0:T(8,128)(2,1)S(1)} %get-tuple-element.32), channel_id=1, source_target_pairs={{0,4},{4,8},{8,12},{12,16},{16,20},{20,24},{24,28},{28,32},{32,36}... | collective-permute-start | bytes 49160 | tf_op jit(solution)/shard_map/ppermute | solution.py:287
  103.9 6.5 %collective-permute-start.15 = (bf16[64,128]{1,0:T(8,128)(2,1)S(1)}, bf16[64,128]{1,0:T(8,128)(2,1)S(1)}, u32[]{:S(2)}, u32[]{:S(2)}) collective-permute-start(bf16[64,128]{1,0:T(8,128)(2,1)S(1)} %get-tuple-element.31), channel_id=1, source_target_pairs={{0,60},{4,0},{8,4},{12,8},{16,12},{20,16},{24,20},{28,24},{32,28},... | collective-permute-start | bytes 49160 | tf_op jit(solution)/shard_map/ppermute | solution.py:287
  111.3 3.0 %collective-permute-start.16 = (bf16[64,128]{1,0:T(8,128)(2,1)S(1)}, bf16[64,128]{1,0:T(8,128)(2,1)S(1)}, u32[]{:S(2)}, u32[]{:S(2)}) collective-permute-start(bf16[64,128]{1,0:T(8,128)(2,1)S(1)} %get-tuple-element.30), channel_id=1, source_target_pairs={{0,1},{1,2},{2,3},{3,0},{4,5},{5,6},{6,7},{7,4},{8,9},{9,10},{10,1... | collective-permute-start | bytes 49160 | tf_op jit(solution)/shard_map/ppermute | solution.py:287
  113.4 7.1 %collective-permute-start.17 = (bf16[64,128]{1,0:T(8,128)(2,1)S(1)}, bf16[64,128]{1,0:T(8,128)(2,1)S(1)}, u32[]{:S(2)}, u32[]{:S(2)}) collective-permute-start(bf16[64,128]{1,0:T(8,128)(2,1)S(1)} %get-tuple-element.29), channel_id=1, source_target_pairs={{0,3},{1,0},{2,1},{3,2},{4,7},{5,4},{6,5},{7,6},{8,11},{9,8},{10,9... | collective-permute-start | bytes 49160 | tf_op jit(solution)/shard_map/ppermute | solution.py:287
  121.9 8.7 %collective-permute-start.18 = (bf16[32,128]{1,0:T(8,128)(2,1)S(1)}, bf16[32,128]{1,0:T(8,128)(2,1)S(1)}, u32[]{:S(2)}, u32[]{:S(2)}) collective-permute-start(bf16[32,128]{1,0:T(8,128)(2,1)S(1)} %get-tuple-element.28), channel_id=1, source_target_pairs={{0,8},{4,12},{8,16},{12,20},{16,24},{20,28},{24,32},{28,36},{32,40... | collective-permute-start | bytes 24584 | tf_op jit(solution)/shard_map/ppermute | solution.py:287
  121.9 8.7 %collective-permute-start.19 = (bf16[32,128]{1,0:T(8,128)(2,1)S(1)}, bf16[32,128]{1,0:T(8,128)(2,1)S(1)}, u32[]{:S(2)}, u32[]{:S(2)}) collective-permute-start(bf16[32,128]{1,0:T(8,128)(2,1)S(1)} %get-tuple-element.27), channel_id=1, source_target_pairs={{0,4},{4,8},{8,12},{12,16},{16,20},{20,24},{24,28},{28,32},{32,36}... | collective-permute-start | bytes 24584 | tf_op jit(solution)/shard_map/ppermute | solution.py:287
  122.0 8.7 %collective-permute-start.20 = (bf16[32,128]{1,0:T(8,128)(2,1)S(1)}, bf16[32,128]{1,0:T(8,128)(2,1)S(1)}, u32[]{:S(2)}, u32[]{:S(2)}) collective-permute-start(bf16[32,128]{1,0:T(8,128)(2,1)S(1)} %get-tuple-element.25), channel_id=1, source_target_pairs={{0,60},{4,0},{8,4},{12,8},{16,12},{20,16},{24,20},{28,24},{32,28},... | collective-permute-start | bytes 24584 | tf_op jit(solution)/shard_map/ppermute | solution.py:287
  127.6 4.0 %collective-permute-start.21 = (bf16[32,128]{1,0:T(8,128)(2,1)S(1)}, bf16[32,128]{1,0:T(8,128)(2,1)S(1)}, u32[]{:S(2)}, u32[]{:S(2)}) collective-permute-start(bf16[32,128]{1,0:T(8,128)(2,1)S(1)} %get-tuple-element.24), channel_id=1, source_target_pairs={{0,56},{4,60},{8,0},{12,4},{16,8},{20,12},{24,16},{28,20},{32,24},... | collective-permute-start | bytes 24584 | tf_op jit(solution)/shard_map/ppermute | solution.py:287
  130.6 1.0 copy-start.13
  130.6 1.0 copy-start.14
  130.6 1.0 copy-start.15
  131.6 0.6 copy-start.16

commit v2 on v1

v2 whole, which is shorter than its diff:
```python
import functools
import math

import jax
import jax.numpy as jnp
from jax import lax
from jax.experimental import pallas as pl
from jax.experimental.pallas import tpu as pltpu
from jax.sharding import PartitionSpec as P

BASIS = 8
F32 = jnp.float32
BF16 = jnp.bfloat16
VMEM = pl.BlockSpec(memory_space=pltpu.VMEM)


def call(kernel, out_shape, operands, scratch=(), limit=8, flops=0, moved=1 << 20):
    many = isinstance(out_shape, (list, tuple))
    return pl.pallas_call(
        kernel,
        out_shape=out_shape,
        in_specs=[VMEM] * len(operands),
        out_specs=[VMEM] * len(out_shape) if many else VMEM,
        scratch_shapes=list(scratch),
        compiler_params=pltpu.CompilerParams(vmem_limit_bytes=limit << 20),
        cost_estimate=pl.CostEstimate(flops=flops, bytes_accessed=moved, transcendentals=0),
    )(*operands)


def dot(a, b):
    return jnp.dot(a, b, preferred_element_type=F32)


def dot_first(a, b):
    return lax.dot_general(a, b, (((0,), (0,)), ((), ())), preferred_element_type=F32)


def harmonics(vx, vy, vz, weight):
    radius = jnp.sqrt(vx * vx + vy * vy + vz * vz)
    inverse = 1.0 / radius
    x, y, z = vx * inverse, vy * inverse, vz * inverse
    xx, yy, zz = x * x, y * y, z * z
    r3, r15, r5, r105, r7 = (math.sqrt(v) for v in (3.0, 15.0, 5.0, 105.0, 7.0))
    outer, inner = math.sqrt(35.0 / 8.0), math.sqrt(21.0 / 8.0)
    rows = [
        jnp.ones_like(x),
        r3 * x,
        r3 * y,
        r3 * z,
        r15 * x * y,
        r15 * y * z,
        0.5 * r5 * (3.0 * zz - 1.0),
        r15 * x * z,
        0.5 * r15 * (xx - yy),
        outer * y * (3.0 * xx - yy),
        r105 * x * y * z,
        inner * y * (5.0 * zz - 1.0),
        0.5 * r7 * z * (5.0 * zz - 3.0),
        inner * x * (5.0 * zz - 1.0),
        0.5 * r105 * z * (xx - yy),
        outer * x * (xx - 3.0 * yy),
    ]
    return [row * weight for row in rows], radius, inverse


def radial_basis(radius, inverse, cutoff):
    u = radius * (1.0 / cutoff)
    u2 = u * u
    envelope = 1.0 + u2 * u2 * u2 * (-28.0 + u * (48.0 - 21.0 * u))
    scale = math.sqrt(2.0 / cutoff) * inverse * envelope
    angle = radius * (math.pi / cutoff)
    before, now = jnp.zeros_like(angle), jnp.sin(angle)
    twice = 2.0 * jnp.cos(angle)
    rows = []
    for _ in range(BASIS):
        rows.append(now * scale)
        before, now = now, twice * now - before
    return rows


def sections(arrays):
    return jnp.where(lax.broadcasted_iota(jnp.int32, (8, 128), 1) < 64, arrays[1], arrays[0])


def swapped(index):
    return jnp.where(index >= 256, index ^ 64, index)


def species_rows(species_ref, pieces):
    parts = [jnp.broadcast_to(species_ref[...].astype(F32), (8, 256))]
    for first in range(0, len(pieces), 2):
        parts.append(sections((pieces[first][...], pieces[first + 1][...])))
    return jnp.concatenate(parts, axis=1)


def onehot_of(chosen, rows):
    row_ids = lax.broadcasted_iota(jnp.int32, (rows, chosen.shape[1]), 0)
    return jnp.where(row_ids == chosen, 1.0, 0.0).astype(BF16)


def section_list(lists_ref, section):
    return lists_ref[:, section * 128 : (section + 1) * 128]


def pick_species(section):
    def kernel(species_ref, lists_ref, *rest):
        table = species_rows(species_ref, rest[:-1]).astype(BF16)
        chosen = swapped(section_list(lists_ref, section))
        rest[-1][...] = dot(table, onehot_of(chosen, table.shape[1]))

    return kernel


def send_rows(lists_ref, section, table, low_ref, high_ref):
    chosen = dot_first(onehot_of(section_list(lists_ref, section), table.shape[0]), table)
    high_ref[...] = chosen[:64].astype(BF16)
    low_ref[...] = chosen[64:].astype(BF16)


def pick_rows(section):
    def kernel(lists_ref, *rest):
        table = jnp.concatenate([piece[...] for piece in rest[:-2]], axis=0)
        send_rows(lists_ref, section, table, *rest[-2:])

    return kernel


def by_group(x):
    rows, lanes = x.shape
    row = lax.broadcasted_iota(jnp.int32, x.shape, 0)
    block = lax.broadcasted_iota(jnp.int32, x.shape, 1) >> 3
    step = 1
    while step < rows:
        up = pltpu.roll(pltpu.roll(x, 8 * step, axis=1), rows - step, axis=0)
        down = pltpu.roll(pltpu.roll(x, lanes - 8 * step, axis=1), step, axis=0)
        moved = jnp.where((block & step) != 0, up, down)
        x = jnp.where(((row ^ block) & step) != 0, moved, x)
        step *= 2
    return x


def store_rows(ref, rows):
    for n, row in enumerate(rows):
        size = row.shape[0]
        for tile in range(ref.shape[0]):
            ref[tile, n * size : (n + 1) * size, :] = row[:, tile * 128 : (tile + 1) * 128]


def spread(ref, row):
    parts = [ref[tile, pl.ds(row, 8, stride=0), :] for tile in range(ref.shape[0])]
    return jnp.concatenate(parts, axis=1)


def basis_rows(ref, slot, slots):
    parts = [ref[tile, pl.ds(slot, BASIS, stride=slots), :] for tile in range(ref.shape[0])]
    return jnp.concatenate(parts, axis=1)


def geometry_kernel(
    vec_ref, count_ref, index_ref, in1_ref, in2_ref, y_ref, hid1_ref, hid2_ref, where_ref, phi
):
    slots, atoms = index_ref.shape
    live = lax.broadcasted_iota(jnp.int32, (slots, atoms), 0) < count_ref[...]
    weight = by_group(jnp.where(live, 0.25, 0.0))
    vx, vy, vz = (by_group(vec_ref[n]) for n in range(3))
    rows, radius, inverse = harmonics(vx, vy, vz, weight)
    store_rows(y_ref, rows)
    store_rows(phi, radial_basis(radius, inverse, 5.0))
    where_ref[...] = by_group(index_ref[...].astype(F32)).astype(jnp.int32)
    into1 = in1_ref[...].astype(F32).T.astype(BF16)
    into2 = in2_ref[...].astype(F32).T.astype(BF16)
    for g in range(slots):
        basis = basis_rows(phi, g, slots).astype(BF16)
        for into, out in ((into1, hid1_ref), (into2, hid2_ref)):
            value = dot(into, basis)
            out[g] = (value / (1.0 + jnp.exp(-value))).astype(BF16)


def group_sums(g, groups, out_t, hid_ref, y_ref, picked):
    radial = dot(out_t, hid_ref[g])
    own = (lax.broadcasted_iota(jnp.int32, (8, 256), 1) & 7) == lax.broadcasted_iota(
        jnp.int32, (8, 256), 0
    )
    sums = []
    for degree in range(4):
        weighted = (radial[degree * 128 : (degree + 1) * 128] * picked).astype(BF16)
        angular = [
            jnp.where(own, spread(y_ref, m * groups + g), 0.0)
            for m in range(degree * degree, (degree + 1) * (degree + 1))
        ]
        total = lax.dot_general(
            jnp.concatenate(angular, axis=0).astype(BF16),
            weighted,
            (((1,), (1,)), ((), ())),
            preferred_element_type=F32,
        )
        sums += [total[8 * m : 8 * (m + 1)] for m in range(2 * degree + 1)]
    return sums


def layer_one_kernel(
    species_ref, xl, xh, yl, yh, zl, zh, where_ref, y_ref, hid_ref, out_ref, emb_ref, msg1_ref,
    self_ref, mix_ref, msg2_ref, lists_ref, next_ref, low_ref, high_ref, kinds, feats,
):
    groups, edges = where_ref.shape
    atoms = species_ref.shape[1]
    table = species_rows(species_ref, (xl, xh, yl, yh, zl, zh))
    for row in range(0, groups, 8):
        for lane in range(0, edges, 128):
            where = swapped(where_ref[row : row + 8, lane : lane + 128])
            found = jnp.zeros((8, 128), F32)
            for b in range(5):
                part = jnp.take_along_axis(table[:, b * 128 : (b + 1) * 128], where & 127, axis=1)
                found = jnp.where((where >> 7) == b, part, found)
            kinds[lane // 128, row : row + 8, :] = found
    rows_t = dot(emb_ref[...], msg1_ref[...]).astype(BF16).astype(F32).T.astype(BF16)
    out_t = out_ref[...].astype(F32).T.astype(BF16)
    kind_ids = lax.broadcasted_iota(jnp.int32, (8, 256), 0).astype(F32)

    def pair(j, carry):
        parts = []
        for g in (2 * j, 2 * j + 1):
            onehot = jnp.where(spread(kinds, g) == kind_ids, 1.0, 0.0).astype(BF16)
            sums = group_sums(g, groups, out_t, hid_ref, y_ref, dot(rows_t, onehot))
            part = [sums[0]]
            for degree in (1, 2, 3):
                part.append(sum(v * v for v in sums[degree * degree : (degree + 1) ** 2]))
            parts.append(jnp.concatenate(part, axis=1))
        first = pl.multiple_of(j * 16, 16)
        feats[pl.ds(first, 16), :] = jnp.concatenate(parts, axis=0).astype(BF16)
        return carry

    lax.fori_loop(0, groups // 2, pair, 0, unroll=2)
    own = jnp.where(table[:, :atoms] == kind_ids, 1.0, 0.0).astype(BF16)
    start = dot_first(own, emb_ref[...]).astype(BF16)
    mixed = dot(start, self_ref[...]) + dot(feats[...], mix_ref[...])
    hidden = (mixed / (1.0 + jnp.exp(-mixed))).astype(BF16)
    message = dot(hidden, msg2_ref[...]).astype(BF16)
    next_ref[...] = message
    send_rows(lists_ref, 0, message, low_ref, high_ref)


def layer_two_kernel(
    own_ref, xl, xh, yl, yh, zl, zh, where_ref, y_ref, hid_ref, out_ref, dec_ref, lists_ref,
    coeff_ref, low_ref, high_ref, feats,
):
    groups, edges = where_ref.shape
    pieces = [piece[...].astype(F32) for piece in (own_ref, xl, xh, yl, yh, zl, zh)]
    table = jnp.concatenate(pieces + [jnp.zeros((128, 128), F32)], axis=0)
    rows_t = jnp.concatenate([table[256 * n : 256 * (n + 1)].T for n in range(3)], axis=0)
    rows_t = rows_t.astype(BF16)
    out_t = out_ref[...].astype(F32).T.astype(BF16)

    def pair(j, carry):
        parts = []
        for g in (2 * j, 2 * j + 1):
            where = where_ref[pl.ds(g, 1), :]
            found = dot(rows_t, onehot_of(where & 255, 256))
            picked = jnp.where(where < 256, found[:128], found[128:256])
            picked = jnp.where(where < 512, picked, found[256:])
            sums = group_sums(g, groups, out_t, hid_ref, y_ref, picked)
            parts.append(jnp.concatenate(sums, axis=1))
        first = pl.multiple_of(j * 16, 16)
        feats[pl.ds(first, 16), :] = jnp.concatenate(parts, axis=0).astype(BF16)
        return carry

    lax.fori_loop(0, groups // 2, pair, 0, unroll=2)
    column = lax.broadcasted_iota(jnp.int32, (8, 128), 1)
    repeat = (column & 7) == lax.broadcasted_iota(jnp.int32, (8, 128), 0)
    repeat = jnp.where(repeat, 1.0, 0.0).astype(BF16)
    group = lax.broadcasted_iota(jnp.int32, (128, 128), 1) >> 3
    blocks = []
    for degree in range(4):
        wide = dot_first(dec_ref[degree], repeat)
        for m in range(degree * degree, (degree + 1) * (degree + 1)):
            blocks.append(jnp.where(group == m, wide, 0.0).astype(BF16))
    coeffs = dot(feats[...], jnp.concatenate(blocks, axis=0)).astype(BF16)
    coeff_ref[...] = coeffs
    send_rows(lists_ref, 0, coeffs, low_ref, high_ref)


def brick_kernel(list_ref, *rest):
    table = jnp.concatenate([piece[...] for piece in rest[:7]], axis=0)
    chosen = dot_first(onehot_of(list_ref[...], table.shape[0]), table).astype(BF16)
    for n in range(5):
        rest[7 + n][...] = chosen[32 * n : 32 * (n + 1)]


def probe_kernel(list_ref, count_ref, vec_ref, y_ref, phi_ref):
    slots, probes = vec_ref.shape[1:]
    live = lax.broadcasted_iota(jnp.int32, (slots, probes), 0) < count_ref[...]
    weight = jnp.where(live, 0.125, 0.0)
    rows, radius, inverse = harmonics(vec_ref[0], vec_ref[1], vec_ref[2], weight)
    store_rows(y_ref, rows)
    store_rows(phi_ref, radial_basis(radius, inverse, 4.0))


def density_kernel(column, p0, p1, p2, p3, p4, index_ref, y, phi, out_ref):
    slots, probes = index_ref.shape
    here = lax.axis_index("gy")
    pieces = [piece[...].astype(F32) for piece in (p0, p1, p2, p3, p4)]
    table = jnp.concatenate(pieces + [jnp.zeros((96, 128), F32)], axis=0)
    rows_t = table.T[:, :160].astype(BF16)

    def slot(k, total):
        index = index_ref[pl.ds(k, 1), :]
        source = (index >> 5) - here + 2
        source = jnp.where(source < 0, source + column, source)
        source = jnp.where(source >= column, source - column, source)
        picked = dot(rows_t, onehot_of(source * 32 + (index & 31), 160))
        part = jnp.zeros((8, probes), F32)
        for m in range(16):
            part = part + spread(y, m * slots + k) * picked[m * 8 : (m + 1) * 8]
        return total + part * basis_rows(phi, k, slots)

    total = lax.fori_loop(0, slots, slot, jnp.zeros((8, probes), F32), unroll=2)
    out_ref[...] = jnp.sum(total, axis=0, keepdims=True)


def shifted(block, axis, step):
    size = lax.axis_size(axis)
    return lax.ppermute(block, axis, [(i, (i + step) % size) for i in range(size)])


def extend(rows, low, high, lists):
    half = jax.ShapeDtypeStruct((64, 128), BF16)
    pieces = []
    for section, axis in enumerate(("gx", "gy", "gz")):
        if section:
            low, high = call(pick_rows(section), (half, half), (lists, rows, *pieces))
        pieces += [shifted(low, axis, 1), shifted(high, axis, -1)]
    return pieces


def shards(
    species, neighbour_index, neighbour_count, edge_vectors, ghost_send, brick_send, probe_index,
    probe_count, probe_vectors, embedding, message_one, radial_in_one, radial_out_one, self_mix,
    basis_mix, message_two, radial_in_two, radial_out_two, decoder,
):
    slots, atoms = neighbour_index.shape[3:]
    probes = probe_index.shape[-1]
    kinds = species.reshape(1, atoms)
    lists = ghost_send.reshape(1, 384)
    shape = jax.ShapeDtypeStruct
    half = shape((64, 128), BF16)
    column = lax.axis_size("gy")
    here = lax.axis_index("gy")

    ghosts = []
    for section, axis in enumerate(("gx", "gy", "gz")):
        chosen = call(pick_species(section), shape((8, 128), F32), (kinds, lists, *ghosts))
        ghosts += [shifted(chosen, axis, 1), shifted(chosen, axis, -1)]
    angular, hidden_one, hidden_two, where = call(
        geometry_kernel,
        (
            shape((2, 16 * slots, 128), F32),
            shape((slots, 64, atoms), BF16),
            shape((slots, 64, atoms), BF16),
            shape((slots, atoms), jnp.int32),
        ),
        (
            edge_vectors.reshape(3, slots, atoms),
            neighbour_count.reshape(1, atoms),
            neighbour_index.reshape(slots, atoms),
            radial_in_one,
            radial_in_two,
        ),
        [pltpu.VMEM((2, BASIS * slots, 128), F32)],
    )
    probe_y, probe_phi = call(
        probe_kernel,
        (shape((probes // 128, 16 * slots, 128), F32), shape((probes // 128, 256, 128), F32)),
        (lists, probe_count.reshape(1, probes), probe_vectors.reshape(3, slots, probes)),
    )
    bricks = brick_send.reshape(1, -1)
    bricks = jnp.concatenate([bricks, bricks], axis=1)
    nearby = lax.dynamic_slice_in_dim(bricks, ((here + column - 2) % column) * 32, 160, 1)
    second = call(
        layer_one_kernel,
        (shape((atoms, 128), BF16), half, half),
        (kinds, *ghosts, where, angular, hidden_one, radial_out_one, embedding, message_one,
         self_mix, basis_mix, message_two, lists),
        [pltpu.VMEM((2, slots, 128), F32), pltpu.VMEM((atoms, 512), BF16)],
        limit=16,
    )
    coeffs = call(
        layer_two_kernel,
        (shape((atoms, 128), BF16), half, half),
        (second[0], *extend(*second, lists), where, angular, hidden_two, radial_out_two,
         decoder.transpose(0, 2, 1), lists),
        [pltpu.VMEM((atoms, 2048), BF16)],
        limit=16,
    )
    sent = call(
        brick_kernel, [shape((32, 128), BF16)] * 5, (nearby, coeffs[0], *extend(*coeffs, lists))
    )
    pieces = []
    for n in range(5):
        step = 2 - n
        pieces.append(shifted(sent[step + 2], "gy", step) if step else sent[2])
    density = call(
        functools.partial(density_kernel, column),
        shape((1, probes), F32),
        (*pieces, probe_index.reshape(slots, probes), probe_y, probe_phi),
    )
    return density.reshape(1, 1, 1, probes)


def solution(mesh):
    domain = ("gx", "gy", "gz")
    placed = tuple(P(*domain) for _ in range(9)) + tuple(P() for _ in range(10))
    return jax.shard_map(
        shards, mesh=mesh, in_specs=placed, out_specs=P(*domain), check_vma=False
    )
```

time: 142 us -> 116 us (0.82)
  Pallas kernels: 50.5 us -> 31.2 us
  local copies, waits for them, and re-layouts: 14.5 us -> 8.12 us
  starting transfers between devices: 50.4 us -> 53.3 us
    pallas_call x7 -> x13, Pallas kernels: 50.5 us -> 31.2 us  [call(): pl.pallas_call(kernel, out_shape=out_shape, in_specs=[VMEM] * len(operand...]
    gather x7 -> x0, local copies, waits for them, and re-layouts: 6.58 us -> none  [the longest x6 5.83 us: extend(): chosen = jnp.take(table, lists[section], axis=0)]
    ppermute x22, starting transfers between devices: 50.4 us -> 53.3 us  [shifted(): lax.ppermute(block, axis, [(i, (i + step) % size) for i in range(size)])]
    unnamed x53 -> x40, local copies, waits for them, and re-layouts: 7.28 us -> 8.12 us
  transfers between devices with their start and end apart: 22 -> 22, of which waited for: 12 -> 13; matrix products, arithmetic and copies ran while one was open for 1% -> 0% of each run, Pallas kernels for 3% -> 2%
where the time goes in v2:
time: 116 us
  starting transfers between devices  53.3 us (46%)
  Pallas kernels  31.2 us (27%)
  waiting for transfers between devices  22.9 us (20%)
  local copies, waits for them, and re-layouts  8.12 us (7%)
    ppermute x22, starting transfers between devices, shifted(): lax.ppermute(block, axis, [(i, (i + step) % size) for i in range(size)])  53.3 us
    pallas_call x13, Pallas kernels, call(): pl.pallas_call(kernel, out_shape=out_shape, in_specs=[VMEM] * len(operand...  31.2 us
    ppermute x22, waiting for transfers between devices, shifted(): lax.ppermute(block, axis, [(i, (i + step) % size) for i in range(size)])  22.9 us
    unnamed x40, local copies, waits for them, and re-layouts  8.12 us
  transfers between devices with their start and end apart: 22, of which 13 were waited for; matrix products, arithmetic and copies ran while one was open for 0% of the time, Pallas kernels for 2%

profile of v2, /device:TPU:1, one launch (start us, length us, event | category | flops | bytes accessed | tf_op | source)
XLA Modules:
  0.0 115.8 jit_solution(6585135496602449351)
XLA Ops:
  0.0 0.7 copy-done.1
  0.7 0.7 copy-done.11
  1.4 0.1 shard_map.181
  1.5 2.0 %collective-permute-start = (f32[8,128]{1,0:T(8,128)S(1)}, f32[8,128]{1,0:T(8,128)S(1)}, u32[]{:S(2)}, u32[]{:S(2)}) collective-permute-start(f32[8,128]{1,0:T(8,128)S(1)} %shard_map.181), channel_id=1, source_target_pairs={{0,64},{64,128},{128,192},{192,0},{1,65},{65,129},{129,193},{193,1... | collective-permute-start | bytes 12296 | tf_op jit(solution)/shard_map/ppermute | solution.py:322
  3.5 1.3 %collective-permute-start.1 = (f32[8,128]{1,0:T(8,128)S(1)}, f32[8,128]{1,0:T(8,128)S(1)}, u32[]{:S(2)}, u32[]{:S(2)}) collective-permute-start(f32[8,128]{1,0:T(8,128)S(1)} %shard_map.181), channel_id=1, source_target_pairs={{0,192},{64,0},{128,64},{192,128},{1,193},{65,1},{129,65},{193,129... | collective-permute-start | bytes 12296 | tf_op jit(solution)/shard_map/ppermute | solution.py:322
  4.8 0.9 collective-permute-done.rest_0_.xl
  5.8 0.2 collective-permute-done.1.rest_1_.xh
  6.0 0.1 shard_map.182
  6.1 1.3 %collective-permute-start.2 = (f32[8,128]{1,0:T(8,128)S(1)}, f32[8,128]{1,0:T(8,128)S(1)}, u32[]{:S(2)}, u32[]{:S(2)}) collective-permute-start(f32[8,128]{1,0:T(8,128)S(1)} %shard_map.182), channel_id=1, source_target_pairs={{0,4},{4,8},{8,12},{12,16},{16,20},{20,24},{24,28},{28,32},{32,36}... | collective-permute-start | bytes 12296 | tf_op jit(solution)/shard_map/ppermute | solution.py:322
  7.4 5.6 %collective-permute-start.3 = (f32[8,128]{1,0:T(8,128)S(1)}, f32[8,128]{1,0:T(8,128)S(1)}, u32[]{:S(2)}, u32[]{:S(2)}) collective-permute-start(f32[8,128]{1,0:T(8,128)S(1)} %shard_map.182), channel_id=1, source_target_pairs={{0,60},{4,0},{8,4},{12,8},{16,12},{20,16},{24,20},{28,24},{32,28},... | collective-permute-start | bytes 12296 | tf_op jit(solution)/shard_map/ppermute | solution.py:322
  13.0 0.9 collective-permute-done.2.rest_2_.yl
  13.9 0.0 collective-permute-done.3.rest_3_.yh
  13.9 0.1 shard_map.183
  14.1 8.6 %collective-permute-start.4 = (f32[8,128]{1,0:T(8,128)S(1)}, f32[8,128]{1,0:T(8,128)S(1)}, u32[]{:S(2)}, u32[]{:S(2)}) collective-permute-start(f32[8,128]{1,0:T(8,128)S(1)} %shard_map.183), channel_id=1, source_target_pairs={{0,1},{1,2},{2,3},{3,0},{4,5},{5,6},{6,7},{7,4},{8,9},{9,10},{10,1... | collective-permute-start | bytes 12296 | tf_op jit(solution)/shard_map/ppermute | solution.py:322
  22.7 0.0 collective-permute-start.5
  22.7 0.9 copy-done.3
  23.6 0.8 copy-done.10
  24.3 0.7 copy-done.14
  25.0 0.7 copy-done.15
  25.7 0.7 copy-done.18
  26.4 1.9 %shard_map.184 = (f32[2,512,128]{2,1,0:T(8,128)S(1)}, bf16[32,64,256]{2,1,0:T(8,128)(2,1)S(1)}, bf16[32,64,256]{2,1,0:T(8,128)(2,1)S(1)}, s32[32,256]{1,0:T(8,128)S(1)}) custom-call(f32[3,32,256]{2,1,0:T(8,128)S(1)} %bitcast.22, s32[1,256]{1,0:T(1,128)S(1)} %bitcast.31, s32[32,256]{1,0:T(8,128)S(1)} %bitcast.24, bf16[8,64]{1,0:T(8,128)(2,1)S(1)} %copy-done.14, ...), custom_call_target="tpu_custom_call" | custom-call | bytes 1048576 | tf_op jit(solution)/shard_map/pallas_call | solution.py:19
  28.3 0.0 collective-permute-done.4.zl
  28.3 1.3 %collective-permute-done.5.zh = f32[8,128]{1,0:T(8,128)S(1)} collective-permute-done((f32[8,128]{1,0:T(8,128)S(1)}, f32[8,128]{1,0:T(8,128)S(1)}, u32[]{:S(2)}, u32[]{:S(2)}) %collective-permute-start.5) | collective-permute-done | bytes 4128 | tf_op jit(solution)/shard_map/ppermute | solution.py:322
  29.6 0.7 copy-done.17
  30.3 0.0 copy-done.12
  30.3 0.8 copy-done.4
  31.2 0.8 copy-done.8
  31.9 0.8 copy-done.9
  32.7 10.7 %shard_map.185 = (bf16[256,128]{1,0:T(8,128)(2,1)S(1)}, bf16[64,128]{1,0:T(8,128)(2,1)S(1)}, bf16[64,128]{1,0:T(8,128)(2,1)S(1)}) custom-call(s32[1,256]{1,0:T(1,128)S(1)} %bitcast.28, f32[8,128]{1,0:T(8,128)S(1)} %collective-permute-done.rest_0_.xl, f32[8,128]{1,0:T(8,128)S(1)} %collective-permute-done.1.rest_1_.xh, ...), custom_call_target="tpu_custom_call" | custom-call | bytes 1048576 | tf_op jit(solution)/shard_map/pallas_call | solution.py:19
  43.4 1.3 %collective-permute-start.6 = (bf16[64,128]{1,0:T(8,128)(2,1)S(1)}, bf16[64,128]{1,0:T(8,128)(2,1)S(1)}, u32[]{:S(2)}, u32[]{:S(2)}) collective-permute-start(bf16[64,128]{1,0:T(8,128)(2,1)S(1)} %get-tuple-element.34), channel_id=1, source_target_pairs={{0,64},{64,128},{128,192},{192,0},{1,65},{65,129},{129,193},{193,1... | collective-permute-start | bytes 49160 | tf_op jit(solution)/shard_map/ppermute | solution.py:322
  44.7 1.6 %collective-permute-start.7 = (bf16[64,128]{1,0:T(8,128)(2,1)S(1)}, bf16[64,128]{1,0:T(8,128)(2,1)S(1)}, u32[]{:S(2)}, u32[]{:S(2)}) collective-permute-start(bf16[64,128]{1,0:T(8,128)(2,1)S(1)} %get-tuple-element.35), channel_id=1, source_target_pairs={{0,192},{64,0},{128,64},{192,128},{1,193},{65,1},{129,65},{193,129... | collective-permute-start | bytes 49160 | tf_op jit(solution)/shard_map/ppermute | solution.py:322
  46.2 1.0 collective-permute-done.6.rest_1_.xl
  47.3 0.2 shard_map.186
  47.5 0.1 collective-permute-start.8
  47.6 0.0 copy-start.6
  47.6 5.7 %collective-permute-start.9 = (bf16[64,128]{1,0:T(8,128)(2,1)S(1)}, bf16[64,128]{1,0:T(8,128)(2,1)S(1)}, u32[]{:S(2)}, u32[]{:S(2)}) collective-permute-start(bf16[64,128]{1,0:T(8,128)(2,1)S(1)} %get-tuple-element.37), channel_id=1, source_target_pairs={{0,60},{4,0},{8,4},{12,8},{16,12},{20,16},{24,20},{28,24},{32,28},... | collective-permute-start | bytes 49160 | tf_op jit(solution)/shard_map/ppermute | solution.py:322
  53.3 1.0 collective-permute-done.8.rest_3_.yl
  54.4 0.2 shard_map.187
  54.6 6.8 %collective-permute-start.10 = (bf16[64,128]{1,0:T(8,128)(2,1)S(1)}, bf16[64,128]{1,0:T(8,128)(2,1)S(1)}, u32[]{:S(2)}, u32[]{:S(2)}) collective-permute-start(bf16[64,128]{1,0:T(8,128)(2,1)S(1)} %get-tuple-element.38), channel_id=1, source_target_pairs={{0,1},{1,2},{2,3},{3,0},{4,5},{5,6},{6,7},{7,4},{8,9},{9,10},{10,1... | collective-permute-start | bytes 49160 | tf_op jit(solution)/shard_map/ppermute | solution.py:322
  61.3 0.0 collective-permute-start.11
  61.3 0.9 collective-permute-done.10.zl
  62.2 6.2 %collective-permute-done.11.zh = bf16[64,128]{1,0:T(8,128)(2,1)S(1)} collective-permute-done((bf16[64,128]{1,0:T(8,128)(2,1)S(1)}, bf16[64,128]{1,0:T(8,128)(2,1)S(1)}, u32[]{:S(2)}, u32[]{:S(2)}) %collective-permute-start.11) | collective-permute-done | bytes 16416 | tf_op jit(solution)/shard_map/ppermute | solution.py:322
  68.4 11.8 %shard_map.188 = (bf16[256,128]{1,0:T(8,128)(2,1)S(1)}, bf16[64,128]{1,0:T(8,128)(2,1)S(1)}, bf16[64,128]{1,0:T(8,128)(2,1)S(1)}) custom-call(bf16[256,128]{1,0:T(8,128)(2,1)S(1)} %get-tuple-element.33.rest_0_.own_ref, bf16[64,128]{1,0:T(8,128)(2,1)S(1)} %collective-permute-done.6.rest_1_.xl, bf16[64,128]{1,0:T(8,128)(2,1)S(1)} %collective-permute-done.7.rest_2_.xh, ...), custom_call_target="tpu_custom_call" | custom-call | bytes 1048576 | tf_op jit(solution)/shard_map/pallas_call | solution.py:19
  80.2 1.0 collective-permute-start.12
  81.2 1.8 %collective-permute-start.13 = (bf16[64,128]{1,0:T(8,128)(2,1)S(1)}, bf16[64,128]{1,0:T(8,128)(2,1)S(1)}, u32[]{:S(2)}, u32[]{:S(2)}) collective-permute-start(bf16[64,128]{1,0:T(8,128)(2,1)S(1)} %get-tuple-element.43), channel_id=1, source_target_pairs={{0,192},{64,0},{128,64},{192,128},{1,193},{65,1},{129,65},{193,129... | collective-permute-start | bytes 49160 | tf_op jit(solution)/shard_map/ppermute | solution.py:322
  83.0 1.0 collective-permute-done.12.rest_1_
  84.1 0.2 shard_map.189
  84.3 0.0 copy-start
  84.3 0.1 collective-permute-start.14
  84.4 5.8 %collective-permute-start.15 = (bf16[64,128]{1,0:T(8,128)(2,1)S(1)}, bf16[64,128]{1,0:T(8,128)(2,1)S(1)}, u32[]{:S(2)}, u32[]{:S(2)}) collective-permute-start(bf16[64,128]{1,0:T(8,128)(2,1)S(1)} %get-tuple-element.45), channel_id=1, source_target_pairs={{0,60},{4,0},{8,4},{12,8},{16,12},{20,16},{24,20},{28,24},{32,28},... | collective-permute-start | bytes 49160 | tf_op jit(solution)/shard_map/ppermute | solution.py:322
  90.2 1.0 collective-permute-done.14.rest_3_
  91.3 0.2 shard_map.190
  91.5 2.1 %collective-permute-start.16 = (bf16[64,128]{1,0:T(8,128)(2,1)S(1)}, bf16[64,128]{1,0:T(8,128)(2,1)S(1)}, u32[]{:S(2)}, u32[]{:S(2)}) collective-permute-start(bf16[64,128]{1,0:T(8,128)(2,1)S(1)} %get-tuple-element.46), channel_id=1, source_target_pairs={{0,1},{1,2},{2,3},{3,0},{4,5},{5,6},{6,7},{7,4},{8,9},{9,10},{10,1... | collective-permute-start | bytes 49160 | tf_op jit(solution)/shard_map/ppermute | solution.py:322
  93.6 0.1 fusion.list_ref
  93.7 0.8 collective-permute-done.16.rest_5_
  94.5 6.2 %collective-permute-done.17.rest_6_ = bf16[64,128]{1,0:T(8,128)(2,1)S(1)} collective-permute-done((bf16[64,128]{1,0:T(8,128)(2,1)S(1)}, bf16[64,128]{1,0:T(8,128)(2,1)S(1)}, u32[]{:S(2)}, u32[]{:S(2)}) %collective-permute-start.17) | collective-permute-done | bytes 16416 | tf_op jit(solution)/shard_map/ppermute | solution.py:322
  100.7 0.3 shard_map.191
  101.0 0.1 collective-permute-start.18
  101.1 0.1 collective-permute-start.19
  101.1 5.8 %collective-permute-start.20 = (bf16[32,128]{1,0:T(8,128)(2,1)S(1)}, bf16[32,128]{1,0:T(8,128)(2,1)S(1)}, u32[]{:S(2)}, u32[]{:S(2)}) collective-permute-start(bf16[32,128]{1,0:T(8,128)(2,1)S(1)} %get-tuple-element.51), channel_id=1, source_target_pairs={{0,60},{4,0},{8,4},{12,8},{16,12},{20,16},{24,20},{28,24},{32,28},... | collective-permute-start | bytes 24584 | tf_op jit(solution)/shard_map/ppermute | solution.py:322
  107.0 2.2 %collective-permute-start.21 = (bf16[32,128]{1,0:T(8,128)(2,1)S(1)}, bf16[32,128]{1,0:T(8,128)(2,1)S(1)}, u32[]{:S(2)}, u32[]{:S(2)}) collective-permute-start(bf16[32,128]{1,0:T(8,128)(2,1)S(1)} %get-tuple-element.52), channel_id=1, source_target_pairs={{0,56},{4,60},{8,0},{12,4},{16,8},{20,12},{24,16},{28,20},{32,24},... | collective-permute-start | bytes 24584 | tf_op jit(solution)/shard_map/ppermute | solution.py:322
  109.2 0.5 shard_map.192
  109.7 1.3 %collective-permute-done.21.p4 = bf16[32,128]{1,0:T(8,128)(2,1)S(1)} collective-permute-done((bf16[32,128]{1,0:T(8,128)(2,1)S(1)}, bf16[32,128]{1,0:T(8,128)(2,1)S(1)}, u32[]{:S(2)}, u32[]{:S(2)}) %collective-permute-start.21) | collective-permute-done | bytes 8224 | tf_op jit(solution)/shard_map/ppermute | solution.py:322
  111.0 4.8 %shard_map.193 = f32[1,512]{1,0:T(1,128)} custom-call(bf16[32,128]{1,0:T(8,128)(2,1)S(1)} %collective-permute-done.18.p0, bf16[32,128]{1,0:T(8,128)(2,1)S(1)} %collective-permute-done.19.p1, bf16[32,128]{1,0:T(8,128)(2,1)S(1)} %get-tuple-element.50.p2, bf16[32,128]{1,0:T(8,128)(2,1)S(1)} %collective-permute-done.20.p3, ...), custom_call_target="tpu_custom_call" | custom-call | bytes 1048576 | tf_op jit(solution)/shard_map/pallas_call | solution.py:19
  (34 shorter events, 0.1 us)
Async XLA Ops:
  0.0 0.7 copy-start.1
  0.0 29.6 %copy-start.2 = (bf16[512,128]{1,0:T(8,128)(2,1)S(1)}, bf16[512,128]{1,0:T(8,128)(2,1)}, u32[]{:S(2)}) copy-start(bf16[512,128]{1,0:T(8,128)(2,1)} %mix_ref.1) | copy-start | bytes 393220
  0.7 0.7 copy-start.11
  1.5 4.3 %collective-permute-start = (f32[8,128]{1,0:T(8,128)S(1)}, f32[8,128]{1,0:T(8,128)S(1)}, u32[]{:S(2)}, u32[]{:S(2)}) collective-permute-start(f32[8,128]{1,0:T(8,128)S(1)} %shard_map.181), channel_id=1, source_target_pairs={{0,64},{64,128},{128,192},{192,0},{1,65},{65,129},{129,193},{193,1... | collective-permute-start | bytes 12296 | tf_op jit(solution)/shard_map/ppermute | solution.py:322
  3.5 2.5 %collective-permute-start.1 = (f32[8,128]{1,0:T(8,128)S(1)}, f32[8,128]{1,0:T(8,128)S(1)}, u32[]{:S(2)}, u32[]{:S(2)}) collective-permute-start(f32[8,128]{1,0:T(8,128)S(1)} %shard_map.181), channel_id=1, source_target_pairs={{0,192},{64,0},{128,64},{192,128},{1,193},{65,1},{129,65},{193,129... | collective-permute-start | bytes 12296 | tf_op jit(solution)/shard_map/ppermute | solution.py:322
  6.1 7.8 %collective-permute-start.2 = (f32[8,128]{1,0:T(8,128)S(1)}, f32[8,128]{1,0:T(8,128)S(1)}, u32[]{:S(2)}, u32[]{:S(2)}) collective-permute-start(f32[8,128]{1,0:T(8,128)S(1)} %shard_map.182), channel_id=1, source_target_pairs={{0,4},{4,8},{8,12},{12,16},{16,20},{20,24},{24,28},{28,32},{32,36}... | collective-permute-start | bytes 12296 | tf_op jit(solution)/shard_map/ppermute | solution.py:322
  7.4 6.5 %collective-permute-start.3 = (f32[8,128]{1,0:T(8,128)S(1)}, f32[8,128]{1,0:T(8,128)S(1)}, u32[]{:S(2)}, u32[]{:S(2)}) collective-permute-start(f32[8,128]{1,0:T(8,128)S(1)} %shard_map.182), channel_id=1, source_target_pairs={{0,60},{4,0},{8,4},{12,8},{16,12},{20,16},{24,20},{28,24},{32,28},... | collective-permute-start | bytes 12296 | tf_op jit(solution)/shard_map/ppermute | solution.py:322
  14.1 14.3 %collective-permute-start.4 = (f32[8,128]{1,0:T(8,128)S(1)}, f32[8,128]{1,0:T(8,128)S(1)}, u32[]{:S(2)}, u32[]{:S(2)}) collective-permute-start(f32[8,128]{1,0:T(8,128)S(1)} %shard_map.183), channel_id=1, source_target_pairs={{0,1},{1,2},{2,3},{3,0},{4,5},{5,6},{6,7},{7,4},{8,9},{9,10},{10,1... | collective-permute-start | bytes 12296 | tf_op jit(solution)/shard_map/ppermute | solution.py:322
  22.7 6.9 %collective-permute-start.5 = (f32[8,128]{1,0:T(8,128)S(1)}, f32[8,128]{1,0:T(8,128)S(1)}, u32[]{:S(2)}, u32[]{:S(2)}) collective-permute-start(f32[8,128]{1,0:T(8,128)S(1)} %shard_map.183), channel_id=1, source_target_pairs={{0,3},{1,0},{2,1},{3,2},{4,7},{5,4},{6,5},{7,6},{8,11},{9,8},{10,9... | collective-permute-start | bytes 12296 | tf_op jit(solution)/shard_map/ppermute | solution.py:322
  22.7 0.9 copy-start.3
  23.6 0.8 copy-start.10
  24.3 0.7 copy-start.14
  25.0 0.7 copy-start.15
  25.7 0.7 copy-start.18
  26.4 3.3 %copy-start.7 = (bf16[128,128]{1,0:T(8,128)(2,1)S(1)}, bf16[128,128]{1,0:T(8,128)(2,1)}, u32[]{:S(2)}) copy-start(bf16[128,128]{1,0:T(8,128)(2,1)} %msg1_ref.1) | copy-start | bytes 98308
  29.6 0.7 copy-start.17
  29.6 0.7 copy-start.12
  30.3 0.8 copy-start.4
  31.2 0.8 copy-start.8
  31.9 0.8 copy-start.9
  43.4 3.9 %collective-permute-start.6 = (bf16[64,128]{1,0:T(8,128)(2,1)S(1)}, bf16[64,128]{1,0:T(8,128)(2,1)S(1)}, u32[]{:S(2)}, u32[]{:S(2)}) collective-permute-start(bf16[64,128]{1,0:T(8,128)(2,1)S(1)} %get-tuple-element.34), channel_id=1, source_target_pairs={{0,64},{64,128},{128,192},{192,0},{1,65},{65,129},{129,193},{193,1... | collective-permute-start | bytes 49160 | tf_op jit(solution)/shard_map/ppermute | solution.py:322
  44.7 2.6 %collective-permute-start.7 = (bf16[64,128]{1,0:T(8,128)(2,1)S(1)}, bf16[64,128]{1,0:T(8,128)(2,1)S(1)}, u32[]{:S(2)}, u32[]{:S(2)}) collective-permute-start(bf16[64,128]{1,0:T(8,128)(2,1)S(1)} %get-tuple-element.35), channel_id=1, source_target_pairs={{0,192},{64,0},{128,64},{192,128},{1,193},{65,1},{129,65},{193,129... | collective-permute-start | bytes 49160 | tf_op jit(solution)/shard_map/ppermute | solution.py:322
  47.5 6.9 %collective-permute-start.8 = (bf16[64,128]{1,0:T(8,128)(2,1)S(1)}, bf16[64,128]{1,0:T(8,128)(2,1)S(1)}, u32[]{:S(2)}, u32[]{:S(2)}) collective-permute-start(bf16[64,128]{1,0:T(8,128)(2,1)S(1)} %get-tuple-element.36), channel_id=1, source_target_pairs={{0,4},{4,8},{8,12},{12,16},{16,20},{20,24},{24,28},{28,32},{32,36}... | collective-permute-start | bytes 49160 | tf_op jit(solution)/shard_map/ppermute | solution.py:322
  47.6 20.8 %copy-start.6 = (bf16[64,512]{1,0:T(8,128)(2,1)S(1)}, bf16[64,512]{1,0:T(8,128)(2,1)}, u32[]{:S(2)}) copy-start(bf16[64,512]{1,0:T(8,128)(2,1)} %out_ref.3) | copy-start | bytes 196612
  47.6 6.8 %collective-permute-start.9 = (bf16[64,128]{1,0:T(8,128)(2,1)S(1)}, bf16[64,128]{1,0:T(8,128)(2,1)S(1)}, u32[]{:S(2)}, u32[]{:S(2)}) collective-permute-start(bf16[64,128]{1,0:T(8,128)(2,1)S(1)} %get-tuple-element.37), channel_id=1, source_target_pairs={{0,60},{4,0},{8,4},{12,8},{16,12},{20,16},{24,20},{28,24},{32,28},... | collective-permute-start | bytes 49160 | tf_op jit(solution)/shard_map/ppermute | solution.py:322
  54.4 14.1 %copy-start.13 = (bf16[4,128,8]{1,2,0:T(8,128)(2,1)S(1)}, bf16[4,128,8]{1,2,0:T(8,128)(2,1)}, u32[]{:S(2)}) copy-start(bf16[4,128,8]{1,2,0:T(8,128)(2,1)} %param.37) | copy-start | bytes 24580
  54.6 7.6 %collective-permute-start.10 = (bf16[64,128]{1,0:T(8,128)(2,1)S(1)}, bf16[64,128]{1,0:T(8,128)(2,1)S(1)}, u32[]{:S(2)}, u32[]{:S(2)}) collective-permute-start(bf16[64,128]{1,0:T(8,128)(2,1)S(1)} %get-tuple-element.38), channel_id=1, source_target_pairs={{0,1},{1,2},{2,3},{3,0},{4,5},{5,6},{6,7},{7,4},{8,9},{9,10},{10,1... | collective-permute-start | bytes 49160 | tf_op jit(solution)/shard_map/ppermute | solution.py:322
  61.3 7.1 %collective-permute-start.11 = (bf16[64,128]{1,0:T(8,128)(2,1)S(1)}, bf16[64,128]{1,0:T(8,128)(2,1)S(1)}, u32[]{:S(2)}, u32[]{:S(2)}) collective-permute-start(bf16[64,128]{1,0:T(8,128)(2,1)S(1)} %get-tuple-element.39), channel_id=1, source_target_pairs={{0,3},{1,0},{2,1},{3,2},{4,7},{5,4},{6,5},{7,6},{8,11},{9,8},{10,9... | collective-permute-start | bytes 49160 | tf_op jit(solution)/shard_map/ppermute | solution.py:322
  80.2 3.9 %collective-permute-start.12 = (bf16[64,128]{1,0:T(8,128)(2,1)S(1)}, bf16[64,128]{1,0:T(8,128)(2,1)S(1)}, u32[]{:S(2)}, u32[]{:S(2)}) collective-permute-start(bf16[64,128]{1,0:T(8,128)(2,1)S(1)} %get-tuple-element.42), channel_id=1, source_target_pairs={{0,64},{64,128},{128,192},{192,0},{1,65},{65,129},{129,193},{193,1... | collective-permute-start | bytes 49160 | tf_op jit(solution)/shard_map/ppermute | solution.py:322
  81.2 2.9 %collective-permute-start.13 = (bf16[64,128]{1,0:T(8,128)(2,1)S(1)}, bf16[64,128]{1,0:T(8,128)(2,1)S(1)}, u32[]{:S(2)}, u32[]{:S(2)}) collective-permute-start(bf16[64,128]{1,0:T(8,128)(2,1)S(1)} %get-tuple-element.43), channel_id=1, source_target_pairs={{0,192},{64,0},{128,64},{192,128},{1,193},{65,1},{129,65},{193,129... | collective-permute-start | bytes 49160 | tf_op jit(solution)/shard_map/ppermute | solution.py:322
  84.1 9.5 %copy-start.19 = (s32[1,1,1,512]{3,2,1,0:T(1,128)S(1)}, s32[1,1,1,512]{3,2,1,0:T(1,128)}, u32[]{:S(2)}) copy-start(s32[1,1,1,512]{3,2,1,0:T(1,128)} %param.24) | copy-start | bytes 6148
  84.3 24.8 %copy-start = (f32[1,1,1,3,32,512]{5,4,3,2,1,0:T(8,128)S(1)}, f32[1,1,1,3,32,512]{5,4,3,2,1,0:T(8,128)}, u32[]{:S(2)}) copy-start(f32[1,1,1,3,32,512]{5,4,3,2,1,0:T(8,128)} %param.27) | copy-start | bytes 589828
  84.3 6.9 %collective-permute-start.14 = (bf16[64,128]{1,0:T(8,128)(2,1)S(1)}, bf16[64,128]{1,0:T(8,128)(2,1)S(1)}, u32[]{:S(2)}, u32[]{:S(2)}) collective-permute-start(bf16[64,128]{1,0:T(8,128)(2,1)S(1)} %get-tuple-element.44), channel_id=1, source_target_pairs={{0,4},{4,8},{8,12},{12,16},{16,20},{20,24},{24,28},{28,32},{32,36}... | collective-permute-start | bytes 49160 | tf_op jit(solution)/shard_map/ppermute | solution.py:322
  84.4 6.9 %collective-permute-start.15 = (bf16[64,128]{1,0:T(8,128)(2,1)S(1)}, bf16[64,128]{1,0:T(8,128)(2,1)S(1)}, u32[]{:S(2)}, u32[]{:S(2)}) collective-permute-start(bf16[64,128]{1,0:T(8,128)(2,1)S(1)} %get-tuple-element.45), channel_id=1, source_target_pairs={{0,60},{4,0},{8,4},{12,8},{16,12},{20,16},{24,20},{28,24},{32,28},... | collective-permute-start | bytes 49160 | tf_op jit(solution)/shard_map/ppermute | solution.py:322
  91.5 3.0 %collective-permute-start.16 = (bf16[64,128]{1,0:T(8,128)(2,1)S(1)}, bf16[64,128]{1,0:T(8,128)(2,1)S(1)}, u32[]{:S(2)}, u32[]{:S(2)}) collective-permute-start(bf16[64,128]{1,0:T(8,128)(2,1)S(1)} %get-tuple-element.46), channel_id=1, source_target_pairs={{0,1},{1,2},{2,3},{3,0},{4,5},{5,6},{6,7},{7,4},{8,9},{9,10},{10,1... | collective-permute-start | bytes 49160 | tf_op jit(solution)/shard_map/ppermute | solution.py:322
  93.6 7.1 %collective-permute-start.17 = (bf16[64,128]{1,0:T(8,128)(2,1)S(1)}, bf16[64,128]{1,0:T(8,128)(2,1)S(1)}, u32[]{:S(2)}, u32[]{:S(2)}) collective-permute-start(bf16[64,128]{1,0:T(8,128)(2,1)S(1)} %get-tuple-element.47), channel_id=1, source_target_pairs={{0,3},{1,0},{2,1},{3,2},{4,7},{5,4},{6,5},{7,6},{8,11},{9,8},{10,9... | collective-permute-start | bytes 49160 | tf_op jit(solution)/shard_map/ppermute | solution.py:322
  101.0 8.7 %collective-permute-start.18 = (bf16[32,128]{1,0:T(8,128)(2,1)S(1)}, bf16[32,128]{1,0:T(8,128)(2,1)S(1)}, u32[]{:S(2)}, u32[]{:S(2)}) collective-permute-start(bf16[32,128]{1,0:T(8,128)(2,1)S(1)} %get-tuple-element.48), channel_id=1, source_target_pairs={{0,8},{4,12},{8,16},{12,20},{16,24},{20,28},{24,32},{28,36},{32,40... | collective-permute-start | bytes 24584 | tf_op jit(solution)/shard_map/ppermute | solution.py:322
  101.1 8.6 %collective-permute-start.19 = (bf16[32,128]{1,0:T(8,128)(2,1)S(1)}, bf16[32,128]{1,0:T(8,128)(2,1)S(1)}, u32[]{:S(2)}, u32[]{:S(2)}) collective-permute-start(bf16[32,128]{1,0:T(8,128)(2,1)S(1)} %get-tuple-element.49), channel_id=1, source_target_pairs={{0,4},{4,8},{8,12},{12,16},{16,20},{20,24},{24,28},{28,32},{32,36}... | collective-permute-start | bytes 24584 | tf_op jit(solution)/shard_map/ppermute | solution.py:322
  101.1 8.5 %collective-permute-start.20 = (bf16[32,128]{1,0:T(8,128)(2,1)S(1)}, bf16[32,128]{1,0:T(8,128)(2,1)S(1)}, u32[]{:S(2)}, u32[]{:S(2)}) collective-permute-start(bf16[32,128]{1,0:T(8,128)(2,1)S(1)} %get-tuple-element.51), channel_id=1, source_target_pairs={{0,60},{4,0},{8,4},{12,8},{16,12},{20,16},{24,20},{28,24},{32,28},... | collective-permute-start | bytes 24584 | tf_op jit(solution)/shard_map/ppermute | solution.py:322
  107.0 2.2 %copy-start.16 = (s32[1,1,1,512]{3,2,1,0:T(1,128)S(1)}, s32[1,1,1,512]{3,2,1,0:T(1,128)}, u32[]{:S(2)}) copy-start(s32[1,1,1,512]{3,2,1,0:T(1,128)} %param.26) | copy-start | bytes 6148
  107.0 4.0 %collective-permute-start.21 = (bf16[32,128]{1,0:T(8,128)(2,1)S(1)}, bf16[32,128]{1,0:T(8,128)(2,1)S(1)}, u32[]{:S(2)}, u32[]{:S(2)}) collective-permute-start(bf16[32,128]{1,0:T(8,128)(2,1)S(1)} %get-tuple-element.52), channel_id=1, source_target_pairs={{0,56},{4,60},{8,0},{12,4},{16,8},{20,12},{24,16},{28,20},{32,24},... | collective-permute-start | bytes 24584 | tf_op jit(solution)/shard_map/ppermute | solution.py:322
  109.1 1.8 %copy-start.5 = (s32[1,1,1,32,512]{4,3,2,1,0:T(8,128)S(1)}, s32[1,1,1,32,512]{4,3,2,1,0:T(8,128)}, u32[]{:S(2)}) copy-start(s32[1,1,1,32,512]{4,3,2,1,0:T(8,128)} %param.25) | copy-start | bytes 196612

commit v3 on v2

v3 whole, which is shorter than its diff:
```python
import functools
import math

import jax
import jax.numpy as jnp
from jax import lax
from jax.experimental import pallas as pl
from jax.experimental.pallas import tpu as pltpu
from jax.sharding import PartitionSpec as P

BASIS = 8
F32 = jnp.float32
BF16 = jnp.bfloat16
VMEM = pl.BlockSpec(memory_space=pltpu.VMEM)
ANY = pl.BlockSpec(memory_space=pl.ANY)


def call(kernel, out_shape, operands, scratch=(), limit=8, after=()):
    count = len(operands)

    def body(*refs):
        kernel(*refs[:count], *refs[count + len(after) :])

    return pl.pallas_call(
        body,
        out_shape=out_shape,
        in_specs=[VMEM] * count + [ANY] * len(after),
        out_specs=jax.tree.map(lambda _: VMEM, out_shape),
        scratch_shapes=list(scratch),
        compiler_params=pltpu.CompilerParams(vmem_limit_bytes=limit and limit << 20),
        cost_estimate=pl.CostEstimate(flops=0, bytes_accessed=1 << 20, transcendentals=0),
    )(*operands, *after)


def dot(a, b):
    return jnp.dot(a, b, preferred_element_type=F32)


def dot_first(a, b):
    return lax.dot_general(a, b, (((0,), (0,)), ((), ())), preferred_element_type=F32)


def harmonics(vx, vy, vz, weight):
    radius = jnp.sqrt(vx * vx + vy * vy + vz * vz)
    inverse = 1.0 / radius
    x, y, z = vx * inverse, vy * inverse, vz * inverse
    xx, yy, zz = x * x, y * y, z * z
    r3, r15, r5, r105, r7 = (math.sqrt(v) for v in (3.0, 15.0, 5.0, 105.0, 7.0))
    outer, inner = math.sqrt(35.0 / 8.0), math.sqrt(21.0 / 8.0)
    rows = [
        jnp.ones_like(x),
        r3 * x,
        r3 * y,
        r3 * z,
        r15 * x * y,
        r15 * y * z,
        0.5 * r5 * (3.0 * zz - 1.0),
        r15 * x * z,
        0.5 * r15 * (xx - yy),
        outer * y * (3.0 * xx - yy),
        r105 * x * y * z,
        inner * y * (5.0 * zz - 1.0),
        0.5 * r7 * z * (5.0 * zz - 3.0),
        inner * x * (5.0 * zz - 1.0),
        0.5 * r105 * z * (xx - yy),
        outer * x * (xx - 3.0 * yy),
    ]
    return [row * weight for row in rows], radius, inverse


def radial_basis(radius, inverse, cutoff):
    u = radius * (1.0 / cutoff)
    u2 = u * u
    envelope = 1.0 + u2 * u2 * u2 * (-28.0 + u * (48.0 - 21.0 * u))
    scale = math.sqrt(2.0 / cutoff) * inverse * envelope
    angle = radius * (math.pi / cutoff)
    before, now = jnp.zeros_like(angle), jnp.sin(angle)
    twice = 2.0 * jnp.cos(angle)
    rows = []
    for _ in range(BASIS):
        rows.append(now * scale)
        before, now = now, twice * now - before
    return rows


def sections(arrays):
    return jnp.where(lax.broadcasted_iota(jnp.int32, (8, 128), 1) < 64, arrays[1], arrays[0])


def swapped(index):
    return jnp.where(index >= 256, index ^ 64, index)


def species_rows(species_ref, pieces):
    parts = [jnp.broadcast_to(species_ref[...].astype(F32), (8, 256))]
    for first in range(0, len(pieces), 2):
        parts.append(sections((pieces[first][...], pieces[first + 1][...])))
    return jnp.concatenate(parts, axis=1)


def onehot_of(chosen, rows):
    row_ids = lax.broadcasted_iota(jnp.int32, (rows, chosen.shape[1]), 0)
    return jnp.where(row_ids == chosen, 1.0, 0.0).astype(BF16)


def section_list(lists_ref, section):
    return lists_ref[:, section * 128 : (section + 1) * 128]


def pick_species(section):
    def kernel(species_ref, lists_ref, *rest):
        pieces, out_ref = rest[: 2 * section], rest[2 * section]
        table = species_rows(species_ref, pieces).astype(BF16)
        chosen = swapped(section_list(lists_ref, section))
        out_ref[...] = dot(table, onehot_of(chosen, table.shape[1]))

    return kernel


def first_kernel(species_ref, lists_ref, out_ref, species_copy, lists_copy):
    pick_species(0)(species_ref, lists_ref, out_ref)
    species_copy[...] = species_ref[...]
    lists_copy[...] = lists_ref[...]


def send_rows(lists_ref, section, table, low_ref, high_ref):
    chosen = dot_first(onehot_of(section_list(lists_ref, section), table.shape[0]), table)
    high_ref[...] = chosen[:64].astype(BF16)
    low_ref[...] = chosen[64:].astype(BF16)


def pick_rows(section):
    def kernel(lists_ref, *rest):
        table = jnp.concatenate([piece[...] for piece in rest[:-2]], axis=0)
        send_rows(lists_ref, section, table, *rest[-2:])

    return kernel


def by_group(x):
    rows, lanes = x.shape
    row = lax.broadcasted_iota(jnp.int32, x.shape, 0)
    block = lax.broadcasted_iota(jnp.int32, x.shape, 1) >> 3
    step = 1
    while step < rows:
        up = pltpu.roll(pltpu.roll(x, 8 * step, axis=1), rows - step, axis=0)
        down = pltpu.roll(pltpu.roll(x, lanes - 8 * step, axis=1), step, axis=0)
        moved = jnp.where((block & step) != 0, up, down)
        x = jnp.where(((row ^ block) & step) != 0, moved, x)
        step *= 2
    return x


def store_rows(ref, rows):
    for n, row in enumerate(rows):
        size = row.shape[0]
        for tile in range(ref.shape[0]):
            ref[tile, n * size : (n + 1) * size, :] = row[:, tile * 128 : (tile + 1) * 128]


def spread(ref, row):
    parts = [ref[tile, pl.ds(row, 8, stride=0), :] for tile in range(ref.shape[0])]
    return jnp.concatenate(parts, axis=1)


def basis_rows(ref, slot, slots):
    parts = [ref[tile, pl.ds(slot, BASIS, stride=slots), :] for tile in range(ref.shape[0])]
    return jnp.concatenate(parts, axis=1)


def transposed(ref):
    return ref[...].astype(F32).T.astype(BF16)


def hidden_rows(phi_ref, in_ref, hid_ref):
    groups = hid_ref.shape[0]
    into = transposed(in_ref)
    for g in range(groups):
        value = dot(into, basis_rows(phi_ref, g, groups).astype(BF16))
        hid_ref[g] = (value / (1.0 + jnp.exp(-value))).astype(BF16)


def radial_rows(first, hid_ref, out_ref, radial_ref):
    def step(g, carry):
        radial_ref[g] = dot_first(hid_ref[first + g], out_ref[...])
        return carry

    lax.fori_loop(0, radial_ref.shape[0], step, 0, unroll=2)


def geometry_kernel(
    vec_ref, count_ref, index_ref, y_ref, phi_ref, where_ref
):
    slots, atoms = index_ref.shape
    live = lax.broadcasted_iota(jnp.int32, (slots, atoms), 0) < count_ref[...]
    weight = by_group(jnp.where(live, 0.25, 0.0))
    vx, vy, vz = (by_group(vec_ref[n]) for n in range(3))
    rows, radius, inverse = harmonics(vx, vy, vz, weight)
    store_rows(y_ref, rows)
    store_rows(phi_ref, radial_basis(radius, inverse, 5.0))
    where_ref[...] = by_group(index_ref[...].astype(F32)).astype(jnp.int32)


def first_radial_kernel(
    phi_ref, in_ref, out_ref, emb_ref, msg_ref, hid_ref, rows_ref, radial_ref
):
    rows_ref[...] = dot(emb_ref[...], msg_ref[...]).astype(BF16)
    hidden_rows(phi_ref, in_ref, hid_ref)
    radial_rows(0, hid_ref, out_ref, radial_ref)


def radial_kernel(first):
    def kernel(hid_ref, out_ref, radial_ref):
        radial_rows(first, hid_ref, out_ref, radial_ref)

    return kernel


def second_radial_kernel(phi_ref, in_ref, out_ref, hid_ref, radial_ref):
    hidden_rows(phi_ref, in_ref, hid_ref)
    radial_rows(0, hid_ref, out_ref, radial_ref)


def last_radial_kernel(first):
    def kernel(hid_ref, out_ref, dec_ref, radial_ref, blocks_ref):
        radial_rows(first, hid_ref, out_ref, radial_ref)
        column = lax.broadcasted_iota(jnp.int32, (8, 128), 1)
        repeat = (column & 7) == lax.broadcasted_iota(jnp.int32, (8, 128), 0)
        repeat = jnp.where(repeat, 1.0, 0.0).astype(BF16)
        group = lax.broadcasted_iota(jnp.int32, (128, 128), 1) >> 3
        for degree in range(4):
            wide = dot_first(dec_ref[degree], repeat)
            for m in range(degree * degree, (degree + 1) * (degree + 1)):
                block = jnp.where(group == m, wide, 0.0).astype(BF16)
                blocks_ref[m * 128 : (m + 1) * 128, :] = block

    return kernel


def group_sums(g, groups, radial, y_ref, picked):
    own = (lax.broadcasted_iota(jnp.int32, (8, 256), 1) & 7) == lax.broadcasted_iota(
        jnp.int32, (8, 256), 0
    )
    twice = jnp.concatenate([picked, picked], axis=1)
    sums = []
    for degrees, first, last in (((0, 1), 0, 4), ((2, 3), 4, 16)):
        lane = degrees[0] * 128
        weighted = (radial[:, lane : lane + 256] * twice).astype(BF16)
        angular = [jnp.where(own, spread(y_ref, m * groups + g), 0.0) for m in range(first, last)]
        total = dot(jnp.concatenate(angular, axis=0).astype(BF16), weighted)
        for m in range(first, last):
            side = 0 if m < (degrees[0] + 1) ** 2 else 128
            sums.append(total[8 * (m - first) : 8 * (m - first + 1), side : side + 128])
    return sums


def each_pair(radials, pair):
    first = 0
    for radial in radials:

        def step(j, carry, first=first, radial=radial):
            groups = [(first + 2 * j + n, radial.at[2 * j + n]) for n in range(2)]
            pair(pl.multiple_of((first + 2 * j) * 8, 16), groups)
            return carry

        lax.fori_loop(0, radial.shape[0] // 2, step, 0, unroll=4)
        first += radial.shape[0]


def layer_one_kernel(
    species_ref, xl, xh, yl, yh, zl, zh, where_ref, y_ref, radial_a, radial_b, rows_ref, emb_ref,
    self_ref, mix_ref, msg2_ref, lists_ref, next_ref, low_ref, high_ref, onehot, feats,
):
    groups, edges = where_ref.shape
    atoms = species_ref.shape[1]
    table = species_rows(species_ref, (xl, xh, yl, yh, zl, zh))
    blocks = []
    for lane in range(0, edges, 128):
        column = []
        for row in range(0, groups, 8):
            where = swapped(where_ref[row : row + 8, lane : lane + 128])
            found = jnp.zeros((8, 128), F32)
            for b in range(5):
                part = jnp.take_along_axis(table[:, b * 128 : (b + 1) * 128], where & 127, axis=1)
                found = jnp.where((where >> 7) == b, part, found)
            column.append(found)
        blocks.append(jnp.concatenate(column, axis=0))
    kinds = jnp.concatenate(blocks, axis=1).T.astype(BF16)
    lane_group = lax.broadcasted_iota(jnp.int32, (groups, 8 * groups), 1) >> 3
    widen = lane_group == lax.broadcasted_iota(jnp.int32, (groups, 8 * groups), 0)
    kinds = dot(kinds, jnp.where(widen, 1.0, 0.0).astype(BF16))
    kind_of_lane = lax.broadcasted_iota(jnp.int32, kinds.shape, 1) & 7
    onehot[...] = jnp.where(kinds == kind_of_lane.astype(F32), 1.0, 0.0).astype(BF16)
    tall = jnp.concatenate([rows_ref[...].astype(F32)] * groups, axis=0)
    row_group = lax.broadcasted_iota(jnp.int32, tall.shape, 0) >> 3

    def pair(row, members):
        parts = []
        own_rows = [jnp.where(row_group == g, tall, 0.0) for g, _ in members]
        found = dot(onehot[...], jnp.concatenate(own_rows, axis=1).astype(BF16))
        for n, (g, radial) in enumerate(members):
            sums = group_sums(g, groups, radial, y_ref, found[:, 128 * n : 128 * (n + 1)])
            part = [sums[0]]
            for degree in (1, 2, 3):
                part.append(sum(v * v for v in sums[degree * degree : (degree + 1) ** 2]))
            parts.append(jnp.concatenate(part, axis=1))
        feats[pl.ds(row, 16), :] = jnp.concatenate(parts, axis=0).astype(BF16)

    each_pair((radial_a, radial_b), pair)
    kind_ids = lax.broadcasted_iota(jnp.int32, (8, atoms), 0).astype(F32)
    own = jnp.where(table[:, :atoms] == kind_ids, 1.0, 0.0).astype(BF16)
    start = dot_first(own, emb_ref[...]).astype(BF16)
    mixed = dot(start, self_ref[...]) + dot(feats[...], mix_ref[...])
    hidden = (mixed / (1.0 + jnp.exp(-mixed))).astype(BF16)
    message = dot(hidden, msg2_ref[...]).astype(BF16)
    next_ref[...] = message
    send_rows(lists_ref, 0, message, low_ref, high_ref)


def layer_two_kernel(
    own_ref, xl, xh, yl, yh, zl, zh, where_ref, y_ref, radial_a, radial_b, radial_c, blocks_ref,
    lists_ref, coeff_ref, low_ref, high_ref, feats, wide, index,
):
    groups, edges = where_ref.shape
    pieces = [piece[...].astype(F32) for piece in (own_ref, xl, xh, yl, yh, zl, zh)]
    table = jnp.concatenate(pieces + [jnp.zeros((128, 128), F32)], axis=0)
    table = jnp.concatenate([table[256 * n : 256 * (n + 1)] for n in range(3)], axis=1)
    wide[...] = table[:, :384].astype(BF16)
    halves = (where_ref[...] & 255, where_ref[...] >> 8)
    index[...] = jnp.concatenate([half.astype(F32).T for half in halves], axis=1).astype(BF16)
    source = lax.broadcasted_iota(jnp.int32, (2 * groups, 512), 0)
    target = lax.broadcasted_iota(jnp.int32, (2 * groups, 512), 1) >> 7
    low_ids = lax.broadcasted_iota(jnp.int32, (edges, 128), 1).astype(F32)

    def pair(row, members):
        parts, onehots = [], []
        first = members[0][0]
        picks = source == first + (target & 1) + jnp.where(target < 2, 0, groups)
        spread_index = dot(index[...], jnp.where(picks, 1.0, 0.0).astype(BF16))
        for n in range(2):
            low = spread_index[:, 128 * n : 128 * (n + 1)]
            sides = [jnp.where(low == low_ids + 128.0 * side, 1.0, 0.0) for side in range(2)]
            onehots.append(jnp.concatenate(sides, axis=1))
        found = dot(jnp.concatenate(onehots, axis=0).astype(BF16), wide[...])
        for n, (g, radial) in enumerate(members):
            high = spread_index[:, 256 + 128 * n : 384 + 128 * n]
            mine = found[edges * n : edges * (n + 1)]
            picked = jnp.where(high < 0.5, mine[:, :128], mine[:, 128:256])
            picked = jnp.where(high < 1.5, picked, mine[:, 256:])
            sums = group_sums(g, groups, radial, y_ref, picked)
            parts.append(jnp.concatenate(sums, axis=1))
        feats[pl.ds(row, 16), :] = jnp.concatenate(parts, axis=0).astype(BF16)

    each_pair((radial_a, radial_b, radial_c), pair)
    coeffs = dot(feats[...], blocks_ref[...]).astype(BF16)
    coeff_ref[...] = coeffs
    send_rows(lists_ref, 0, coeffs, low_ref, high_ref)


SWAPS = ((2, 1), (1, 1), (2, 0), (1, 0))


def partner_slot(distance, first):
    ahead = (lax.axis_index("gy") // distance) % 2 == first
    return jnp.where(ahead, 2 + distance, 2 - distance)


def brick_kernel(list_ref, *rest):
    pieces, outs, chosen = rest[:7], rest[7:12], rest[12]
    table = jnp.concatenate([piece[...] for piece in pieces], axis=0)
    chosen[...] = dot_first(onehot_of(list_ref[...], table.shape[0]), table)
    for swap, out in zip(SWAPS, outs):
        first = pl.multiple_of(partner_slot(*swap) * 32, 32)
        out[...] = chosen[pl.ds(first, 32), :].astype(BF16)
    outs[4][...] = chosen[64:96].astype(BF16)


def probe_kernel(
    column, list_ref, count_ref, vec_ref, index_ref, y_ref, phi_ref, where_ref, nearby_ref
):
    slots, probes = index_ref.shape
    live = lax.broadcasted_iota(jnp.int32, (slots, probes), 0) < count_ref[...]
    weight = jnp.where(live, 0.125, 0.0)
    rows, radius, inverse = harmonics(vec_ref[0], vec_ref[1], vec_ref[2], weight)
    store_rows(y_ref, rows)
    store_rows(phi_ref, radial_basis(radius, inverse, 4.0))
    here = lax.axis_index("gy")
    index = index_ref[...]
    source = (index >> 5) - here + 2
    source = jnp.where(source < 0, source + column, source)
    source = jnp.where(source >= column, source - column, source)
    where_ref[...] = source * 32 + (index & 31)
    targets = list_ref.shape[1]
    start = (2 - here) * (targets // column)
    start = jnp.where(start < 0, start + targets, start)
    turned = pltpu.roll(jnp.broadcast_to(list_ref[...], (8, targets)), start, axis=1)
    nearby_ref[...] = turned[:1, :256]


def density_kernel(p0, p1, p2, p3, p4, where_ref, y, phi, out_ref, table):
    slots, probes = where_ref.shape
    table[160:, :] = jnp.zeros((96, 128), F32)
    table[64:96, :] = p4[...].astype(F32)
    for swap, piece in zip(SWAPS, (p0, p1, p2, p3)):
        first = pl.multiple_of(partner_slot(*swap) * 32, 32)
        table[pl.ds(first, 32), :] = piece[...].astype(F32)
    rows_t = table[...].T[:, :160].astype(BF16)

    def slot(k, total):
        picked = dot(rows_t, onehot_of(where_ref[pl.ds(k, 1), :], 160))
        part = jnp.zeros((8, probes), F32)
        for m in range(16):
            part = part + spread(y, m * slots + k) * picked[m * 8 : (m + 1) * 8]
        return total + part * basis_rows(phi, k, slots)

    total = lax.fori_loop(0, slots, slot, jnp.zeros((8, probes), F32), unroll=4)
    out_ref[...] = jnp.sum(total, axis=0, keepdims=True)


def shifted(block, axis, step):
    size = lax.axis_size(axis)
    return lax.ppermute(block, axis, [(i, (i + step) % size) for i in range(size)])


def swapped_with(block, distance, first):
    size = lax.axis_size("gy")
    pairs = []
    for low in range(size):
        if (low // distance) % 2 == first:
            high = (low + distance) % size
            pairs += [(low, high), (high, low)]
    return lax.ppermute(block, "gy", sorted(pairs))


def extend(rows, low, high, lists, fillers):
    half = jax.ShapeDtypeStruct((64, 128), BF16)
    pieces, made, begin = [], [], rows
    for section, axis in enumerate(("gx", "gy", "gz")):
        if section:
            done = made[-1][-1:] if made[-1] else ()
            low, high = call(
                pick_rows(section), (half, half), (lists, rows, *pieces), after=done
            )
            begin = low
        pieces += [shifted(low, axis, 1), shifted(high, axis, -1)]
        made.append(fillers[section](made, begin) if fillers[section] else ())
    return pieces, made


def shards(
    species, neighbour_index, neighbour_count, edge_vectors, ghost_send, brick_send, probe_index,
    probe_count, probe_vectors, embedding, message_one, radial_in_one, radial_out_one, self_mix,
    basis_mix, message_two, radial_in_two, radial_out_two, decoder,
):
    slots, atoms = neighbour_index.shape[3:]
    probes = probe_index.shape[-1]
    kinds = species.reshape(1, atoms)
    lists = ghost_send.reshape(1, 384)
    shape = jax.ShapeDtypeStruct
    half = shape((64, 128), BF16)
    column = lax.axis_size("gy")

    def both(block, axis):
        return [shifted(block, axis, 1), shifted(block, axis, -1)]

    row = shape((8, 128), F32)
    hidden = shape((slots, 64, atoms), BF16)

    def radial(count):
        return shape((count, atoms, 512), F32)

    chosen, kinds, lists = call(
        first_kernel,
        (row, shape(kinds.shape, jnp.int32), shape(lists.shape, jnp.int32)),
        (kinds, lists),
    )
    ghosts = both(chosen, "gx")
    angular, phi, where = call(
        geometry_kernel,
        (
            shape((2, 16 * slots, 128), F32),
            shape((2, BASIS * slots, 128), F32),
            shape((slots, atoms), jnp.int32),
        ),
        (
            edge_vectors.reshape(3, slots, atoms),
            neighbour_count.reshape(1, atoms),
            neighbour_index.reshape(slots, atoms),
        ),
        after=(chosen,),
    )
    chosen = call(pick_species(1), row, (kinds, lists, *ghosts), after=(where,))
    ghosts += both(chosen, "gy")
    hidden_one, rows, radial_a = call(
        first_radial_kernel,
        (hidden, shape((8, 128), BF16), radial(16)),
        (phi, radial_in_one, radial_out_one, embedding, message_one),
        limit=20,
        after=(chosen,),
    )
    chosen = call(pick_species(2), row, (kinds, lists, *ghosts), after=(radial_a,))
    ghosts += both(chosen, "gz")
    radial_b = call(radial_kernel(16), radial(16), (hidden_one, radial_out_one), limit=20, after=(chosen,))
    second = call(
        layer_one_kernel,
        (shape((atoms, 128), BF16), half, half),
        (kinds, *ghosts, where, angular, radial_a, radial_b, rows, embedding, self_mix,
         basis_mix, message_two, lists),
        [pltpu.VMEM((atoms, 256), BF16), pltpu.VMEM((atoms, 512), BF16)],
        limit=16,
    )
    pieces, made = extend(
        *second,
        lists,
        (
            lambda made, begin: call(
                second_radial_kernel,
                (hidden, radial(8)),
                (phi, radial_in_two, radial_out_two),
                limit=20,
                after=(begin,),
            ),
            lambda made, begin: (
                call(
                    radial_kernel(8),
                    radial(16),
                    (made[0][0], radial_out_two),
                    limit=20,
                    after=(begin,),
                ),
            ),
            lambda made, begin: call(
                last_radial_kernel(24),
                (radial(8), shape((2048, 128), BF16)),
                (made[0][0], radial_out_two, decoder.transpose(0, 2, 1)),
                limit=20,
                after=(begin,),
            ),
        ),
    )
    coeffs = call(
        layer_two_kernel,
        (shape((atoms, 128), BF16), half, half),
        (second[0], *pieces, where, angular, made[0][1], made[1][0], *made[2], lists),
        [
            pltpu.VMEM((atoms, 2048), BF16),
            pltpu.VMEM((256, 384), BF16),
            pltpu.VMEM((atoms, 2 * slots), BF16),
        ],
        limit=16,
    )
    pieces, made = extend(
        *coeffs,
        lists,
        (
            lambda made, begin: call(
                functools.partial(probe_kernel, column),
                (
                    shape((probes // 128, 16 * slots, 128), F32),
                    shape((probes // 128, BASIS * slots, 128), F32),
                    shape((slots, probes), jnp.int32),
                    shape((1, 256), jnp.int32),
                ),
                (
                    brick_send.reshape(1, -1),
                    probe_count.reshape(1, probes),
                    probe_vectors.reshape(3, slots, probes),
                    probe_index.reshape(slots, probes),
                ),
                after=(begin,),
            ),
            None,
            None,
        ),
    )
    probe_y, probe_phi, probe_where, nearby = made[0]
    sent = call(
        brick_kernel,
        [shape((32, 128), BF16)] * 5,
        (nearby, coeffs[0], *pieces),
        [pltpu.VMEM((256, 128), F32)],
    )
    pieces = [swapped_with(sent[n], *SWAPS[n]) for n in (3, 2, 1, 0)][::-1] + [sent[4]]
    density = call(
        density_kernel,
        shape((1, probes), F32),
        (*pieces, probe_where, probe_y, probe_phi),
        [pltpu.VMEM((256, 128), F32)],
    )
    return density.reshape(1, 1, 1, probes)


def solution(mesh):
    domain = ("gx", "gy", "gz")
    placed = tuple(P(*domain) for _ in range(9)) + tuple(P() for _ in range(10))
    return jax.shard_map(
        shards, mesh=mesh, in_specs=placed, out_specs=P(*domain), check_vma=False
    )
```

time: 116 us -> 108 us (0.931)
  starting transfers between devices: 53.3 us -> 47 us
  waiting for transfers between devices: 22.9 us -> 21.2 us
  local copies, waits for them, and re-layouts: 8.12 us -> 6.69 us
    ppermute x22 -> x18, starting transfers between devices: 53.3 us -> 38.9 us  [shifted(): lax.ppermute(block, axis, [(i, (i + step) % size) for i in range(size)])]
    ppermute x0 -> x4, starting transfers between devices: none -> 8.1 us  [swapped_with(): return lax.ppermute(block, 'gy', sorted(pairs))]
    ppermute x22 -> x18, waiting for transfers between devices: 22.9 us -> 18.7 us  [shifted(): lax.ppermute(block, axis, [(i, (i + step) % size) for i in range(size)])]
    ppermute x0 -> x4, waiting for transfers between devices: none -> 2.5 us  [swapped_with(): return lax.ppermute(block, 'gy', sorted(pairs))]
    unnamed x40 -> x38, local copies, waits for them, and re-layouts: 8.12 us -> 6.69 us
    pallas_call x13 -> x18, Pallas kernels: 31.2 us -> 32.2 us  [call(): pl.pallas_call(body, out_shape=out_shape, in_specs=[VMEM] * count + [ANY]...]
  transfers between devices with their start and end apart: 22 -> 22, of which waited for: 13 -> 9; matrix products, arithmetic and copies ran while one was open for 0% -> 0% of each run, Pallas kernels for 2% -> 12%
where the time goes in v3:
time: 108 us; the launch traced here: 107 us
  starting transfers between devices  47 us (44%)
  Pallas kernels  32.2 us (30%)
  waiting for transfers between devices  21.2 us (20%)
  local copies, waits for them, and re-layouts  6.69 us (6%)
    ppermute x18, starting transfers between devices, shifted(): lax.ppermute(block, axis, [(i, (i + step) % size) for i in range(size)])  38.9 us
    pallas_call x18, Pallas kernels, call(): pl.pallas_call(body, out_shape=out_shape, in_specs=[VMEM] * count + [ANY]...  32.2 us
    ppermute x18, waiting for transfers between devices, shifted(): lax.ppermute(block, axis, [(i, (i + step) % size) for i in range(size)])  18.7 us
    ppermute x4, starting transfers between devices, swapped_with(): return lax.ppermute(block, 'gy', sorted(pairs))  8.1 us
    unnamed x38, local copies, waits for them, and re-layouts  6.69 us
    ppermute x4, waiting for transfers between devices, swapped_with(): return lax.ppermute(block, 'gy', sorted(pairs))  2.5 us
  transfers between devices with their start and end apart: 22, of which 9 were waited for; matrix products, arithmetic and copies ran while one was open for 0% of the time, Pallas kernels for 12%

profile of v3, /device:TPU:1, one launch (start us, length us, event | category | flops | bytes accessed | tf_op | source)
XLA Modules:
  0.0 107.3 jit_solution(16404402451278490804)
XLA Ops:
  0.0 0.7 copy-done.16
  0.7 0.7 copy-done.18
  1.4 0.1 shard_map.181
  1.5 2.0 %collective-permute-start = (f32[8,128]{1,0:T(8,128)S(1)}, f32[8,128]{1,0:T(8,128)S(1)}, u32[]{:S(2)}, u32[]{:S(2)}) collective-permute-start(f32[8,128]{1,0:T(8,128)S(1)} %get-tuple-element.42.refs_3_), channel_id=1, source_target_pairs={{0,64},{64,128},{128,192},{192,0},{1,65},{65,129},{129,193},{193,1... | collective-permute-start | bytes 12296 | tf_op jit(solution)/shard_map/ppermute | solution.py:422
  3.5 1.3 %collective-permute-start.1 = (f32[8,128]{1,0:T(8,128)S(1)}, f32[8,128]{1,0:T(8,128)S(1)}, u32[]{:S(2)}, u32[]{:S(2)}) collective-permute-start(f32[8,128]{1,0:T(8,128)S(1)} %get-tuple-element.42.refs_3_), channel_id=1, source_target_pairs={{0,192},{64,0},{128,64},{192,128},{1,193},{65,1},{129,65},{193,129... | collective-permute-start | bytes 12296 | tf_op jit(solution)/shard_map/ppermute | solution.py:422
  4.9 0.9 copy-done.4
  5.7 0.8 copy-done.9
  6.5 0.7 copy-done.17
  7.2 0.7 shard_map.182
  7.9 0.1 shard_map.183.refs_5_
  8.1 1.4 %collective-permute-start.2 = (f32[8,128]{1,0:T(8,128)S(1)}, f32[8,128]{1,0:T(8,128)S(1)}, u32[]{:S(2)}, u32[]{:S(2)}) collective-permute-start(f32[8,128]{1,0:T(8,128)S(1)} %shard_map.183.refs_5_), channel_id=1, source_target_pairs={{0,4},{4,8},{8,12},{12,16},{16,20},{20,24},{24,28},{28,32},{32,36}... | collective-permute-start | bytes 12296 | tf_op jit(solution)/shard_map/ppermute | solution.py:422
  9.5 5.6 %collective-permute-start.3 = (f32[8,128]{1,0:T(8,128)S(1)}, f32[8,128]{1,0:T(8,128)S(1)}, u32[]{:S(2)}, u32[]{:S(2)}) collective-permute-start(f32[8,128]{1,0:T(8,128)S(1)} %shard_map.183.refs_5_), channel_id=1, source_target_pairs={{0,60},{4,0},{8,4},{12,8},{16,12},{20,16},{24,20},{28,24},{32,28},... | collective-permute-start | bytes 12296 | tf_op jit(solution)/shard_map/ppermute | solution.py:422
  15.1 0.8 copy-done.1
  15.9 0.8 copy-done.8
  16.7 0.7 copy-done.11
  17.3 0.7 copy-done.12
  18.0 3.4 %shard_map.184 = (bf16[32,64,256]{2,1,0:T(8,128)(2,1)S(1)}, bf16[8,128]{1,0:T(8,128)(2,1)S(1)}, f32[16,256,512]{2,1,0:T(8,128)S(1)}) custom-call(f32[2,256,128]{2,1,0:T(8,128)S(1)} %get-tuple-element.45.refs_0_, bf16[8,64]{1,0:T(8,128)(2,1)S(1)} %copy-done.12, bf16[64,512]{1,0:T(8,128)(2,1)S(1)} %copy-done.1, bf16[8,128]{1,0:T(8,128)(2,1)S(1)} %copy-done.11, ...), custom_call_target="tpu_custom_call" | custom-call | bytes 1048576 | tf_op jit(solution)/shard_map/pallas_call | solution.py:24
  21.4 0.0 collective-permute-done.2.refs_4_.refs_3_
  21.4 0.0 copy-start.3
  21.4 0.0 copy-start.6
  21.4 0.0 copy-start.7
  21.5 0.1 shard_map.185.refs_2_
  21.6 7.1 %collective-permute-start.4 = (f32[8,128]{1,0:T(8,128)S(1)}, f32[8,128]{1,0:T(8,128)S(1)}, u32[]{:S(2)}, u32[]{:S(2)}) collective-permute-start(f32[8,128]{1,0:T(8,128)S(1)} %shard_map.185.refs_2_), channel_id=1, source_target_pairs={{0,1},{1,2},{2,3},{3,0},{4,5},{5,6},{6,7},{7,4},{8,9},{9,10},{10,1... | collective-permute-start | bytes 12296 | tf_op jit(solution)/shard_map/ppermute | solution.py:422
  28.7 2.6 %shard_map.186.refs_10_ = f32[16,256,512]{2,1,0:T(8,128)S(1)} custom-call(bf16[32,64,256]{2,1,0:T(8,128)(2,1)S(1)} %get-tuple-element.48.refs_0_, bf16[64,512]{1,0:T(8,128)(2,1)S(1)} %copy-done.1, f32[8,128]{1,0:T(8,128)S(1)} %shard_map.185.refs_2_), custom_call_target="tpu_custom_call" | custom-call | bytes 1048576 | tf_op jit(solution)/shard_map/pallas_call | solution.py:24
  31.3 0.0 collective-permute-done.4.refs_5_
  31.3 4.4 %collective-permute-done.5.refs_6_ = f32[8,128]{1,0:T(8,128)S(1)} collective-permute-done((f32[8,128]{1,0:T(8,128)S(1)}, f32[8,128]{1,0:T(8,128)S(1)}, u32[]{:S(2)}, u32[]{:S(2)}) %collective-permute-start.5) | collective-permute-done | bytes 4128 | tf_op jit(solution)/shard_map/ppermute | solution.py:422
  35.6 0.0 copy-start
  35.7 0.0 copy-start.13
  35.7 5.6 %shard_map.187 = (bf16[256,128]{1,0:T(8,128)(2,1)S(1)}, bf16[64,128]{1,0:T(8,128)(2,1)S(1)}, bf16[64,128]{1,0:T(8,128)(2,1)S(1)}) custom-call(s32[1,256]{1,0:T(1,128)S(1)} %get-tuple-element.41.refs_0_, f32[8,128]{1,0:T(8,128)S(1)} %collective-permute-done.refs_2_.refs_1_, f32[8,128]{1,0:T(8,128)S(1)} %collective-permute-done.1.refs_3_.refs_2_, ...), custom_call_target="tpu_custom_call" | custom-call | bytes 1048576 | tf_op jit(solution)/shard_map/pallas_call | solution.py:24
  41.3 0.1 collective-permute-start.6
  41.4 2.7 %collective-permute-start.7 = (bf16[64,128]{1,0:T(8,128)(2,1)S(1)}, bf16[64,128]{1,0:T(8,128)(2,1)S(1)}, u32[]{:S(2)}, u32[]{:S(2)}) collective-permute-start(bf16[64,128]{1,0:T(8,128)(2,1)S(1)} %get-tuple-element.52), channel_id=1, source_target_pairs={{0,192},{64,0},{128,64},{192,128},{1,193},{65,1},{129,65},{193,129... | collective-permute-start | bytes 49160 | tf_op jit(solution)/shard_map/ppermute | solution.py:422
  44.1 2.1 %shard_map.188 = (bf16[32,64,256]{2,1,0:T(8,128)(2,1)S(1)}, f32[8,256,512]{2,1,0:T(8,128)S(1)}) custom-call(f32[2,256,128]{2,1,0:T(8,128)S(1)} %get-tuple-element.45.refs_0_, bf16[8,64]{1,0:T(8,128)(2,1)S(1)} %copy-done.13, bf16[64,512]{1,0:T(8,128)(2,1)S(1)} %copy-done, bf16[256,128]{1,0:T(8,128)(2,1)S(1)} %get-tuple-element.50.refs_3_.refs_1_.refs_0_), custom_call_target="tpu_custom_call" | custom-call | bytes 1048576 | tf_op jit(solution)/shard_map/pallas_call | solution.py:24
  46.2 0.0 collective-permute-done.6.refs_2_.refs_1_
  46.2 0.2 shard_map.189
  46.4 0.1 collective-permute-start.8
  46.5 5.4 %collective-permute-start.9 = (bf16[64,128]{1,0:T(8,128)(2,1)S(1)}, bf16[64,128]{1,0:T(8,128)(2,1)S(1)}, u32[]{:S(2)}, u32[]{:S(2)}) collective-permute-start(bf16[64,128]{1,0:T(8,128)(2,1)S(1)} %get-tuple-element.55), channel_id=1, source_target_pairs={{0,60},{4,0},{8,4},{12,8},{16,12},{20,16},{24,20},{28,24},{32,28},... | collective-permute-start | bytes 49160 | tf_op jit(solution)/shard_map/ppermute | solution.py:422
  51.9 2.6 %shard_map.190.refs_6_.refs_10_ = f32[16,256,512]{2,1,0:T(8,128)S(1)} custom-call(bf16[32,64,256]{2,1,0:T(8,128)(2,1)S(1)} %get-tuple-element.56.refs_0_, bf16[64,512]{1,0:T(8,128)(2,1)S(1)} %copy-done, bf16[64,128]{1,0:T(8,128)(2,1)S(1)} %get-tuple-element.54.refs_2_), custom_call_target="tpu_custom_call" | custom-call | bytes 1048576 | tf_op jit(solution)/shard_map/pallas_call | solution.py:24
  54.4 0.0 collective-permute-done.8.refs_4_.refs_3_
  54.5 0.2 shard_map.191
  54.7 2.5 %collective-permute-start.10 = (bf16[64,128]{1,0:T(8,128)(2,1)S(1)}, bf16[64,128]{1,0:T(8,128)(2,1)S(1)}, u32[]{:S(2)}, u32[]{:S(2)}) collective-permute-start(bf16[64,128]{1,0:T(8,128)(2,1)S(1)} %get-tuple-element.57.refs_3_), channel_id=1, source_target_pairs={{0,1},{1,2},{2,3},{3,0},{4,5},{5,6},{6,7},{7,4},{8,9},{9,10},{10,1... | collective-permute-start | bytes 49160 | tf_op jit(solution)/shard_map/ppermute | solution.py:422
  57.2 1.5 %shard_map.192 = (f32[8,256,512]{2,1,0:T(8,128)S(1)}, bf16[2048,128]{1,0:T(8,128)(2,1)S(1)}) custom-call(bf16[32,64,256]{2,1,0:T(8,128)(2,1)S(1)} %get-tuple-element.56.refs_0_, bf16[64,512]{1,0:T(8,128)(2,1)S(1)} %copy-done, bf16[4,8,128]{2,1,0:T(8,128)(2,1)S(1)} %bitcast.15, bf16[64,128]{1,0:T(8,128)(2,1)S(1)} %get-tuple-element.57.refs_3_), custom_call_target="tpu_custom_call" | custom-call | bytes 1048576 | tf_op jit(solution)/shard_map/pallas_call | solution.py:24
  58.7 5.6 %collective-permute-done.11.refs_6_ = bf16[64,128]{1,0:T(8,128)(2,1)S(1)} collective-permute-done((bf16[64,128]{1,0:T(8,128)(2,1)S(1)}, bf16[64,128]{1,0:T(8,128)(2,1)S(1)}, u32[]{:S(2)}, u32[]{:S(2)}) %collective-permute-start.11) | collective-permute-done | bytes 16416 | tf_op jit(solution)/shard_map/ppermute | solution.py:422
  64.3 8.2 %shard_map.193 = (bf16[256,128]{1,0:T(8,128)(2,1)S(1)}, bf16[64,128]{1,0:T(8,128)(2,1)S(1)}, bf16[64,128]{1,0:T(8,128)(2,1)S(1)}) custom-call(bf16[256,128]{1,0:T(8,128)(2,1)S(1)} %get-tuple-element.50.refs_3_.refs_1_.refs_0_, bf16[64,128]{1,0:T(8,128)(2,1)S(1)} %collective-permute-done.6.refs_2_.refs_1_, ...), custom_call_target="tpu_custom_call" | custom-call | bytes 1048576 | tf_op jit(solution)/shard_map/pallas_call | solution.py:24
  72.5 0.1 collective-permute-start.12
  72.6 2.7 %collective-permute-start.13 = (bf16[64,128]{1,0:T(8,128)(2,1)S(1)}, bf16[64,128]{1,0:T(8,128)(2,1)S(1)}, u32[]{:S(2)}, u32[]{:S(2)}) collective-permute-start(bf16[64,128]{1,0:T(8,128)(2,1)S(1)} %get-tuple-element.64), channel_id=1, source_target_pairs={{0,192},{64,0},{128,64},{192,128},{1,193},{65,1},{129,65},{193,129... | collective-permute-start | bytes 49160 | tf_op jit(solution)/shard_map/ppermute | solution.py:422
  75.3 0.6 shard_map.194
  75.9 0.5 collective-permute-done.12.refs_2_
  76.4 0.2 shard_map.195
  76.6 0.1 collective-permute-start.14
  76.7 5.4 %collective-permute-start.15 = (bf16[64,128]{1,0:T(8,128)(2,1)S(1)}, bf16[64,128]{1,0:T(8,128)(2,1)S(1)}, u32[]{:S(2)}, u32[]{:S(2)}) collective-permute-start(bf16[64,128]{1,0:T(8,128)(2,1)S(1)} %get-tuple-element.66), channel_id=1, source_target_pairs={{0,60},{4,0},{8,4},{12,8},{16,12},{20,16},{24,20},{28,24},{32,28},... | collective-permute-start | bytes 49160 | tf_op jit(solution)/shard_map/ppermute | solution.py:422
  82.1 1.1 %collective-permute-done.14.refs_4_ = bf16[64,128]{1,0:T(8,128)(2,1)S(1)} collective-permute-done((bf16[64,128]{1,0:T(8,128)(2,1)S(1)}, bf16[64,128]{1,0:T(8,128)(2,1)S(1)}, u32[]{:S(2)}, u32[]{:S(2)}) %collective-permute-start.14) | collective-permute-done | bytes 16416 | tf_op jit(solution)/shard_map/ppermute | solution.py:422
  83.2 0.2 shard_map.196
  83.4 2.5 %collective-permute-start.16 = (bf16[64,128]{1,0:T(8,128)(2,1)S(1)}, bf16[64,128]{1,0:T(8,128)(2,1)S(1)}, u32[]{:S(2)}, u32[]{:S(2)}) collective-permute-start(bf16[64,128]{1,0:T(8,128)(2,1)S(1)} %get-tuple-element.67), channel_id=1, source_target_pairs={{0,1},{1,2},{2,3},{3,0},{4,5},{5,6},{6,7},{7,4},{8,9},{9,10},{10,1... | collective-permute-start | bytes 49160 | tf_op jit(solution)/shard_map/ppermute | solution.py:422
  85.9 0.0 collective-permute-start.17
  85.9 0.9 collective-permute-done.16.refs_6_
  86.8 6.2 %collective-permute-done.17.refs_7_ = bf16[64,128]{1,0:T(8,128)(2,1)S(1)} collective-permute-done((bf16[64,128]{1,0:T(8,128)(2,1)S(1)}, bf16[64,128]{1,0:T(8,128)(2,1)S(1)}, u32[]{:S(2)}, u32[]{:S(2)}) %collective-permute-start.17) | collective-permute-done | bytes 16416 | tf_op jit(solution)/shard_map/ppermute | solution.py:422
  93.0 0.3 shard_map.197
  93.3 2.4 %collective-permute-start.18 = (bf16[32,128]{1,0:T(8,128)(2,1)S(1)}, bf16[32,128]{1,0:T(8,128)(2,1)S(1)}, u32[]{:S(2)}, u32[]{:S(2)}) collective-permute-start(bf16[32,128]{1,0:T(8,128)(2,1)S(1)} %get-tuple-element.69), channel_id=1, source_target_pairs={{0,56},{4,60},{8,16},{12,20},{16,8},{20,12},{24,32},{28,36},{32,24... | collective-permute-start | bytes 24584 | tf_op jit(solution)/shard_map/ppermute | solution.py:432
  95.7 3.4 %collective-permute-start.19 = (bf16[32,128]{1,0:T(8,128)(2,1)S(1)}, bf16[32,128]{1,0:T(8,128)(2,1)S(1)}, u32[]{:S(2)}, u32[]{:S(2)}) collective-permute-start(bf16[32,128]{1,0:T(8,128)(2,1)S(1)} %get-tuple-element.70), channel_id=1, source_target_pairs={{0,60},{4,8},{8,4},{12,16},{16,12},{20,24},{24,20},{28,32},{32,28}... | collective-permute-start | bytes 24584 | tf_op jit(solution)/shard_map/ppermute | solution.py:432
  99.2 2.3 %collective-permute-start.20 = (bf16[32,128]{1,0:T(8,128)(2,1)S(1)}, bf16[32,128]{1,0:T(8,128)(2,1)S(1)}, u32[]{:S(2)}, u32[]{:S(2)}) collective-permute-start(bf16[32,128]{1,0:T(8,128)(2,1)S(1)} %get-tuple-element.71), channel_id=1, source_target_pairs={{0,8},{4,12},{8,0},{12,4},{16,24},{20,28},{24,16},{28,20},{32,40},... | collective-permute-start | bytes 24584 | tf_op jit(solution)/shard_map/ppermute | solution.py:432
  101.4 0.7 collective-permute-done.19.refs_1_
  102.1 1.0 collective-permute-done.20.refs_2_
  103.2 0.8 collective-permute-done.21.refs_3_
  103.9 3.4 %shard_map.198 = f32[1,512]{1,0:T(1,128)} custom-call(bf16[32,128]{1,0:T(8,128)(2,1)S(1)} %collective-permute-done.18.refs_0_, bf16[32,128]{1,0:T(8,128)(2,1)S(1)} %collective-permute-done.19.refs_1_, bf16[32,128]{1,0:T(8,128)(2,1)S(1)} %collective-permute-done.20.refs_2_, bf16[32,128]{1,0:T(8,128)(2,1)S(1)} %collective-permute-done.21.refs_3_, ...), custom_call_target="tpu_custom_call" | custom-call | bytes 1048576 | tf_op jit(solution)/shard_map/pallas_call | solution.py:24
  (36 shorter events, 0.1 us)
Async XLA Ops:
  0.0 0.7 copy-start.16
  0.7 0.7 copy-start.18
  1.5 6.4 %collective-permute-start = (f32[8,128]{1,0:T(8,128)S(1)}, f32[8,128]{1,0:T(8,128)S(1)}, u32[]{:S(2)}, u32[]{:S(2)}) collective-permute-start(f32[8,128]{1,0:T(8,128)S(1)} %get-tuple-element.42.refs_3_), channel_id=1, source_target_pairs={{0,64},{64,128},{128,192},{192,0},{1,65},{65,129},{129,193},{193,1... | collective-permute-start | bytes 12296 | tf_op jit(solution)/shard_map/ppermute | solution.py:422
  3.5 4.4 %collective-permute-start.1 = (f32[8,128]{1,0:T(8,128)S(1)}, f32[8,128]{1,0:T(8,128)S(1)}, u32[]{:S(2)}, u32[]{:S(2)}) collective-permute-start(f32[8,128]{1,0:T(8,128)S(1)} %get-tuple-element.42.refs_3_), channel_id=1, source_target_pairs={{0,192},{64,0},{128,64},{192,128},{1,193},{65,1},{129,65},{193,129... | collective-permute-start | bytes 12296 | tf_op jit(solution)/shard_map/ppermute | solution.py:422
  4.8 0.9 copy-start.4
  5.7 0.8 copy-start.9
  6.5 0.7 copy-start.17
  8.1 13.3 %collective-permute-start.2 = (f32[8,128]{1,0:T(8,128)S(1)}, f32[8,128]{1,0:T(8,128)S(1)}, u32[]{:S(2)}, u32[]{:S(2)}) collective-permute-start(f32[8,128]{1,0:T(8,128)S(1)} %shard_map.183.refs_5_), channel_id=1, source_target_pairs={{0,4},{4,8},{8,12},{12,16},{16,20},{20,24},{24,28},{28,32},{32,36}... | collective-permute-start | bytes 12296 | tf_op jit(solution)/shard_map/ppermute | solution.py:422
  9.5 11.9 %collective-permute-start.3 = (f32[8,128]{1,0:T(8,128)S(1)}, f32[8,128]{1,0:T(8,128)S(1)}, u32[]{:S(2)}, u32[]{:S(2)}) collective-permute-start(f32[8,128]{1,0:T(8,128)S(1)} %shard_map.183.refs_5_), channel_id=1, source_target_pairs={{0,60},{4,0},{8,4},{12,8},{16,12},{20,16},{24,20},{28,24},{32,28},... | collective-permute-start | bytes 12296 | tf_op jit(solution)/shard_map/ppermute | solution.py:422
  15.1 0.8 copy-start.1
  15.9 0.8 copy-start.8
  16.7 0.7 copy-start.11
  17.3 0.7 copy-start.12
  21.4 14.2 %copy-start.3 = (bf16[512,128]{1,0:T(8,128)(2,1)S(1)}, bf16[512,128]{1,0:T(8,128)(2,1)}, u32[]{:S(2)}) copy-start(bf16[512,128]{1,0:T(8,128)(2,1)} %refs_14_.1) | copy-start | bytes 393220
  21.4 14.2 %copy-start.6 = (bf16[128,128]{1,0:T(8,128)(2,1)S(1)}, bf16[128,128]{1,0:T(8,128)(2,1)}, u32[]{:S(2)}) copy-start(bf16[128,128]{1,0:T(8,128)(2,1)} %refs_13_.1) | copy-start | bytes 98308
  21.4 14.2 %copy-start.7 = (bf16[128,128]{1,0:T(8,128)(2,1)S(1)}, bf16[128,128]{1,0:T(8,128)(2,1)}, u32[]{:S(2)}) copy-start(bf16[128,128]{1,0:T(8,128)(2,1)} %refs_15_.1) | copy-start | bytes 98308
  21.6 9.7 %collective-permute-start.4 = (f32[8,128]{1,0:T(8,128)S(1)}, f32[8,128]{1,0:T(8,128)S(1)}, u32[]{:S(2)}, u32[]{:S(2)}) collective-permute-start(f32[8,128]{1,0:T(8,128)S(1)} %shard_map.185.refs_2_), channel_id=1, source_target_pairs={{0,1},{1,2},{2,3},{3,0},{4,5},{5,6},{6,7},{7,4},{8,9},{9,10},{10,1... | collective-permute-start | bytes 12296 | tf_op jit(solution)/shard_map/ppermute | solution.py:422
  28.7 6.9 %collective-permute-start.5 = (f32[8,128]{1,0:T(8,128)S(1)}, f32[8,128]{1,0:T(8,128)S(1)}, u32[]{:S(2)}, u32[]{:S(2)}) collective-permute-start(f32[8,128]{1,0:T(8,128)S(1)} %shard_map.185.refs_2_), channel_id=1, source_target_pairs={{0,3},{1,0},{2,1},{3,2},{4,7},{5,4},{6,5},{7,6},{8,11},{9,8},{10,9... | collective-permute-start | bytes 12296 | tf_op jit(solution)/shard_map/ppermute | solution.py:422
  35.6 8.4 %copy-start = (bf16[64,512]{1,0:T(8,128)(2,1)S(1)}, bf16[64,512]{1,0:T(8,128)(2,1)}, u32[]{:S(2)}) copy-start(bf16[64,512]{1,0:T(8,128)(2,1)} %refs_1_.9) | copy-start | bytes 196612
  35.7 8.4 %copy-start.13 = (bf16[8,64]{1,0:T(8,128)(2,1)S(1)}, bf16[8,64]{1,0:T(8,128)(2,1)}, u32[]{:S(2)}) copy-start(bf16[8,64]{1,0:T(8,128)(2,1)} %refs_1_.7) | copy-start | bytes 3076
  41.3 4.9 %collective-permute-start.6 = (bf16[64,128]{1,0:T(8,128)(2,1)S(1)}, bf16[64,128]{1,0:T(8,128)(2,1)S(1)}, u32[]{:S(2)}, u32[]{:S(2)}) collective-permute-start(bf16[64,128]{1,0:T(8,128)(2,1)S(1)} %get-tuple-element.51), channel_id=1, source_target_pairs={{0,64},{64,128},{128,192},{192,0},{1,65},{65,129},{129,193},{193,1... | collective-permute-start | bytes 49160 | tf_op jit(solution)/shard_map/ppermute | solution.py:422
  41.4 4.8 %collective-permute-start.7 = (bf16[64,128]{1,0:T(8,128)(2,1)S(1)}, bf16[64,128]{1,0:T(8,128)(2,1)S(1)}, u32[]{:S(2)}, u32[]{:S(2)}) collective-permute-start(bf16[64,128]{1,0:T(8,128)(2,1)S(1)} %get-tuple-element.52), channel_id=1, source_target_pairs={{0,192},{64,0},{128,64},{192,128},{1,193},{65,1},{129,65},{193,129... | collective-permute-start | bytes 49160 | tf_op jit(solution)/shard_map/ppermute | solution.py:422
  46.4 8.0 %collective-permute-start.8 = (bf16[64,128]{1,0:T(8,128)(2,1)S(1)}, bf16[64,128]{1,0:T(8,128)(2,1)S(1)}, u32[]{:S(2)}, u32[]{:S(2)}) collective-permute-start(bf16[64,128]{1,0:T(8,128)(2,1)S(1)} %get-tuple-element.54.refs_2_), channel_id=1, source_target_pairs={{0,4},{4,8},{8,12},{12,16},{16,20},{20,24},{24,28},{28,32},{32,36}... | collective-permute-start | bytes 49160 | tf_op jit(solution)/shard_map/ppermute | solution.py:422
  46.5 7.9 %collective-permute-start.9 = (bf16[64,128]{1,0:T(8,128)(2,1)S(1)}, bf16[64,128]{1,0:T(8,128)(2,1)S(1)}, u32[]{:S(2)}, u32[]{:S(2)}) collective-permute-start(bf16[64,128]{1,0:T(8,128)(2,1)S(1)} %get-tuple-element.55), channel_id=1, source_target_pairs={{0,60},{4,0},{8,4},{12,8},{16,12},{20,16},{24,20},{28,24},{32,28},... | collective-permute-start | bytes 49160 | tf_op jit(solution)/shard_map/ppermute | solution.py:422
  51.9 5.3 %copy-start.10 = (bf16[4,128,8]{1,2,0:T(8,128)(2,1)S(1)}, bf16[4,128,8]{1,2,0:T(8,128)(2,1)}, u32[]{:S(2)}) copy-start(bf16[4,128,8]{1,2,0:T(8,128)(2,1)} %param.37) | copy-start | bytes 24580
  54.7 4.0 %collective-permute-start.10 = (bf16[64,128]{1,0:T(8,128)(2,1)S(1)}, bf16[64,128]{1,0:T(8,128)(2,1)S(1)}, u32[]{:S(2)}, u32[]{:S(2)}) collective-permute-start(bf16[64,128]{1,0:T(8,128)(2,1)S(1)} %get-tuple-element.57.refs_3_), channel_id=1, source_target_pairs={{0,1},{1,2},{2,3},{3,0},{4,5},{5,6},{6,7},{7,4},{8,9},{9,10},{10,1... | collective-permute-start | bytes 49160 | tf_op jit(solution)/shard_map/ppermute | solution.py:422
  57.2 7.1 %collective-permute-start.11 = (bf16[64,128]{1,0:T(8,128)(2,1)S(1)}, bf16[64,128]{1,0:T(8,128)(2,1)S(1)}, u32[]{:S(2)}, u32[]{:S(2)}) collective-permute-start(bf16[64,128]{1,0:T(8,128)(2,1)S(1)} %get-tuple-element.58), channel_id=1, source_target_pairs={{0,3},{1,0},{2,1},{3,2},{4,7},{5,4},{6,5},{7,6},{8,11},{9,8},{10,9... | collective-permute-start | bytes 49160 | tf_op jit(solution)/shard_map/ppermute | solution.py:422
  64.3 11.0 %copy-start.2 = (f32[1,1,1,3,32,512]{5,4,3,2,1,0:T(8,128)S(1)}, f32[1,1,1,3,32,512]{5,4,3,2,1,0:T(8,128)}, u32[]{:S(2)}) copy-start(f32[1,1,1,3,32,512]{5,4,3,2,1,0:T(8,128)} %param.27) | copy-start | bytes 589828
  64.3 11.0 %copy-start.5 = (s32[1,1,1,32,512]{4,3,2,1,0:T(8,128)S(1)}, s32[1,1,1,32,512]{4,3,2,1,0:T(8,128)}, u32[]{:S(2)}) copy-start(s32[1,1,1,32,512]{4,3,2,1,0:T(8,128)} %param.25) | copy-start | bytes 196612
  64.3 11.0 %copy-start.14 = (s32[1,1,1,512]{3,2,1,0:T(1,128)S(1)}, s32[1,1,1,512]{3,2,1,0:T(1,128)}, u32[]{:S(2)}) copy-start(s32[1,1,1,512]{3,2,1,0:T(1,128)} %param.24) | copy-start | bytes 6148
  64.3 11.0 %copy-start.15 = (s32[1,1,1,512]{3,2,1,0:T(1,128)S(1)}, s32[1,1,1,512]{3,2,1,0:T(1,128)}, u32[]{:S(2)}) copy-start(s32[1,1,1,512]{3,2,1,0:T(1,128)} %param.26) | copy-start | bytes 6148
  72.5 3.9 %collective-permute-start.12 = (bf16[64,128]{1,0:T(8,128)(2,1)S(1)}, bf16[64,128]{1,0:T(8,128)(2,1)S(1)}, u32[]{:S(2)}, u32[]{:S(2)}) collective-permute-start(bf16[64,128]{1,0:T(8,128)(2,1)S(1)} %get-tuple-element.63), channel_id=1, source_target_pairs={{0,64},{64,128},{128,192},{192,0},{1,65},{65,129},{129,193},{193,1... | collective-permute-start | bytes 49160 | tf_op jit(solution)/shard_map/ppermute | solution.py:422
  72.6 3.8 %collective-permute-start.13 = (bf16[64,128]{1,0:T(8,128)(2,1)S(1)}, bf16[64,128]{1,0:T(8,128)(2,1)S(1)}, u32[]{:S(2)}, u32[]{:S(2)}) collective-permute-start(bf16[64,128]{1,0:T(8,128)(2,1)S(1)} %get-tuple-element.64), channel_id=1, source_target_pairs={{0,192},{64,0},{128,64},{192,128},{1,193},{65,1},{129,65},{193,129... | collective-permute-start | bytes 49160 | tf_op jit(solution)/shard_map/ppermute | solution.py:422
  76.6 6.6 %collective-permute-start.14 = (bf16[64,128]{1,0:T(8,128)(2,1)S(1)}, bf16[64,128]{1,0:T(8,128)(2,1)S(1)}, u32[]{:S(2)}, u32[]{:S(2)}) collective-permute-start(bf16[64,128]{1,0:T(8,128)(2,1)S(1)} %get-tuple-element.65), channel_id=1, source_target_pairs={{0,4},{4,8},{8,12},{12,16},{16,20},{20,24},{24,28},{28,32},{32,36}... | collective-permute-start | bytes 49160 | tf_op jit(solution)/shard_map/ppermute | solution.py:422
  76.7 6.5 %collective-permute-start.15 = (bf16[64,128]{1,0:T(8,128)(2,1)S(1)}, bf16[64,128]{1,0:T(8,128)(2,1)S(1)}, u32[]{:S(2)}, u32[]{:S(2)}) collective-permute-start(bf16[64,128]{1,0:T(8,128)(2,1)S(1)} %get-tuple-element.66), channel_id=1, source_target_pairs={{0,60},{4,0},{8,4},{12,8},{16,12},{20,16},{24,20},{28,24},{32,28},... | collective-permute-start | bytes 49160 | tf_op jit(solution)/shard_map/ppermute | solution.py:422
  83.4 3.4 %collective-permute-start.16 = (bf16[64,128]{1,0:T(8,128)(2,1)S(1)}, bf16[64,128]{1,0:T(8,128)(2,1)S(1)}, u32[]{:S(2)}, u32[]{:S(2)}) collective-permute-start(bf16[64,128]{1,0:T(8,128)(2,1)S(1)} %get-tuple-element.67), channel_id=1, source_target_pairs={{0,1},{1,2},{2,3},{3,0},{4,5},{5,6},{6,7},{7,4},{8,9},{9,10},{10,1... | collective-permute-start | bytes 49160 | tf_op jit(solution)/shard_map/ppermute | solution.py:422
  85.9 7.1 %collective-permute-start.17 = (bf16[64,128]{1,0:T(8,128)(2,1)S(1)}, bf16[64,128]{1,0:T(8,128)(2,1)S(1)}, u32[]{:S(2)}, u32[]{:S(2)}) collective-permute-start(bf16[64,128]{1,0:T(8,128)(2,1)S(1)} %get-tuple-element.68), channel_id=1, source_target_pairs={{0,3},{1,0},{2,1},{3,2},{4,7},{5,4},{6,5},{7,6},{8,11},{9,8},{10,9... | collective-permute-start | bytes 49160 | tf_op jit(solution)/shard_map/ppermute | solution.py:422
  93.3 8.1 %collective-permute-start.18 = (bf16[32,128]{1,0:T(8,128)(2,1)S(1)}, bf16[32,128]{1,0:T(8,128)(2,1)S(1)}, u32[]{:S(2)}, u32[]{:S(2)}) collective-permute-start(bf16[32,128]{1,0:T(8,128)(2,1)S(1)} %get-tuple-element.69), channel_id=1, source_target_pairs={{0,56},{4,60},{8,16},{12,20},{16,8},{20,12},{24,32},{28,36},{32,24... | collective-permute-start | bytes 24584 | tf_op jit(solution)/shard_map/ppermute | solution.py:432
  95.7 6.4 %collective-permute-start.19 = (bf16[32,128]{1,0:T(8,128)(2,1)S(1)}, bf16[32,128]{1,0:T(8,128)(2,1)S(1)}, u32[]{:S(2)}, u32[]{:S(2)}) collective-permute-start(bf16[32,128]{1,0:T(8,128)(2,1)S(1)} %get-tuple-element.70), channel_id=1, source_target_pairs={{0,60},{4,8},{8,4},{12,16},{16,12},{20,24},{24,20},{28,32},{32,28}... | collective-permute-start | bytes 24584 | tf_op jit(solution)/shard_map/ppermute | solution.py:432
  99.2 4.0 %collective-permute-start.20 = (bf16[32,128]{1,0:T(8,128)(2,1)S(1)}, bf16[32,128]{1,0:T(8,128)(2,1)S(1)}, u32[]{:S(2)}, u32[]{:S(2)}) collective-permute-start(bf16[32,128]{1,0:T(8,128)(2,1)S(1)} %get-tuple-element.71), channel_id=1, source_target_pairs={{0,8},{4,12},{8,0},{12,4},{16,24},{20,28},{24,16},{28,20},{32,40},... | collective-permute-start | bytes 24584 | tf_op jit(solution)/shard_map/ppermute | solution.py:432
  101.4 2.5 %collective-permute-start.21 = (bf16[32,128]{1,0:T(8,128)(2,1)S(1)}, bf16[32,128]{1,0:T(8,128)(2,1)S(1)}, u32[]{:S(2)}, u32[]{:S(2)}) collective-permute-start(bf16[32,128]{1,0:T(8,128)(2,1)S(1)} %get-tuple-element.72), channel_id=1, source_target_pairs={{0,4},{4,0},{8,12},{12,8},{16,20},{20,16},{24,28},{28,24},{32,36},... | collective-permute-start | bytes 24584 | tf_op jit(solution)/shard_map/ppermute | solution.py:432

commit v4 on v3

--- a/solution.py
+++ b/solution.py
@@ -12,24 +12,40 @@
 F32 = jnp.float32
 BF16 = jnp.bfloat16
 VMEM = pl.BlockSpec(memory_space=pltpu.VMEM)
+HBM = pl.BlockSpec(memory_space=pltpu.HBM)
 ANY = pl.BlockSpec(memory_space=pl.ANY)
 
 
-def call(kernel, out_shape, operands, scratch=(), limit=8, after=()):
-    count = len(operands)
+def call(kernel, out_shape, operands, scratch=(), limit=8, staged=(), after=()):
+    first, last = len(staged), len(staged) + len(operands)
 
     def body(*refs):
-        kernel(*refs[:count], *refs[count + len(after) :])
-
+        if not staged:
+            return kernel(*refs[:last], *refs[last + len(after) :])
+        buffers, arrived = refs[-1 - first : -1], refs[-1]
+        copies = [
+            pltpu.make_async_copy(source, target, arrived.at[n])
+            for n, (source, target) in enumerate(zip(refs, buffers))
+        ]
+        for copy in copies:
+            copy.start()
+        for copy in copies:
+            copy.wait()
+        kernel(*buffers, *refs[first:last], *refs[last + len(after) : -1 - first])
+
+    room = [pltpu.VMEM(x.shape, x.dtype) for x in staged]
+    if staged:
+        room.append(pltpu.SemaphoreType.DMA((first,)))
+    held = [pltpu.with_memory_space_constraint(x, pltpu.HBM) for x in staged]
     return pl.pallas_call(
         body,
         out_shape=out_shape,
-        in_specs=[VMEM] * count + [ANY] * len(after),
+        in_specs=[HBM] * first + [VMEM] * len(operands) + [ANY] * len(after),
         out_specs=jax.tree.map(lambda _: VMEM, out_shape),
-        scratch_shapes=list(scratch),
-        compiler_params=pltpu.CompilerParams(vmem_limit_bytes=limit and limit << 20),
+        scratch_shapes=[*scratch, *room],
+        compiler_params=pltpu.CompilerParams(vmem_limit_bytes=limit << 20),
         cost_estimate=pl.CostEstimate(flops=0, bytes_accessed=1 << 20, transcendentals=0),
-    )(*operands, *after)
+    )(*held, *operands, *after)
 
 
 def dot(a, b):
@@ -168,21 +184,9 @@
     return jnp.concatenate(parts, axis=1)
 
 
-def transposed(ref):
-    return ref[...].astype(F32).T.astype(BF16)
-
-
-def hidden_rows(phi_ref, in_ref, hid_ref):
-    groups = hid_ref.shape[0]
-    into = transposed(in_ref)
-    for g in range(groups):
-        value = dot(into, basis_rows(phi_ref, g, groups).astype(BF16))
-        hid_ref[g] = (value / (1.0 + jnp.exp(-value))).astype(BF16)
-
-
 def radial_rows(first, hid_ref, out_ref, radial_ref):
     def step(g, carry):
-        radial_ref[g] = dot_first(hid_ref[first + g], out_ref[...])
+        radial_ref[g] = dot(hid_ref[first + g], out_ref[...])
         return carry
 
     lax.fori_loop(0, radial_ref.shape[0], step, 0, unroll=2)
@@ -202,11 +206,19 @@
 
 
 def first_radial_kernel(
-    phi_ref, in_ref, out_ref, emb_ref, msg_ref, hid_ref, rows_ref, radial_ref
+    in1_ref, in2_ref, out1_ref, out2_ref, emb_ref, msg_ref, phi_ref,
+    hid_ref, rows_ref, wide1_ref, wide2_ref, radial_ref,
 ):
     rows_ref[...] = dot(emb_ref[...], msg_ref[...]).astype(BF16)
-    hidden_rows(phi_ref, in_ref, hid_ref)
-    radial_rows(0, hid_ref, out_ref, radial_ref)
+    empty = jnp.zeros((64, 512), BF16)
+    wide1_ref[:64, :], wide1_ref[64:, :] = out1_ref[...], empty
+    wide2_ref[:64, :], wide2_ref[64:, :] = empty, out2_ref[...]
+    groups = hid_ref.shape[0]
+    into = jnp.concatenate([in1_ref[...], in2_ref[...]], axis=1)
+    for g in range(groups):
+        value = dot_first(basis_rows(phi_ref, g, groups).astype(BF16), into)
+        hid_ref[g] = (value / (1.0 + jnp.exp(-value))).astype(BF16)
+    radial_rows(0, hid_ref, wide1_ref, radial_ref)
 
 
 def radial_kernel(first):
@@ -214,11 +226,6 @@
         radial_rows(first, hid_ref, out_ref, radial_ref)
 
     return kernel
-
-
-def second_radial_kernel(phi_ref, in_ref, out_ref, hid_ref, radial_ref):
-    hidden_rows(phi_ref, in_ref, hid_ref)
-    radial_rows(0, hid_ref, out_ref, radial_ref)
 
 
 def last_radial_kernel(first):
@@ -464,7 +471,8 @@
         return [shifted(block, axis, 1), shifted(block, axis, -1)]
 
     row = shape((8, 128), F32)
-    hidden = shape((slots, 64, atoms), BF16)
+    hidden = shape((slots, atoms, 128), BF16)
+    wide = shape((128, 512), BF16)
 
     def radial(count):
         return shape((count, atoms, 512), F32)
@@ -472,7 +480,8 @@
     chosen, kinds, lists = call(
         first_kernel,
         (row, shape(kinds.shape, jnp.int32), shape(lists.shape, jnp.int32)),
-        (kinds, lists),
+        (),
+        staged=(kinds, lists),
     )
     ghosts = both(chosen, "gx")
     angular, phi, where = call(
@@ -482,7 +491,8 @@
             shape((2, BASIS * slots, 128), F32),
             shape((slots, atoms), jnp.int32),
         ),
-        (
+        (),
+        staged=(
             edge_vectors.reshape(3, slots, atoms),
             neighbour_count.reshape(1, atoms),
             neighbour_index.reshape(slots, atoms),
@@ -491,16 +501,26 @@
     )
     chosen = call(pick_species(1), row, (kinds, lists, *ghosts), after=(where,))
     ghosts += both(chosen, "gy")
-    hidden_one, rows, radial_a = call(
+    hidden_both, rows, wide_one, wide_two, radial_a = call(
         first_radial_kernel,
-        (hidden, shape((8, 128), BF16), radial(16)),
-        (phi, radial_in_one, radial_out_one, embedding, message_one),
+        (hidden, shape((8, 128), BF16), wide, wide, radial(8)),
+        (phi,),
         limit=20,
+        staged=(
+            radial_in_one,
+            radial_in_two,
+            radial_out_one,
+            radial_out_two,
+            embedding,
+            message_one,
+        ),
         after=(chosen,),
     )
     chosen = call(pick_species(2), row, (kinds, lists, *ghosts), after=(radial_a,))
     ghosts += both(chosen, "gz")
-    radial_b = call(radial_kernel(16), radial(16), (hidden_one, radial_out_one), limit=20, after=(chosen,))
+    radial_b = call(
+        radial_kernel(8), radial(24), (hidden_both, wide_one), limit=30, after=(chosen,)
+    )
     second = call(
         layer_one_kernel,
         (shape((atoms, 128), BF16), half, half),
@@ -513,18 +533,20 @@
         *second,
         lists,
         (
-            lambda made, begin: call(
-                second_radial_kernel,
-                (hidden, radial(8)),
-                (phi, radial_in_two, radial_out_two),
-                limit=20,
-                after=(begin,),
+            lambda made, begin: (
+                call(
+                    radial_kernel(0),
+                    radial(8),
+                    (hidden_both, wide_two),
+                    limit=20,
+                    after=(begin,),
+                ),
             ),
             lambda made, begin: (
                 call(
                     radial_kernel(8),
                     radial(16),
-                    (made[0][0], radial_out_two),
+                    (hidden_both, wide_two),
                     limit=20,
                     after=(begin,),
                 ),
@@ -532,7 +554,7 @@
             lambda made, begin: call(
                 last_radial_kernel(24),
                 (radial(8), shape((2048, 128), BF16)),
-                (made[0][0], radial_out_two, decoder.transpose(0, 2, 1)),
+                (hidden_both, wide_two, decoder.transpose(0, 2, 1)),
                 limit=20,
                 after=(begin,),
             ),
@@ -541,7 +563,7 @@
     coeffs = call(
         layer_two_kernel,
         (shape((atoms, 128), BF16), half, half),
-        (second[0], *pieces, where, angular, made[0][1], made[1][0], *made[2], lists),
+        (second[0], *pieces, where, angular, made[0][0], made[1][0], *made[2], lists),
         [
             pltpu.VMEM((atoms, 2048), BF16),
             pltpu.VMEM((256, 384), BF16),

time: 108 us -> 103 us (0.954)
  local copies, waits for them, and re-layouts: 6.69 us -> 0.04 us
  starting transfers between devices: 47 us -> 48.9 us
    unnamed x38 -> x18, local copies, waits for them, and re-layouts: 6.69 us -> 0.04 us
    ppermute x18, starting transfers between devices: 38.9 us -> 40.8 us  [shifted(): lax.ppermute(block, axis, [(i, (i + step) % size) for i in range(size)])]
  transfers between devices with their start and end apart: 22 -> 22, of which waited for: 9 -> 9; matrix products, arithmetic and copies ran while one was open for 0% -> 0% of each run, Pallas kernels for 12% -> 13%
where the time goes in v4:
time: 103 us
  starting transfers between devices  48.9 us (47%)
  Pallas kernels  33.1 us (32%)
  waiting for transfers between devices  20.4 us (20%)
    ppermute x18, starting transfers between devices, shifted(): lax.ppermute(block, axis, [(i, (i + step) % size) for i in range(size)])  40.8 us
    pallas_call x18, Pallas kernels, call(): pl.pallas_call(body, out_shape=out_shape, in_specs=[HBM] * first + [VMEM]...  33.1 us
    ppermute x18, waiting for transfers between devices, shifted(): lax.ppermute(block, axis, [(i, (i + step) % size) for i in range(size)])  17.9 us
    ppermute x4, starting transfers between devices, swapped_with(): return lax.ppermute(block, 'gy', sorted(pairs))  8.1 us
    ppermute x4, waiting for transfers between devices, swapped_with(): return lax.ppermute(block, 'gy', sorted(pairs))  2.5 us
  transfers between devices with their start and end apart: 22, of which 9 were waited for; matrix products, arithmetic and copies ran while one was open for 0% of the time, Pallas kernels for 13%

profile of v4, /device:TPU:1, one launch (start us, length us, event | category | flops | bytes accessed | tf_op | source)
XLA Modules:
  0.0 102.7 jit_solution(3284686899689924581)
XLA Ops:
  0.0 0.8 shard_map.181
  0.9 2.1 %collective-permute-start = (f32[8,128]{1,0:T(8,128)S(1)}, f32[8,128]{1,0:T(8,128)S(1)}, u32[]{:S(2)}, u32[]{:S(2)}) collective-permute-start(f32[8,128]{1,0:T(8,128)S(1)} %get-tuple-element.42.refs_3_), channel_id=1, source_target_pairs={{0,64},{64,128},{128,192},{192,0},{1,65},{65,129},{129,193},{193,1... | collective-permute-start | bytes 12296 | tf_op jit(solution)/shard_map/ppermute | solution.py:429
  3.0 1.4 %collective-permute-start.1 = (f32[8,128]{1,0:T(8,128)S(1)}, f32[8,128]{1,0:T(8,128)S(1)}, u32[]{:S(2)}, u32[]{:S(2)}) collective-permute-start(f32[8,128]{1,0:T(8,128)S(1)} %get-tuple-element.42.refs_3_), channel_id=1, source_target_pairs={{0,192},{64,0},{128,64},{192,128},{1,193},{65,1},{129,65},{193,129... | collective-permute-start | bytes 12296 | tf_op jit(solution)/shard_map/ppermute | solution.py:429
  4.3 1.6 %shard_map.182 = (f32[2,512,128]{2,1,0:T(8,128)S(1)}, f32[2,256,128]{2,1,0:T(8,128)S(1)}, s32[32,256]{1,0:T(8,128)S(1)}) custom-call(f32[3,32,256]{2,1,0:T(8,128)} %bitcast.16, s32[1,256]{1,0:T(1,128)} %bitcast.19, s32[32,256]{1,0:T(8,128)} %bitcast.17, f32[8,128]{1,0:T(8,128)S(1)} %get-tuple-element.42.refs_3_), custom_call_target="tpu_custom_call" | custom-call | bytes 1048576 | tf_op jit(solution)/shard_map/pallas_call | solution.py:40
  6.0 0.0 collective-permute-done.refs_2_.refs_1_
  6.0 0.0 collective-permute-done.1.refs_3_.refs_2_
  6.0 0.1 shard_map.183.refs_7_
  6.1 1.4 %collective-permute-start.2 = (f32[8,128]{1,0:T(8,128)S(1)}, f32[8,128]{1,0:T(8,128)S(1)}, u32[]{:S(2)}, u32[]{:S(2)}) collective-permute-start(f32[8,128]{1,0:T(8,128)S(1)} %shard_map.183.refs_7_), channel_id=1, source_target_pairs={{0,4},{4,8},{8,12},{12,16},{16,20},{20,24},{24,28},{28,32},{32,36}... | collective-permute-start | bytes 12296 | tf_op jit(solution)/shard_map/ppermute | solution.py:429
  7.5 5.6 %collective-permute-start.3 = (f32[8,128]{1,0:T(8,128)S(1)}, f32[8,128]{1,0:T(8,128)S(1)}, u32[]{:S(2)}, u32[]{:S(2)}) collective-permute-start(f32[8,128]{1,0:T(8,128)S(1)} %shard_map.183.refs_7_), channel_id=1, source_target_pairs={{0,60},{4,0},{8,4},{12,8},{16,12},{20,16},{24,20},{28,24},{32,28},... | collective-permute-start | bytes 12296 | tf_op jit(solution)/shard_map/ppermute | solution.py:429
  13.1 3.4 %shard_map.184 = (bf16[32,256,128]{2,1,0:T(8,128)(2,1)S(1)}, bf16[8,128]{1,0:T(8,128)(2,1)S(1)}, bf16[128,512]{1,0:T(8,128)(2,1)S(1)}, bf16[128,512]{1,0:T(8,128)(2,1)S(1)}, f32[8,256,512]{2,1,0:T(8,128)S(1)}) custom-call(bf16[8,64]{1,0:T(8,128)(2,1)} %refs_0_.1, bf16[8,64]{1,0:T(8,128)(2,1)} %refs_1_.1, bf16[64,512]{1,0:T(8,128)(2,1)} %refs_2_.1, ...), custom_call_target="tpu_custom_call" | custom-call | bytes 1048576 | tf_op jit(solution)/shard_map/pallas_call | solution.py:40
  16.5 0.0 collective-permute-done.2.refs_4_.refs_3_
  16.5 0.0 collective-permute-done.3.refs_5_.refs_4_
  16.6 0.1 shard_map.185.refs_2_
  16.7 7.3 %collective-permute-start.4 = (f32[8,128]{1,0:T(8,128)S(1)}, f32[8,128]{1,0:T(8,128)S(1)}, u32[]{:S(2)}, u32[]{:S(2)}) collective-permute-start(f32[8,128]{1,0:T(8,128)S(1)} %shard_map.185.refs_2_), channel_id=1, source_target_pairs={{0,1},{1,2},{2,3},{3,0},{4,5},{5,6},{6,7},{7,4},{8,9},{9,10},{10,1... | collective-permute-start | bytes 12296 | tf_op jit(solution)/shard_map/ppermute | solution.py:429
  24.0 0.0 collective-permute-start.5
  24.0 0.0 copy-start.6
  24.0 3.3 %shard_map.186.refs_10_ = f32[24,256,512]{2,1,0:T(8,128)S(1)} custom-call(bf16[32,256,128]{2,1,0:T(8,128)(2,1)S(1)} %get-tuple-element.48.refs_0_, bf16[128,512]{1,0:T(8,128)(2,1)S(1)} %get-tuple-element.49.refs_1_, f32[8,128]{1,0:T(8,128)S(1)} %shard_map.185.refs_2_), custom_call_target="tpu_custom_call" | custom-call | bytes 1048576 | tf_op jit(solution)/shard_map/pallas_call | solution.py:40
  27.4 0.0 collective-permute-done.4.refs_5_
  27.4 3.6 %collective-permute-done.5.refs_6_ = f32[8,128]{1,0:T(8,128)S(1)} collective-permute-done((f32[8,128]{1,0:T(8,128)S(1)}, f32[8,128]{1,0:T(8,128)S(1)}, u32[]{:S(2)}, u32[]{:S(2)}) %collective-permute-start.5) | collective-permute-done | bytes 4128 | tf_op jit(solution)/shard_map/ppermute | solution.py:429
  31.0 5.5 %shard_map.187 = (bf16[256,128]{1,0:T(8,128)(2,1)S(1)}, bf16[64,128]{1,0:T(8,128)(2,1)S(1)}, bf16[64,128]{1,0:T(8,128)(2,1)S(1)}) custom-call(s32[1,256]{1,0:T(1,128)S(1)} %get-tuple-element.41.refs_0_, f32[8,128]{1,0:T(8,128)S(1)} %collective-permute-done.refs_2_.refs_1_, f32[8,128]{1,0:T(8,128)S(1)} %collective-permute-done.1.refs_3_.refs_2_, ...), custom_call_target="tpu_custom_call" | custom-call | bytes 1048576 | tf_op jit(solution)/shard_map/pallas_call | solution.py:40
  36.5 1.3 %collective-permute-start.6 = (bf16[64,128]{1,0:T(8,128)(2,1)S(1)}, bf16[64,128]{1,0:T(8,128)(2,1)S(1)}, u32[]{:S(2)}, u32[]{:S(2)}) collective-permute-start(bf16[64,128]{1,0:T(8,128)(2,1)S(1)} %get-tuple-element.52), channel_id=1, source_target_pairs={{0,64},{64,128},{128,192},{192,0},{1,65},{65,129},{129,193},{193,1... | collective-permute-start | bytes 49160 | tf_op jit(solution)/shard_map/ppermute | solution.py:429
  37.8 1.6 %collective-permute-start.7 = (bf16[64,128]{1,0:T(8,128)(2,1)S(1)}, bf16[64,128]{1,0:T(8,128)(2,1)S(1)}, u32[]{:S(2)}, u32[]{:S(2)}) collective-permute-start(bf16[64,128]{1,0:T(8,128)(2,1)S(1)} %get-tuple-element.53), channel_id=1, source_target_pairs={{0,192},{64,0},{128,64},{192,128},{1,193},{65,1},{129,65},{193,129... | collective-permute-start | bytes 49160 | tf_op jit(solution)/shard_map/ppermute | solution.py:429
  39.3 1.1 %shard_map.188.refs_4_.refs_9_ = f32[8,256,512]{2,1,0:T(8,128)S(1)} custom-call(bf16[32,256,128]{2,1,0:T(8,128)(2,1)S(1)} %get-tuple-element.48.refs_0_, bf16[128,512]{1,0:T(8,128)(2,1)S(1)} %get-tuple-element.54.refs_1_, bf16[256,128]{1,0:T(8,128)(2,1)S(1)} %get-tuple-element.51.refs_2_.refs_1_.refs_0_), custom_call_target="tpu_custom_call" | custom-call | bytes 1048576 | tf_op jit(solution)/shard_map/pallas_call | solution.py:40
  40.4 0.0 collective-permute-done.6.refs_2_.refs_1_
  40.5 0.0 collective-permute-done.7.refs_3_.refs_2_
  40.5 0.2 shard_map.189
  40.7 0.1 collective-permute-start.8
  40.8 5.4 %collective-permute-start.9 = (bf16[64,128]{1,0:T(8,128)(2,1)S(1)}, bf16[64,128]{1,0:T(8,128)(2,1)S(1)}, u32[]{:S(2)}, u32[]{:S(2)}) collective-permute-start(bf16[64,128]{1,0:T(8,128)(2,1)S(1)} %get-tuple-element.56), channel_id=1, source_target_pairs={{0,60},{4,0},{8,4},{12,8},{16,12},{20,16},{24,20},{28,24},{32,28},... | collective-permute-start | bytes 49160 | tf_op jit(solution)/shard_map/ppermute | solution.py:429
  46.1 2.2 %shard_map.190.refs_6_.refs_10_ = f32[16,256,512]{2,1,0:T(8,128)S(1)} custom-call(bf16[32,256,128]{2,1,0:T(8,128)(2,1)S(1)} %get-tuple-element.48.refs_0_, bf16[128,512]{1,0:T(8,128)(2,1)S(1)} %get-tuple-element.54.refs_1_, bf16[64,128]{1,0:T(8,128)(2,1)S(1)} %get-tuple-element.55.refs_2_), custom_call_target="tpu_custom_call" | custom-call | bytes 1048576 | tf_op jit(solution)/shard_map/pallas_call | solution.py:40
  48.4 0.0 copy-start.5
  48.4 0.0 collective-permute-done.8.refs_4_.refs_3_
  48.4 0.0 collective-permute-done.9.refs_5_.refs_4_
  48.4 0.2 shard_map.191
  48.6 4.1 %collective-permute-start.10 = (bf16[64,128]{1,0:T(8,128)(2,1)S(1)}, bf16[64,128]{1,0:T(8,128)(2,1)S(1)}, u32[]{:S(2)}, u32[]{:S(2)}) collective-permute-start(bf16[64,128]{1,0:T(8,128)(2,1)S(1)} %get-tuple-element.57.refs_3_), channel_id=1, source_target_pairs={{0,1},{1,2},{2,3},{3,0},{4,5},{5,6},{6,7},{7,4},{8,9},{9,10},{10,1... | collective-permute-start | bytes 49160 | tf_op jit(solution)/shard_map/ppermute | solution.py:429
  52.7 0.0 collective-permute-start.11
  52.7 1.3 %shard_map.192 = (f32[8,256,512]{2,1,0:T(8,128)S(1)}, bf16[2048,128]{1,0:T(8,128)(2,1)S(1)}) custom-call(bf16[32,256,128]{2,1,0:T(8,128)(2,1)S(1)} %get-tuple-element.48.refs_0_, bf16[128,512]{1,0:T(8,128)(2,1)S(1)} %get-tuple-element.54.refs_1_, bf16[4,8,128]{2,1,0:T(8,128)(2,1)S(1)} %bitcast.13, bf16[64,128]{1,0:T(8,128)(2,1)S(1)} %get-tuple-element.57.refs_3_), custom_call_target="tpu_custom_call" | custom-call | bytes 1048576 | tf_op jit(solution)/shard_map/pallas_call | solution.py:40
  54.0 0.0 collective-permute-done.10.refs_5_
  54.1 5.7 %collective-permute-done.11.refs_6_ = bf16[64,128]{1,0:T(8,128)(2,1)S(1)} collective-permute-done((bf16[64,128]{1,0:T(8,128)(2,1)S(1)}, bf16[64,128]{1,0:T(8,128)(2,1)S(1)}, u32[]{:S(2)}, u32[]{:S(2)}) %collective-permute-start.11) | collective-permute-done | bytes 16416 | tf_op jit(solution)/shard_map/ppermute | solution.py:429
  59.8 8.2 %shard_map.193 = (bf16[256,128]{1,0:T(8,128)(2,1)S(1)}, bf16[64,128]{1,0:T(8,128)(2,1)S(1)}, bf16[64,128]{1,0:T(8,128)(2,1)S(1)}) custom-call(bf16[256,128]{1,0:T(8,128)(2,1)S(1)} %get-tuple-element.51.refs_2_.refs_1_.refs_0_, bf16[64,128]{1,0:T(8,128)(2,1)S(1)} %collective-permute-done.6.refs_2_.refs_1_, ...), custom_call_target="tpu_custom_call" | custom-call | bytes 1048576 | tf_op jit(solution)/shard_map/pallas_call | solution.py:40
  68.0 1.0 collective-permute-start.12
  69.0 1.9 %collective-permute-start.13 = (bf16[64,128]{1,0:T(8,128)(2,1)S(1)}, bf16[64,128]{1,0:T(8,128)(2,1)S(1)}, u32[]{:S(2)}, u32[]{:S(2)}) collective-permute-start(bf16[64,128]{1,0:T(8,128)(2,1)S(1)} %get-tuple-element.64), channel_id=1, source_target_pairs={{0,192},{64,0},{128,64},{192,128},{1,193},{65,1},{129,65},{193,129... | collective-permute-start | bytes 49160 | tf_op jit(solution)/shard_map/ppermute | solution.py:429
  70.9 0.6 shard_map.194
  71.5 0.4 collective-permute-done.12.refs_2_
  71.9 0.0 collective-permute-done.13.refs_3_
  71.9 0.2 shard_map.195
  72.2 0.1 collective-permute-start.14
  72.2 5.4 %collective-permute-start.15 = (bf16[64,128]{1,0:T(8,128)(2,1)S(1)}, bf16[64,128]{1,0:T(8,128)(2,1)S(1)}, u32[]{:S(2)}, u32[]{:S(2)}) collective-permute-start(bf16[64,128]{1,0:T(8,128)(2,1)S(1)} %get-tuple-element.66), channel_id=1, source_target_pairs={{0,60},{4,0},{8,4},{12,8},{16,12},{20,16},{24,20},{28,24},{32,28},... | collective-permute-start | bytes 49160 | tf_op jit(solution)/shard_map/ppermute | solution.py:429
  77.6 1.1 %collective-permute-done.14.refs_4_ = bf16[64,128]{1,0:T(8,128)(2,1)S(1)} collective-permute-done((bf16[64,128]{1,0:T(8,128)(2,1)S(1)}, bf16[64,128]{1,0:T(8,128)(2,1)S(1)}, u32[]{:S(2)}, u32[]{:S(2)}) %collective-permute-start.14) | collective-permute-done | bytes 16416 | tf_op jit(solution)/shard_map/ppermute | solution.py:429
  78.7 0.0 collective-permute-done.15.refs_5_
  78.7 0.2 shard_map.196
  79.0 2.4 %collective-permute-start.16 = (bf16[64,128]{1,0:T(8,128)(2,1)S(1)}, bf16[64,128]{1,0:T(8,128)(2,1)S(1)}, u32[]{:S(2)}, u32[]{:S(2)}) collective-permute-start(bf16[64,128]{1,0:T(8,128)(2,1)S(1)} %get-tuple-element.67), channel_id=1, source_target_pairs={{0,1},{1,2},{2,3},{3,0},{4,5},{5,6},{6,7},{7,4},{8,9},{9,10},{10,1... | collective-permute-start | bytes 49160 | tf_op jit(solution)/shard_map/ppermute | solution.py:429
  81.3 0.0 collective-permute-start.17
  81.3 0.9 collective-permute-done.16.refs_6_
  82.2 6.2 %collective-permute-done.17.refs_7_ = bf16[64,128]{1,0:T(8,128)(2,1)S(1)} collective-permute-done((bf16[64,128]{1,0:T(8,128)(2,1)S(1)}, bf16[64,128]{1,0:T(8,128)(2,1)S(1)}, u32[]{:S(2)}, u32[]{:S(2)}) %collective-permute-start.17) | collective-permute-done | bytes 16416 | tf_op jit(solution)/shard_map/ppermute | solution.py:429
  88.4 0.3 shard_map.197
  88.7 2.7 %collective-permute-start.18 = (bf16[32,128]{1,0:T(8,128)(2,1)S(1)}, bf16[32,128]{1,0:T(8,128)(2,1)S(1)}, u32[]{:S(2)}, u32[]{:S(2)}) collective-permute-start(bf16[32,128]{1,0:T(8,128)(2,1)S(1)} %get-tuple-element.69), channel_id=1, source_target_pairs={{0,56},{4,60},{8,16},{12,20},{16,8},{20,12},{24,32},{28,36},{32,24... | collective-permute-start | bytes 24584 | tf_op jit(solution)/shard_map/ppermute | solution.py:439
  91.4 3.1 %collective-permute-start.19 = (bf16[32,128]{1,0:T(8,128)(2,1)S(1)}, bf16[32,128]{1,0:T(8,128)(2,1)S(1)}, u32[]{:S(2)}, u32[]{:S(2)}) collective-permute-start(bf16[32,128]{1,0:T(8,128)(2,1)S(1)} %get-tuple-element.70), channel_id=1, source_target_pairs={{0,60},{4,8},{8,4},{12,16},{16,12},{20,24},{24,20},{28,32},{32,28}... | collective-permute-start | bytes 24584 | tf_op jit(solution)/shard_map/ppermute | solution.py:439
  94.5 2.3 %collective-permute-start.20 = (bf16[32,128]{1,0:T(8,128)(2,1)S(1)}, bf16[32,128]{1,0:T(8,128)(2,1)S(1)}, u32[]{:S(2)}, u32[]{:S(2)}) collective-permute-start(bf16[32,128]{1,0:T(8,128)(2,1)S(1)} %get-tuple-element.71), channel_id=1, source_target_pairs={{0,8},{4,12},{8,0},{12,4},{16,24},{20,28},{24,16},{28,20},{32,40},... | collective-permute-start | bytes 24584 | tf_op jit(solution)/shard_map/ppermute | solution.py:439
  96.8 0.0 collective-permute-start.21
  96.8 0.0 collective-permute-done.18.refs_0_
  96.8 1.0 %collective-permute-done.19.refs_1_ = bf16[32,128]{1,0:T(8,128)(2,1)S(1)} collective-permute-done((bf16[32,128]{1,0:T(8,128)(2,1)S(1)}, bf16[32,128]{1,0:T(8,128)(2,1)S(1)}, u32[]{:S(2)}, u32[]{:S(2)}) %collective-permute-start.19) | collective-permute-done | bytes 8224 | tf_op jit(solution)/shard_map/ppermute | solution.py:439
  97.9 0.7 collective-permute-done.20.refs_2_
  98.6 0.8 collective-permute-done.21.refs_3_
  99.3 3.4 %shard_map.198 = f32[1,512]{1,0:T(1,128)} custom-call(bf16[32,128]{1,0:T(8,128)(2,1)S(1)} %collective-permute-done.18.refs_0_, bf16[32,128]{1,0:T(8,128)(2,1)S(1)} %collective-permute-done.19.refs_1_, bf16[32,128]{1,0:T(8,128)(2,1)S(1)} %collective-permute-done.20.refs_2_, bf16[32,128]{1,0:T(8,128)(2,1)S(1)} %collective-permute-done.21.refs_3_, ...), custom_call_target="tpu_custom_call" | custom-call | bytes 1048576 | tf_op jit(solution)/shard_map/pallas_call | solution.py:40
  (16 shorter events, 0.0 us)
Async XLA Ops:
  0.9 5.1 %collective-permute-start = (f32[8,128]{1,0:T(8,128)S(1)}, f32[8,128]{1,0:T(8,128)S(1)}, u32[]{:S(2)}, u32[]{:S(2)}) collective-permute-start(f32[8,128]{1,0:T(8,128)S(1)} %get-tuple-element.42.refs_3_), channel_id=1, source_target_pairs={{0,64},{64,128},{128,192},{192,0},{1,65},{65,129},{129,193},{193,1... | collective-permute-start | bytes 12296 | tf_op jit(solution)/shard_map/ppermute | solution.py:429
  3.0 3.0 %collective-permute-start.1 = (f32[8,128]{1,0:T(8,128)S(1)}, f32[8,128]{1,0:T(8,128)S(1)}, u32[]{:S(2)}, u32[]{:S(2)}) collective-permute-start(f32[8,128]{1,0:T(8,128)S(1)} %get-tuple-element.42.refs_3_), channel_id=1, source_target_pairs={{0,192},{64,0},{128,64},{192,128},{1,193},{65,1},{129,65},{193,129... | collective-permute-start | bytes 12296 | tf_op jit(solution)/shard_map/ppermute | solution.py:429
  6.1 10.4 %collective-permute-start.2 = (f32[8,128]{1,0:T(8,128)S(1)}, f32[8,128]{1,0:T(8,128)S(1)}, u32[]{:S(2)}, u32[]{:S(2)}) collective-permute-start(f32[8,128]{1,0:T(8,128)S(1)} %shard_map.183.refs_7_), channel_id=1, source_target_pairs={{0,4},{4,8},{8,12},{12,16},{16,20},{20,24},{24,28},{28,32},{32,36}... | collective-permute-start | bytes 12296 | tf_op jit(solution)/shard_map/ppermute | solution.py:429
  7.5 9.0 %collective-permute-start.3 = (f32[8,128]{1,0:T(8,128)S(1)}, f32[8,128]{1,0:T(8,128)S(1)}, u32[]{:S(2)}, u32[]{:S(2)}) collective-permute-start(f32[8,128]{1,0:T(8,128)S(1)} %shard_map.183.refs_7_), channel_id=1, source_target_pairs={{0,60},{4,0},{8,4},{12,8},{16,12},{20,16},{24,20},{28,24},{32,28},... | collective-permute-start | bytes 12296 | tf_op jit(solution)/shard_map/ppermute | solution.py:429
  16.7 10.7 %collective-permute-start.4 = (f32[8,128]{1,0:T(8,128)S(1)}, f32[8,128]{1,0:T(8,128)S(1)}, u32[]{:S(2)}, u32[]{:S(2)}) collective-permute-start(f32[8,128]{1,0:T(8,128)S(1)} %shard_map.185.refs_2_), channel_id=1, source_target_pairs={{0,1},{1,2},{2,3},{3,0},{4,5},{5,6},{6,7},{7,4},{8,9},{9,10},{10,1... | collective-permute-start | bytes 12296 | tf_op jit(solution)/shard_map/ppermute | solution.py:429
  24.0 6.9 %collective-permute-start.5 = (f32[8,128]{1,0:T(8,128)S(1)}, f32[8,128]{1,0:T(8,128)S(1)}, u32[]{:S(2)}, u32[]{:S(2)}) collective-permute-start(f32[8,128]{1,0:T(8,128)S(1)} %shard_map.185.refs_2_), channel_id=1, source_target_pairs={{0,3},{1,0},{2,1},{3,2},{4,7},{5,4},{6,5},{7,6},{8,11},{9,8},{10,9... | collective-permute-start | bytes 12296 | tf_op jit(solution)/shard_map/ppermute | solution.py:429
  24.0 6.9 %copy-start.1 = (bf16[512,128]{1,0:T(8,128)(2,1)S(1)}, bf16[512,128]{1,0:T(8,128)(2,1)}, u32[]{:S(2)}) copy-start(bf16[512,128]{1,0:T(8,128)(2,1)} %refs_14_.1) | copy-start | bytes 393220
  24.0 6.9 %copy-start.3 = (bf16[128,128]{1,0:T(8,128)(2,1)S(1)}, bf16[128,128]{1,0:T(8,128)(2,1)}, u32[]{:S(2)}) copy-start(bf16[128,128]{1,0:T(8,128)(2,1)} %refs_13_.1) | copy-start | bytes 98308
  24.0 6.9 %copy-start.4 = (bf16[128,128]{1,0:T(8,128)(2,1)S(1)}, bf16[128,128]{1,0:T(8,128)(2,1)}, u32[]{:S(2)}) copy-start(bf16[128,128]{1,0:T(8,128)(2,1)} %refs_15_.1) | copy-start | bytes 98308
  24.0 6.9 %copy-start.6 = (bf16[8,128]{1,0:T(8,128)(2,1)S(1)}, bf16[8,128]{1,0:T(8,128)(2,1)}, u32[]{:S(2)}) copy-start(bf16[8,128]{1,0:T(8,128)(2,1)} %refs_12_.1) | copy-start | bytes 6148
  36.5 4.0 %collective-permute-start.6 = (bf16[64,128]{1,0:T(8,128)(2,1)S(1)}, bf16[64,128]{1,0:T(8,128)(2,1)S(1)}, u32[]{:S(2)}, u32[]{:S(2)}) collective-permute-start(bf16[64,128]{1,0:T(8,128)(2,1)S(1)} %get-tuple-element.52), channel_id=1, source_target_pairs={{0,64},{64,128},{128,192},{192,0},{1,65},{65,129},{129,193},{193,1... | collective-permute-start | bytes 49160 | tf_op jit(solution)/shard_map/ppermute | solution.py:429
  37.8 2.7 %collective-permute-start.7 = (bf16[64,128]{1,0:T(8,128)(2,1)S(1)}, bf16[64,128]{1,0:T(8,128)(2,1)S(1)}, u32[]{:S(2)}, u32[]{:S(2)}) collective-permute-start(bf16[64,128]{1,0:T(8,128)(2,1)S(1)} %get-tuple-element.53), channel_id=1, source_target_pairs={{0,192},{64,0},{128,64},{192,128},{1,193},{65,1},{129,65},{193,129... | collective-permute-start | bytes 49160 | tf_op jit(solution)/shard_map/ppermute | solution.py:429
  40.7 7.7 %collective-permute-start.8 = (bf16[64,128]{1,0:T(8,128)(2,1)S(1)}, bf16[64,128]{1,0:T(8,128)(2,1)S(1)}, u32[]{:S(2)}, u32[]{:S(2)}) collective-permute-start(bf16[64,128]{1,0:T(8,128)(2,1)S(1)} %get-tuple-element.55.refs_2_), channel_id=1, source_target_pairs={{0,4},{4,8},{8,12},{12,16},{16,20},{20,24},{24,28},{28,32},{32,36}... | collective-permute-start | bytes 49160 | tf_op jit(solution)/shard_map/ppermute | solution.py:429
  40.8 7.6 %collective-permute-start.9 = (bf16[64,128]{1,0:T(8,128)(2,1)S(1)}, bf16[64,128]{1,0:T(8,128)(2,1)S(1)}, u32[]{:S(2)}, u32[]{:S(2)}) collective-permute-start(bf16[64,128]{1,0:T(8,128)(2,1)S(1)} %get-tuple-element.56), channel_id=1, source_target_pairs={{0,60},{4,0},{8,4},{12,8},{16,12},{20,16},{24,20},{28,24},{32,28},... | collective-permute-start | bytes 49160 | tf_op jit(solution)/shard_map/ppermute | solution.py:429
  48.4 4.3 %copy-start.5 = (bf16[4,128,8]{1,2,0:T(8,128)(2,1)S(1)}, bf16[4,128,8]{1,2,0:T(8,128)(2,1)}, u32[]{:S(2)}) copy-start(bf16[4,128,8]{1,2,0:T(8,128)(2,1)} %param.37) | copy-start | bytes 24580
  48.6 5.4 %collective-permute-start.10 = (bf16[64,128]{1,0:T(8,128)(2,1)S(1)}, bf16[64,128]{1,0:T(8,128)(2,1)S(1)}, u32[]{:S(2)}, u32[]{:S(2)}) collective-permute-start(bf16[64,128]{1,0:T(8,128)(2,1)S(1)} %get-tuple-element.57.refs_3_), channel_id=1, source_target_pairs={{0,1},{1,2},{2,3},{3,0},{4,5},{5,6},{6,7},{7,4},{8,9},{9,10},{10,1... | collective-permute-start | bytes 49160 | tf_op jit(solution)/shard_map/ppermute | solution.py:429
  52.7 7.1 %collective-permute-start.11 = (bf16[64,128]{1,0:T(8,128)(2,1)S(1)}, bf16[64,128]{1,0:T(8,128)(2,1)S(1)}, u32[]{:S(2)}, u32[]{:S(2)}) collective-permute-start(bf16[64,128]{1,0:T(8,128)(2,1)S(1)} %get-tuple-element.58), channel_id=1, source_target_pairs={{0,3},{1,0},{2,1},{3,2},{4,7},{5,4},{6,5},{7,6},{8,11},{9,8},{10,9... | collective-permute-start | bytes 49160 | tf_op jit(solution)/shard_map/ppermute | solution.py:429
  59.8 11.1 %copy-start = (f32[1,1,1,3,32,512]{5,4,3,2,1,0:T(8,128)S(1)}, f32[1,1,1,3,32,512]{5,4,3,2,1,0:T(8,128)}, u32[]{:S(2)}) copy-start(f32[1,1,1,3,32,512]{5,4,3,2,1,0:T(8,128)} %param.27) | copy-start | bytes 589828
  59.8 11.1 %copy-start.2 = (s32[1,1,1,32,512]{4,3,2,1,0:T(8,128)S(1)}, s32[1,1,1,32,512]{4,3,2,1,0:T(8,128)}, u32[]{:S(2)}) copy-start(s32[1,1,1,32,512]{4,3,2,1,0:T(8,128)} %param.25) | copy-start | bytes 196612
  59.8 11.1 %copy-start.7 = (s32[1,1,1,512]{3,2,1,0:T(1,128)S(1)}, s32[1,1,1,512]{3,2,1,0:T(1,128)}, u32[]{:S(2)}) copy-start(s32[1,1,1,512]{3,2,1,0:T(1,128)} %param.24) | copy-start | bytes 6148
  59.8 11.1 %copy-start.8 = (s32[1,1,1,512]{3,2,1,0:T(1,128)S(1)}, s32[1,1,1,512]{3,2,1,0:T(1,128)}, u32[]{:S(2)}) copy-start(s32[1,1,1,512]{3,2,1,0:T(1,128)} %param.26) | copy-start | bytes 6148
  68.0 3.9 %collective-permute-start.12 = (bf16[64,128]{1,0:T(8,128)(2,1)S(1)}, bf16[64,128]{1,0:T(8,128)(2,1)S(1)}, u32[]{:S(2)}, u32[]{:S(2)}) collective-permute-start(bf16[64,128]{1,0:T(8,128)(2,1)S(1)} %get-tuple-element.63), channel_id=1, source_target_pairs={{0,64},{64,128},{128,192},{192,0},{1,65},{65,129},{129,193},{193,1... | collective-permute-start | bytes 49160 | tf_op jit(solution)/shard_map/ppermute | solution.py:429
  69.0 2.9 %collective-permute-start.13 = (bf16[64,128]{1,0:T(8,128)(2,1)S(1)}, bf16[64,128]{1,0:T(8,128)(2,1)S(1)}, u32[]{:S(2)}, u32[]{:S(2)}) collective-permute-start(bf16[64,128]{1,0:T(8,128)(2,1)S(1)} %get-tuple-element.64), channel_id=1, source_target_pairs={{0,192},{64,0},{128,64},{192,128},{1,193},{65,1},{129,65},{193,129... | collective-permute-start | bytes 49160 | tf_op jit(solution)/shard_map/ppermute | solution.py:429
  72.2 6.6 %collective-permute-start.14 = (bf16[64,128]{1,0:T(8,128)(2,1)S(1)}, bf16[64,128]{1,0:T(8,128)(2,1)S(1)}, u32[]{:S(2)}, u32[]{:S(2)}) collective-permute-start(bf16[64,128]{1,0:T(8,128)(2,1)S(1)} %get-tuple-element.65), channel_id=1, source_target_pairs={{0,4},{4,8},{8,12},{12,16},{16,20},{20,24},{24,28},{28,32},{32,36}... | collective-permute-start | bytes 49160 | tf_op jit(solution)/shard_map/ppermute | solution.py:429
  72.2 6.5 %collective-permute-start.15 = (bf16[64,128]{1,0:T(8,128)(2,1)S(1)}, bf16[64,128]{1,0:T(8,128)(2,1)S(1)}, u32[]{:S(2)}, u32[]{:S(2)}) collective-permute-start(bf16[64,128]{1,0:T(8,128)(2,1)S(1)} %get-tuple-element.66), channel_id=1, source_target_pairs={{0,60},{4,0},{8,4},{12,8},{16,12},{20,16},{24,20},{28,24},{32,28},... | collective-permute-start | bytes 49160 | tf_op jit(solution)/shard_map/ppermute | solution.py:429
  79.0 3.2 %collective-permute-start.16 = (bf16[64,128]{1,0:T(8,128)(2,1)S(1)}, bf16[64,128]{1,0:T(8,128)(2,1)S(1)}, u32[]{:S(2)}, u32[]{:S(2)}) collective-permute-start(bf16[64,128]{1,0:T(8,128)(2,1)S(1)} %get-tuple-element.67), channel_id=1, source_target_pairs={{0,1},{1,2},{2,3},{3,0},{4,5},{5,6},{6,7},{7,4},{8,9},{9,10},{10,1... | collective-permute-start | bytes 49160 | tf_op jit(solution)/shard_map/ppermute | solution.py:429
  81.3 7.1 %collective-permute-start.17 = (bf16[64,128]{1,0:T(8,128)(2,1)S(1)}, bf16[64,128]{1,0:T(8,128)(2,1)S(1)}, u32[]{:S(2)}, u32[]{:S(2)}) collective-permute-start(bf16[64,128]{1,0:T(8,128)(2,1)S(1)} %get-tuple-element.68), channel_id=1, source_target_pairs={{0,3},{1,0},{2,1},{3,2},{4,7},{5,4},{6,5},{7,6},{8,11},{9,8},{10,9... | collective-permute-start | bytes 49160 | tf_op jit(solution)/shard_map/ppermute | solution.py:429
  88.7 8.1 %collective-permute-start.18 = (bf16[32,128]{1,0:T(8,128)(2,1)S(1)}, bf16[32,128]{1,0:T(8,128)(2,1)S(1)}, u32[]{:S(2)}, u32[]{:S(2)}) collective-permute-start(bf16[32,128]{1,0:T(8,128)(2,1)S(1)} %get-tuple-element.69), channel_id=1, source_target_pairs={{0,56},{4,60},{8,16},{12,20},{16,8},{20,12},{24,32},{28,36},{32,24... | collective-permute-start | bytes 24584 | tf_op jit(solution)/shard_map/ppermute | solution.py:439
  91.4 6.4 %collective-permute-start.19 = (bf16[32,128]{1,0:T(8,128)(2,1)S(1)}, bf16[32,128]{1,0:T(8,128)(2,1)S(1)}, u32[]{:S(2)}, u32[]{:S(2)}) collective-permute-start(bf16[32,128]{1,0:T(8,128)(2,1)S(1)} %get-tuple-element.70), channel_id=1, source_target_pairs={{0,60},{4,8},{8,4},{12,16},{16,12},{20,24},{24,20},{28,32},{32,28}... | collective-permute-start | bytes 24584 | tf_op jit(solution)/shard_map/ppermute | solution.py:439
  94.5 4.0 %collective-permute-start.20 = (bf16[32,128]{1,0:T(8,128)(2,1)S(1)}, bf16[32,128]{1,0:T(8,128)(2,1)S(1)}, u32[]{:S(2)}, u32[]{:S(2)}) collective-permute-start(bf16[32,128]{1,0:T(8,128)(2,1)S(1)} %get-tuple-element.71), channel_id=1, source_target_pairs={{0,8},{4,12},{8,0},{12,4},{16,24},{20,28},{24,16},{28,20},{32,40},... | collective-permute-start | bytes 24584 | tf_op jit(solution)/shard_map/ppermute | solution.py:439
  96.8 2.5 %collective-permute-start.21 = (bf16[32,128]{1,0:T(8,128)(2,1)S(1)}, bf16[32,128]{1,0:T(8,128)(2,1)S(1)}, u32[]{:S(2)}, u32[]{:S(2)}) collective-permute-start(bf16[32,128]{1,0:T(8,128)(2,1)S(1)} %get-tuple-element.72), channel_id=1, source_target_pairs={{0,4},{4,0},{8,12},{12,8},{16,20},{20,16},{24,28},{28,24},{32,36},... | collective-permute-start | bytes 24584 | tf_op jit(solution)/shard_map/ppermute | solution.py:439

commit v5 on v4

--- a/solution.py
+++ b/solution.py
@@ -189,7 +189,7 @@
         radial_ref[g] = dot(hid_ref[first + g], out_ref[...])
         return carry
 
-    lax.fori_loop(0, radial_ref.shape[0], step, 0, unroll=2)
+    lax.fori_loop(0, radial_ref.shape[0], step, 0, unroll=4)
 
 
 def geometry_kernel(
@@ -200,7 +200,8 @@
     weight = by_group(jnp.where(live, 0.25, 0.0))
     vx, vy, vz = (by_group(vec_ref[n]) for n in range(3))
     rows, radius, inverse = harmonics(vx, vy, vz, weight)
-    store_rows(y_ref, rows)
+    coarse = [row.astype(BF16).astype(F32) for row in rows]
+    store_rows(y_ref, coarse + [row - near for row, near in zip(rows, coarse)])
     store_rows(phi_ref, radial_basis(radius, inverse, 5.0))
     where_ref[...] = by_group(index_ref[...].astype(F32)).astype(jnp.int32)
 
@@ -253,8 +254,13 @@
     for degrees, first, last in (((0, 1), 0, 4), ((2, 3), 4, 16)):
         lane = degrees[0] * 128
         weighted = (radial[:, lane : lane + 256] * twice).astype(BF16)
-        angular = [jnp.where(own, spread(y_ref, m * groups + g), 0.0) for m in range(first, last)]
+        angular = [
+            jnp.where(own, spread(y_ref, (m + part) * groups + g), 0.0)
+            for part in (0, 16)
+            for m in range(first, last)
+        ]
         total = dot(jnp.concatenate(angular, axis=0).astype(BF16), weighted)
+        total = total[: 8 * (last - first)] + total[8 * (last - first) :]
         for m in range(first, last):
             side = 0 if m < (degrees[0] + 1) ** 2 else 128
             sums.append(total[8 * (m - first) : 8 * (m - first + 1), side : side + 128])
@@ -487,7 +493,7 @@
     angular, phi, where = call(
         geometry_kernel,
         (
-            shape((2, 16 * slots, 128), F32),
+            shape((2, 32 * slots, 128), F32),
             shape((2, BASIS * slots, 128), F32),
             shape((slots, atoms), jnp.int32),
         ),

time: 103 us -> 102 us (level)
  Pallas kernels: 33.1 us -> 31.2 us
  waiting for transfers between devices: 20.4 us -> 21.7 us
    pallas_call x18, Pallas kernels: 33.1 us -> 31.2 us  [call(): pl.pallas_call(body, out_shape=out_shape, in_specs=[HBM] * first + [VMEM]...]
    ppermute x18, waiting for transfers between devices: 17.9 us -> 19.2 us  [shifted(): lax.ppermute(block, axis, [(i, (i + step) % size) for i in range(size)])]
  transfers between devices with their start and end apart: 22 -> 22, of which waited for: 9 -> 10; matrix products, arithmetic and copies ran while one was open for 0% -> 0% of each run, Pallas kernels for 13% -> 11%
where the time goes in v5:
time: 102 us
  starting transfers between devices  48.6 us (48%)
  Pallas kernels  31.2 us (31%)
  waiting for transfers between devices  21.7 us (21%)
    ppermute x18, starting transfers between devices, shifted(): lax.ppermute(block, axis, [(i, (i + step) % size) for i in range(size)])  40.4 us
    pallas_call x18, Pallas kernels, call(): pl.pallas_call(body, out_shape=out_shape, in_specs=[HBM] * first + [VMEM]...  31.2 us
    ppermute x18, waiting for transfers between devices, shifted(): lax.ppermute(block, axis, [(i, (i + step) % size) for i in range(size)])  19.2 us
    ppermute x4, starting transfers between devices, swapped_with(): return lax.ppermute(block, 'gy', sorted(pairs))  8.16 us
    ppermute x4, waiting for transfers between devices, swapped_with(): return lax.ppermute(block, 'gy', sorted(pairs))  2.5 us
  transfers between devices with their start and end apart: 22, of which 10 were waited for; matrix products, arithmetic and copies ran while one was open for 0% of the time, Pallas kernels for 11%

profile of v5, /device:TPU:1, one launch (start us, length us, event | category | flops | bytes accessed | tf_op | source)
XLA Modules:
  0.0 101.7 jit_solution(3333308494157910756)
XLA Ops:
  0.0 0.8 shard_map.181
  0.9 2.1 %collective-permute-start = (f32[8,128]{1,0:T(8,128)S(1)}, f32[8,128]{1,0:T(8,128)S(1)}, u32[]{:S(2)}, u32[]{:S(2)}) collective-permute-start(f32[8,128]{1,0:T(8,128)S(1)} %get-tuple-element.42.refs_3_), channel_id=1, source_target_pairs={{0,64},{64,128},{128,192},{192,0},{1,65},{65,129},{129,193},{193,1... | collective-permute-start | bytes 12296 | tf_op jit(solution)/shard_map/ppermute | solution.py:435
  3.0 1.4 %collective-permute-start.1 = (f32[8,128]{1,0:T(8,128)S(1)}, f32[8,128]{1,0:T(8,128)S(1)}, u32[]{:S(2)}, u32[]{:S(2)}) collective-permute-start(f32[8,128]{1,0:T(8,128)S(1)} %get-tuple-element.42.refs_3_), channel_id=1, source_target_pairs={{0,192},{64,0},{128,64},{192,128},{1,193},{65,1},{129,65},{193,129... | collective-permute-start | bytes 12296 | tf_op jit(solution)/shard_map/ppermute | solution.py:435
  4.3 1.7 %shard_map.182 = (f32[2,1024,128]{2,1,0:T(8,128)S(1)}, f32[2,256,128]{2,1,0:T(8,128)S(1)}, s32[32,256]{1,0:T(8,128)S(1)}) custom-call(f32[3,32,256]{2,1,0:T(8,128)} %bitcast.16, s32[1,256]{1,0:T(1,128)} %bitcast.19, s32[32,256]{1,0:T(8,128)} %bitcast.17, f32[8,128]{1,0:T(8,128)S(1)} %get-tuple-element.42.refs_3_), custom_call_target="tpu_custom_call" | custom-call | bytes 1048576 | tf_op jit(solution)/shard_map/pallas_call | solution.py:40
  6.0 0.0 collective-permute-done.refs_2_.refs_1_
  6.1 0.0 collective-permute-done.1.refs_3_.refs_2_
  6.1 0.1 shard_map.183.refs_7_
  6.2 1.4 %collective-permute-start.2 = (f32[8,128]{1,0:T(8,128)S(1)}, f32[8,128]{1,0:T(8,128)S(1)}, u32[]{:S(2)}, u32[]{:S(2)}) collective-permute-start(f32[8,128]{1,0:T(8,128)S(1)} %shard_map.183.refs_7_), channel_id=1, source_target_pairs={{0,4},{4,8},{8,12},{12,16},{16,20},{20,24},{24,28},{28,32},{32,36}... | collective-permute-start | bytes 12296 | tf_op jit(solution)/shard_map/ppermute | solution.py:435
  7.6 5.6 %collective-permute-start.3 = (f32[8,128]{1,0:T(8,128)S(1)}, f32[8,128]{1,0:T(8,128)S(1)}, u32[]{:S(2)}, u32[]{:S(2)}) collective-permute-start(f32[8,128]{1,0:T(8,128)S(1)} %shard_map.183.refs_7_), channel_id=1, source_target_pairs={{0,60},{4,0},{8,4},{12,8},{16,12},{20,16},{24,20},{28,24},{32,28},... | collective-permute-start | bytes 12296 | tf_op jit(solution)/shard_map/ppermute | solution.py:435
  13.2 3.1 %shard_map.184 = (bf16[32,256,128]{2,1,0:T(8,128)(2,1)S(1)}, bf16[8,128]{1,0:T(8,128)(2,1)S(1)}, bf16[128,512]{1,0:T(8,128)(2,1)S(1)}, bf16[128,512]{1,0:T(8,128)(2,1)S(1)}, f32[8,256,512]{2,1,0:T(8,128)S(1)}) custom-call(bf16[8,64]{1,0:T(8,128)(2,1)} %refs_0_.1, bf16[8,64]{1,0:T(8,128)(2,1)} %refs_1_.1, bf16[64,512]{1,0:T(8,128)(2,1)} %refs_2_.1, ...), custom_call_target="tpu_custom_call" | custom-call | bytes 1048576 | tf_op jit(solution)/shard_map/pallas_call | solution.py:40
  16.3 0.0 collective-permute-done.2.refs_4_.refs_3_
  16.3 0.0 collective-permute-done.3.refs_5_.refs_4_
  16.4 0.1 shard_map.185.refs_2_
  16.5 7.2 %collective-permute-start.4 = (f32[8,128]{1,0:T(8,128)S(1)}, f32[8,128]{1,0:T(8,128)S(1)}, u32[]{:S(2)}, u32[]{:S(2)}) collective-permute-start(f32[8,128]{1,0:T(8,128)S(1)} %shard_map.185.refs_2_), channel_id=1, source_target_pairs={{0,1},{1,2},{2,3},{3,0},{4,5},{5,6},{6,7},{7,4},{8,9},{9,10},{10,1... | collective-permute-start | bytes 12296 | tf_op jit(solution)/shard_map/ppermute | solution.py:435
  23.7 0.0 collective-permute-start.5
  23.7 0.0 copy-start.6
  23.7 2.5 %shard_map.186.refs_10_ = f32[24,256,512]{2,1,0:T(8,128)S(1)} custom-call(bf16[32,256,128]{2,1,0:T(8,128)(2,1)S(1)} %get-tuple-element.48.refs_0_, bf16[128,512]{1,0:T(8,128)(2,1)S(1)} %get-tuple-element.49.refs_1_, f32[8,128]{1,0:T(8,128)S(1)} %shard_map.185.refs_2_), custom_call_target="tpu_custom_call" | custom-call | bytes 1048576 | tf_op jit(solution)/shard_map/pallas_call | solution.py:40
  26.3 0.0 collective-permute-done.4.refs_5_
  26.3 4.4 %collective-permute-done.5.refs_6_ = f32[8,128]{1,0:T(8,128)S(1)} collective-permute-done((f32[8,128]{1,0:T(8,128)S(1)}, f32[8,128]{1,0:T(8,128)S(1)}, u32[]{:S(2)}, u32[]{:S(2)}) %collective-permute-start.5) | collective-permute-done | bytes 4128 | tf_op jit(solution)/shard_map/ppermute | solution.py:435
  30.7 5.7 %shard_map.187 = (bf16[256,128]{1,0:T(8,128)(2,1)S(1)}, bf16[64,128]{1,0:T(8,128)(2,1)S(1)}, bf16[64,128]{1,0:T(8,128)(2,1)S(1)}) custom-call(s32[1,256]{1,0:T(1,128)S(1)} %get-tuple-element.41.refs_0_, f32[8,128]{1,0:T(8,128)S(1)} %collective-permute-done.refs_2_.refs_1_, f32[8,128]{1,0:T(8,128)S(1)} %collective-permute-done.1.refs_3_.refs_2_, ...), custom_call_target="tpu_custom_call" | custom-call | bytes 1048576 | tf_op jit(solution)/shard_map/pallas_call | solution.py:40
  36.4 1.3 %collective-permute-start.6 = (bf16[64,128]{1,0:T(8,128)(2,1)S(1)}, bf16[64,128]{1,0:T(8,128)(2,1)S(1)}, u32[]{:S(2)}, u32[]{:S(2)}) collective-permute-start(bf16[64,128]{1,0:T(8,128)(2,1)S(1)} %get-tuple-element.52), channel_id=1, source_target_pairs={{0,64},{64,128},{128,192},{192,0},{1,65},{65,129},{129,193},{193,1... | collective-permute-start | bytes 49160 | tf_op jit(solution)/shard_map/ppermute | solution.py:435
  37.7 1.6 %collective-permute-start.7 = (bf16[64,128]{1,0:T(8,128)(2,1)S(1)}, bf16[64,128]{1,0:T(8,128)(2,1)S(1)}, u32[]{:S(2)}, u32[]{:S(2)}) collective-permute-start(bf16[64,128]{1,0:T(8,128)(2,1)S(1)} %get-tuple-element.53), channel_id=1, source_target_pairs={{0,192},{64,0},{128,64},{192,128},{1,193},{65,1},{129,65},{193,129... | collective-permute-start | bytes 49160 | tf_op jit(solution)/shard_map/ppermute | solution.py:435
  39.2 0.8 shard_map.188.refs_4_.refs_9_
  40.1 0.2 collective-permute-done.6.refs_2_.refs_1_
  40.3 0.0 collective-permute-done.7.refs_3_.refs_2_
  40.3 0.2 shard_map.189
  40.5 0.3 collective-permute-start.8
  40.7 5.4 %collective-permute-start.9 = (bf16[64,128]{1,0:T(8,128)(2,1)S(1)}, bf16[64,128]{1,0:T(8,128)(2,1)S(1)}, u32[]{:S(2)}, u32[]{:S(2)}) collective-permute-start(bf16[64,128]{1,0:T(8,128)(2,1)S(1)} %get-tuple-element.56), channel_id=1, source_target_pairs={{0,60},{4,0},{8,4},{12,8},{16,12},{20,16},{24,20},{28,24},{32,28},... | collective-permute-start | bytes 49160 | tf_op jit(solution)/shard_map/ppermute | solution.py:435
  46.1 1.7 %shard_map.190.refs_6_.refs_10_ = f32[16,256,512]{2,1,0:T(8,128)S(1)} custom-call(bf16[32,256,128]{2,1,0:T(8,128)(2,1)S(1)} %get-tuple-element.48.refs_0_, bf16[128,512]{1,0:T(8,128)(2,1)S(1)} %get-tuple-element.54.refs_1_, bf16[64,128]{1,0:T(8,128)(2,1)S(1)} %get-tuple-element.55.refs_2_), custom_call_target="tpu_custom_call" | custom-call | bytes 1048576 | tf_op jit(solution)/shard_map/pallas_call | solution.py:40
  47.8 0.0 copy-start.5
  47.8 0.0 collective-permute-done.8.refs_4_.refs_3_
  47.8 0.0 collective-permute-done.9.refs_5_.refs_4_
  47.8 0.2 shard_map.191
  48.1 3.3 %collective-permute-start.10 = (bf16[64,128]{1,0:T(8,128)(2,1)S(1)}, bf16[64,128]{1,0:T(8,128)(2,1)S(1)}, u32[]{:S(2)}, u32[]{:S(2)}) collective-permute-start(bf16[64,128]{1,0:T(8,128)(2,1)S(1)} %get-tuple-element.57.refs_3_), channel_id=1, source_target_pairs={{0,1},{1,2},{2,3},{3,0},{4,5},{5,6},{6,7},{7,4},{8,9},{9,10},{10,1... | collective-permute-start | bytes 49160 | tf_op jit(solution)/shard_map/ppermute | solution.py:435
  51.4 0.0 collective-permute-start.11
  51.4 1.1 %shard_map.192 = (f32[8,256,512]{2,1,0:T(8,128)S(1)}, bf16[2048,128]{1,0:T(8,128)(2,1)S(1)}) custom-call(bf16[32,256,128]{2,1,0:T(8,128)(2,1)S(1)} %get-tuple-element.48.refs_0_, bf16[128,512]{1,0:T(8,128)(2,1)S(1)} %get-tuple-element.54.refs_1_, bf16[4,8,128]{2,1,0:T(8,128)(2,1)S(1)} %bitcast.13, bf16[64,128]{1,0:T(8,128)(2,1)S(1)} %get-tuple-element.57.refs_3_), custom_call_target="tpu_custom_call" | custom-call | bytes 1048576 | tf_op jit(solution)/shard_map/pallas_call | solution.py:40
  52.5 0.0 collective-permute-done.10.refs_5_
  52.5 6.0 %collective-permute-done.11.refs_6_ = bf16[64,128]{1,0:T(8,128)(2,1)S(1)} collective-permute-done((bf16[64,128]{1,0:T(8,128)(2,1)S(1)}, bf16[64,128]{1,0:T(8,128)(2,1)S(1)}, u32[]{:S(2)}, u32[]{:S(2)}) %collective-permute-start.11) | collective-permute-done | bytes 16416 | tf_op jit(solution)/shard_map/ppermute | solution.py:435
  58.5 8.2 %shard_map.193 = (bf16[256,128]{1,0:T(8,128)(2,1)S(1)}, bf16[64,128]{1,0:T(8,128)(2,1)S(1)}, bf16[64,128]{1,0:T(8,128)(2,1)S(1)}) custom-call(bf16[256,128]{1,0:T(8,128)(2,1)S(1)} %get-tuple-element.51.refs_2_.refs_1_.refs_0_, bf16[64,128]{1,0:T(8,128)(2,1)S(1)} %collective-permute-done.6.refs_2_.refs_1_, ...), custom_call_target="tpu_custom_call" | custom-call | bytes 1048576 | tf_op jit(solution)/shard_map/pallas_call | solution.py:40
  66.7 1.0 collective-permute-start.12
  67.7 1.8 %collective-permute-start.13 = (bf16[64,128]{1,0:T(8,128)(2,1)S(1)}, bf16[64,128]{1,0:T(8,128)(2,1)S(1)}, u32[]{:S(2)}, u32[]{:S(2)}) collective-permute-start(bf16[64,128]{1,0:T(8,128)(2,1)S(1)} %get-tuple-element.64), channel_id=1, source_target_pairs={{0,192},{64,0},{128,64},{192,128},{1,193},{65,1},{129,65},{193,129... | collective-permute-start | bytes 49160 | tf_op jit(solution)/shard_map/ppermute | solution.py:435
  69.5 0.6 shard_map.194
  70.1 0.5 collective-permute-done.12.refs_2_
  70.6 0.0 collective-permute-done.13.refs_3_
  70.6 0.2 shard_map.195
  70.8 0.1 collective-permute-start.14
  70.9 5.7 %collective-permute-start.15 = (bf16[64,128]{1,0:T(8,128)(2,1)S(1)}, bf16[64,128]{1,0:T(8,128)(2,1)S(1)}, u32[]{:S(2)}, u32[]{:S(2)}) collective-permute-start(bf16[64,128]{1,0:T(8,128)(2,1)S(1)} %get-tuple-element.66), channel_id=1, source_target_pairs={{0,60},{4,0},{8,4},{12,8},{16,12},{20,16},{24,20},{28,24},{32,28},... | collective-permute-start | bytes 49160 | tf_op jit(solution)/shard_map/ppermute | solution.py:435
  76.6 1.0 %collective-permute-done.14.refs_4_ = bf16[64,128]{1,0:T(8,128)(2,1)S(1)} collective-permute-done((bf16[64,128]{1,0:T(8,128)(2,1)S(1)}, bf16[64,128]{1,0:T(8,128)(2,1)S(1)}, u32[]{:S(2)}, u32[]{:S(2)}) %collective-permute-start.14) | collective-permute-done | bytes 16416 | tf_op jit(solution)/shard_map/ppermute | solution.py:435
  77.7 0.0 collective-permute-done.15.refs_5_
  77.7 0.2 shard_map.196
  77.9 2.3 %collective-permute-start.16 = (bf16[64,128]{1,0:T(8,128)(2,1)S(1)}, bf16[64,128]{1,0:T(8,128)(2,1)S(1)}, u32[]{:S(2)}, u32[]{:S(2)}) collective-permute-start(bf16[64,128]{1,0:T(8,128)(2,1)S(1)} %get-tuple-element.67), channel_id=1, source_target_pairs={{0,1},{1,2},{2,3},{3,0},{4,5},{5,6},{6,7},{7,4},{8,9},{9,10},{10,1... | collective-permute-start | bytes 49160 | tf_op jit(solution)/shard_map/ppermute | solution.py:435
  80.2 0.0 collective-permute-start.17
  80.2 0.9 collective-permute-done.16.refs_6_
  81.1 6.2 %collective-permute-done.17.refs_7_ = bf16[64,128]{1,0:T(8,128)(2,1)S(1)} collective-permute-done((bf16[64,128]{1,0:T(8,128)(2,1)S(1)}, bf16[64,128]{1,0:T(8,128)(2,1)S(1)}, u32[]{:S(2)}, u32[]{:S(2)}) %collective-permute-start.17) | collective-permute-done | bytes 16416 | tf_op jit(solution)/shard_map/ppermute | solution.py:435
  87.3 0.3 shard_map.197
  87.6 3.3 %collective-permute-start.18 = (bf16[32,128]{1,0:T(8,128)(2,1)S(1)}, bf16[32,128]{1,0:T(8,128)(2,1)S(1)}, u32[]{:S(2)}, u32[]{:S(2)}) collective-permute-start(bf16[32,128]{1,0:T(8,128)(2,1)S(1)} %get-tuple-element.69), channel_id=1, source_target_pairs={{0,56},{4,60},{8,16},{12,20},{16,8},{20,12},{24,32},{28,36},{32,24... | collective-permute-start | bytes 24584 | tf_op jit(solution)/shard_map/ppermute | solution.py:445
  90.9 2.6 %collective-permute-start.19 = (bf16[32,128]{1,0:T(8,128)(2,1)S(1)}, bf16[32,128]{1,0:T(8,128)(2,1)S(1)}, u32[]{:S(2)}, u32[]{:S(2)}) collective-permute-start(bf16[32,128]{1,0:T(8,128)(2,1)S(1)} %get-tuple-element.70), channel_id=1, source_target_pairs={{0,60},{4,8},{8,4},{12,16},{16,12},{20,24},{24,20},{28,32},{32,28}... | collective-permute-start | bytes 24584 | tf_op jit(solution)/shard_map/ppermute | solution.py:445
  93.5 2.3 %collective-permute-start.20 = (bf16[32,128]{1,0:T(8,128)(2,1)S(1)}, bf16[32,128]{1,0:T(8,128)(2,1)S(1)}, u32[]{:S(2)}, u32[]{:S(2)}) collective-permute-start(bf16[32,128]{1,0:T(8,128)(2,1)S(1)} %get-tuple-element.71), channel_id=1, source_target_pairs={{0,8},{4,12},{8,0},{12,4},{16,24},{20,28},{24,16},{28,20},{32,40},... | collective-permute-start | bytes 24584 | tf_op jit(solution)/shard_map/ppermute | solution.py:445
  95.8 0.0 collective-permute-start.21
  95.8 0.0 collective-permute-done.18.refs_0_
  95.8 1.5 %collective-permute-done.19.refs_1_ = bf16[32,128]{1,0:T(8,128)(2,1)S(1)} collective-permute-done((bf16[32,128]{1,0:T(8,128)(2,1)S(1)}, bf16[32,128]{1,0:T(8,128)(2,1)S(1)}, u32[]{:S(2)}, u32[]{:S(2)}) %collective-permute-start.19) | collective-permute-done | bytes 8224 | tf_op jit(solution)/shard_map/ppermute | solution.py:445
  97.3 0.2 collective-permute-done.20.refs_2_
  97.5 0.8 collective-permute-done.21.refs_3_
  98.3 3.4 %shard_map.198 = f32[1,512]{1,0:T(1,128)} custom-call(bf16[32,128]{1,0:T(8,128)(2,1)S(1)} %collective-permute-done.18.refs_0_, bf16[32,128]{1,0:T(8,128)(2,1)S(1)} %collective-permute-done.19.refs_1_, bf16[32,128]{1,0:T(8,128)(2,1)S(1)} %collective-permute-done.20.refs_2_, bf16[32,128]{1,0:T(8,128)(2,1)S(1)} %collective-permute-done.21.refs_3_, ...), custom_call_target="tpu_custom_call" | custom-call | bytes 1048576 | tf_op jit(solution)/shard_map/pallas_call | solution.py:40
  (16 shorter events, 0.0 us)
Async XLA Ops:
  0.9 5.2 %collective-permute-start = (f32[8,128]{1,0:T(8,128)S(1)}, f32[8,128]{1,0:T(8,128)S(1)}, u32[]{:S(2)}, u32[]{:S(2)}) collective-permute-start(f32[8,128]{1,0:T(8,128)S(1)} %get-tuple-element.42.refs_3_), channel_id=1, source_target_pairs={{0,64},{64,128},{128,192},{192,0},{1,65},{65,129},{129,193},{193,1... | collective-permute-start | bytes 12296 | tf_op jit(solution)/shard_map/ppermute | solution.py:435
  3.0 3.1 %collective-permute-start.1 = (f32[8,128]{1,0:T(8,128)S(1)}, f32[8,128]{1,0:T(8,128)S(1)}, u32[]{:S(2)}, u32[]{:S(2)}) collective-permute-start(f32[8,128]{1,0:T(8,128)S(1)} %get-tuple-element.42.refs_3_), channel_id=1, source_target_pairs={{0,192},{64,0},{128,64},{192,128},{1,193},{65,1},{129,65},{193,129... | collective-permute-start | bytes 12296 | tf_op jit(solution)/shard_map/ppermute | solution.py:435
  6.2 10.1 %collective-permute-start.2 = (f32[8,128]{1,0:T(8,128)S(1)}, f32[8,128]{1,0:T(8,128)S(1)}, u32[]{:S(2)}, u32[]{:S(2)}) collective-permute-start(f32[8,128]{1,0:T(8,128)S(1)} %shard_map.183.refs_7_), channel_id=1, source_target_pairs={{0,4},{4,8},{8,12},{12,16},{16,20},{20,24},{24,28},{28,32},{32,36}... | collective-permute-start | bytes 12296 | tf_op jit(solution)/shard_map/ppermute | solution.py:435
  7.6 8.7 %collective-permute-start.3 = (f32[8,128]{1,0:T(8,128)S(1)}, f32[8,128]{1,0:T(8,128)S(1)}, u32[]{:S(2)}, u32[]{:S(2)}) collective-permute-start(f32[8,128]{1,0:T(8,128)S(1)} %shard_map.183.refs_7_), channel_id=1, source_target_pairs={{0,60},{4,0},{8,4},{12,8},{16,12},{20,16},{24,20},{28,24},{32,28},... | collective-permute-start | bytes 12296 | tf_op jit(solution)/shard_map/ppermute | solution.py:435
  16.5 9.8 %collective-permute-start.4 = (f32[8,128]{1,0:T(8,128)S(1)}, f32[8,128]{1,0:T(8,128)S(1)}, u32[]{:S(2)}, u32[]{:S(2)}) collective-permute-start(f32[8,128]{1,0:T(8,128)S(1)} %shard_map.185.refs_2_), channel_id=1, source_target_pairs={{0,1},{1,2},{2,3},{3,0},{4,5},{5,6},{6,7},{7,4},{8,9},{9,10},{10,1... | collective-permute-start | bytes 12296 | tf_op jit(solution)/shard_map/ppermute | solution.py:435
  23.7 6.9 %collective-permute-start.5 = (f32[8,128]{1,0:T(8,128)S(1)}, f32[8,128]{1,0:T(8,128)S(1)}, u32[]{:S(2)}, u32[]{:S(2)}) collective-permute-start(f32[8,128]{1,0:T(8,128)S(1)} %shard_map.185.refs_2_), channel_id=1, source_target_pairs={{0,3},{1,0},{2,1},{3,2},{4,7},{5,4},{6,5},{7,6},{8,11},{9,8},{10,9... | collective-permute-start | bytes 12296 | tf_op jit(solution)/shard_map/ppermute | solution.py:435
  23.7 6.9 %copy-start.1 = (bf16[512,128]{1,0:T(8,128)(2,1)S(1)}, bf16[512,128]{1,0:T(8,128)(2,1)}, u32[]{:S(2)}) copy-start(bf16[512,128]{1,0:T(8,128)(2,1)} %refs_14_.1) | copy-start | bytes 393220
  23.7 6.9 %copy-start.3 = (bf16[128,128]{1,0:T(8,128)(2,1)S(1)}, bf16[128,128]{1,0:T(8,128)(2,1)}, u32[]{:S(2)}) copy-start(bf16[128,128]{1,0:T(8,128)(2,1)} %refs_13_.1) | copy-start | bytes 98308
  23.7 6.9 %copy-start.4 = (bf16[128,128]{1,0:T(8,128)(2,1)S(1)}, bf16[128,128]{1,0:T(8,128)(2,1)}, u32[]{:S(2)}) copy-start(bf16[128,128]{1,0:T(8,128)(2,1)} %refs_15_.1) | copy-start | bytes 98308
  23.7 6.9 %copy-start.6 = (bf16[8,128]{1,0:T(8,128)(2,1)S(1)}, bf16[8,128]{1,0:T(8,128)(2,1)}, u32[]{:S(2)}) copy-start(bf16[8,128]{1,0:T(8,128)(2,1)} %refs_12_.1) | copy-start | bytes 6148
  36.4 3.9 %collective-permute-start.6 = (bf16[64,128]{1,0:T(8,128)(2,1)S(1)}, bf16[64,128]{1,0:T(8,128)(2,1)S(1)}, u32[]{:S(2)}, u32[]{:S(2)}) collective-permute-start(bf16[64,128]{1,0:T(8,128)(2,1)S(1)} %get-tuple-element.52), channel_id=1, source_target_pairs={{0,64},{64,128},{128,192},{192,0},{1,65},{65,129},{129,193},{193,1... | collective-permute-start | bytes 49160 | tf_op jit(solution)/shard_map/ppermute | solution.py:435
  37.7 2.6 %collective-permute-start.7 = (bf16[64,128]{1,0:T(8,128)(2,1)S(1)}, bf16[64,128]{1,0:T(8,128)(2,1)S(1)}, u32[]{:S(2)}, u32[]{:S(2)}) collective-permute-start(bf16[64,128]{1,0:T(8,128)(2,1)S(1)} %get-tuple-element.53), channel_id=1, source_target_pairs={{0,192},{64,0},{128,64},{192,128},{1,193},{65,1},{129,65},{193,129... | collective-permute-start | bytes 49160 | tf_op jit(solution)/shard_map/ppermute | solution.py:435
  40.5 7.3 %collective-permute-start.8 = (bf16[64,128]{1,0:T(8,128)(2,1)S(1)}, bf16[64,128]{1,0:T(8,128)(2,1)S(1)}, u32[]{:S(2)}, u32[]{:S(2)}) collective-permute-start(bf16[64,128]{1,0:T(8,128)(2,1)S(1)} %get-tuple-element.55.refs_2_), channel_id=1, source_target_pairs={{0,4},{4,8},{8,12},{12,16},{16,20},{20,24},{24,28},{28,32},{32,36}... | collective-permute-start | bytes 49160 | tf_op jit(solution)/shard_map/ppermute | solution.py:435
  40.7 7.1 %collective-permute-start.9 = (bf16[64,128]{1,0:T(8,128)(2,1)S(1)}, bf16[64,128]{1,0:T(8,128)(2,1)S(1)}, u32[]{:S(2)}, u32[]{:S(2)}) collective-permute-start(bf16[64,128]{1,0:T(8,128)(2,1)S(1)} %get-tuple-element.56), channel_id=1, source_target_pairs={{0,60},{4,0},{8,4},{12,8},{16,12},{20,16},{24,20},{28,24},{32,28},... | collective-permute-start | bytes 49160 | tf_op jit(solution)/shard_map/ppermute | solution.py:435
  47.8 3.6 %copy-start.5 = (bf16[4,128,8]{1,2,0:T(8,128)(2,1)S(1)}, bf16[4,128,8]{1,2,0:T(8,128)(2,1)}, u32[]{:S(2)}) copy-start(bf16[4,128,8]{1,2,0:T(8,128)(2,1)} %param.37) | copy-start | bytes 24580
  48.1 4.4 %collective-permute-start.10 = (bf16[64,128]{1,0:T(8,128)(2,1)S(1)}, bf16[64,128]{1,0:T(8,128)(2,1)S(1)}, u32[]{:S(2)}, u32[]{:S(2)}) collective-permute-start(bf16[64,128]{1,0:T(8,128)(2,1)S(1)} %get-tuple-element.57.refs_3_), channel_id=1, source_target_pairs={{0,1},{1,2},{2,3},{3,0},{4,5},{5,6},{6,7},{7,4},{8,9},{9,10},{10,1... | collective-permute-start | bytes 49160 | tf_op jit(solution)/shard_map/ppermute | solution.py:435
  51.4 7.1 %collective-permute-start.11 = (bf16[64,128]{1,0:T(8,128)(2,1)S(1)}, bf16[64,128]{1,0:T(8,128)(2,1)S(1)}, u32[]{:S(2)}, u32[]{:S(2)}) collective-permute-start(bf16[64,128]{1,0:T(8,128)(2,1)S(1)} %get-tuple-element.58), channel_id=1, source_target_pairs={{0,3},{1,0},{2,1},{3,2},{4,7},{5,4},{6,5},{7,6},{8,11},{9,8},{10,9... | collective-permute-start | bytes 49160 | tf_op jit(solution)/shard_map/ppermute | solution.py:435
  58.5 11.0 %copy-start = (f32[1,1,1,3,32,512]{5,4,3,2,1,0:T(8,128)S(1)}, f32[1,1,1,3,32,512]{5,4,3,2,1,0:T(8,128)}, u32[]{:S(2)}) copy-start(f32[1,1,1,3,32,512]{5,4,3,2,1,0:T(8,128)} %param.27) | copy-start | bytes 589828
  58.5 11.0 %copy-start.2 = (s32[1,1,1,32,512]{4,3,2,1,0:T(8,128)S(1)}, s32[1,1,1,32,512]{4,3,2,1,0:T(8,128)}, u32[]{:S(2)}) copy-start(s32[1,1,1,32,512]{4,3,2,1,0:T(8,128)} %param.25) | copy-start | bytes 196612
  58.5 11.0 %copy-start.7 = (s32[1,1,1,512]{3,2,1,0:T(1,128)S(1)}, s32[1,1,1,512]{3,2,1,0:T(1,128)}, u32[]{:S(2)}) copy-start(s32[1,1,1,512]{3,2,1,0:T(1,128)} %param.24) | copy-start | bytes 6148
  58.5 11.0 %copy-start.8 = (s32[1,1,1,512]{3,2,1,0:T(1,128)S(1)}, s32[1,1,1,512]{3,2,1,0:T(1,128)}, u32[]{:S(2)}) copy-start(s32[1,1,1,512]{3,2,1,0:T(1,128)} %param.26) | copy-start | bytes 6148
  66.7 3.9 %collective-permute-start.12 = (bf16[64,128]{1,0:T(8,128)(2,1)S(1)}, bf16[64,128]{1,0:T(8,128)(2,1)S(1)}, u32[]{:S(2)}, u32[]{:S(2)}) collective-permute-start(bf16[64,128]{1,0:T(8,128)(2,1)S(1)} %get-tuple-element.63), channel_id=1, source_target_pairs={{0,64},{64,128},{128,192},{192,0},{1,65},{65,129},{129,193},{193,1... | collective-permute-start | bytes 49160 | tf_op jit(solution)/shard_map/ppermute | solution.py:435
  67.7 2.9 %collective-permute-start.13 = (bf16[64,128]{1,0:T(8,128)(2,1)S(1)}, bf16[64,128]{1,0:T(8,128)(2,1)S(1)}, u32[]{:S(2)}, u32[]{:S(2)}) collective-permute-start(bf16[64,128]{1,0:T(8,128)(2,1)S(1)} %get-tuple-element.64), channel_id=1, source_target_pairs={{0,192},{64,0},{128,64},{192,128},{1,193},{65,1},{129,65},{193,129... | collective-permute-start | bytes 49160 | tf_op jit(solution)/shard_map/ppermute | solution.py:435
  70.8 6.8 %collective-permute-start.14 = (bf16[64,128]{1,0:T(8,128)(2,1)S(1)}, bf16[64,128]{1,0:T(8,128)(2,1)S(1)}, u32[]{:S(2)}, u32[]{:S(2)}) collective-permute-start(bf16[64,128]{1,0:T(8,128)(2,1)S(1)} %get-tuple-element.65), channel_id=1, source_target_pairs={{0,4},{4,8},{8,12},{12,16},{16,20},{20,24},{24,28},{28,32},{32,36}... | collective-permute-start | bytes 49160 | tf_op jit(solution)/shard_map/ppermute | solution.py:435
  70.9 6.8 %collective-permute-start.15 = (bf16[64,128]{1,0:T(8,128)(2,1)S(1)}, bf16[64,128]{1,0:T(8,128)(2,1)S(1)}, u32[]{:S(2)}, u32[]{:S(2)}) collective-permute-start(bf16[64,128]{1,0:T(8,128)(2,1)S(1)} %get-tuple-element.66), channel_id=1, source_target_pairs={{0,60},{4,0},{8,4},{12,8},{16,12},{20,16},{24,20},{28,24},{32,28},... | collective-permute-start | bytes 49160 | tf_op jit(solution)/shard_map/ppermute | solution.py:435
  77.9 3.2 %collective-permute-start.16 = (bf16[64,128]{1,0:T(8,128)(2,1)S(1)}, bf16[64,128]{1,0:T(8,128)(2,1)S(1)}, u32[]{:S(2)}, u32[]{:S(2)}) collective-permute-start(bf16[64,128]{1,0:T(8,128)(2,1)S(1)} %get-tuple-element.67), channel_id=1, source_target_pairs={{0,1},{1,2},{2,3},{3,0},{4,5},{5,6},{6,7},{7,4},{8,9},{9,10},{10,1... | collective-permute-start | bytes 49160 | tf_op jit(solution)/shard_map/ppermute | solution.py:435
  80.2 7.1 %collective-permute-start.17 = (bf16[64,128]{1,0:T(8,128)(2,1)S(1)}, bf16[64,128]{1,0:T(8,128)(2,1)S(1)}, u32[]{:S(2)}, u32[]{:S(2)}) collective-permute-start(bf16[64,128]{1,0:T(8,128)(2,1)S(1)} %get-tuple-element.68), channel_id=1, source_target_pairs={{0,3},{1,0},{2,1},{3,2},{4,7},{5,4},{6,5},{7,6},{8,11},{9,8},{10,9... | collective-permute-start | bytes 49160 | tf_op jit(solution)/shard_map/ppermute | solution.py:435
  87.6 8.2 %collective-permute-start.18 = (bf16[32,128]{1,0:T(8,128)(2,1)S(1)}, bf16[32,128]{1,0:T(8,128)(2,1)S(1)}, u32[]{:S(2)}, u32[]{:S(2)}) collective-permute-start(bf16[32,128]{1,0:T(8,128)(2,1)S(1)} %get-tuple-element.69), channel_id=1, source_target_pairs={{0,56},{4,60},{8,16},{12,20},{16,8},{20,12},{24,32},{28,36},{32,24... | collective-permute-start | bytes 24584 | tf_op jit(solution)/shard_map/ppermute | solution.py:445
  90.9 6.4 %collective-permute-start.19 = (bf16[32,128]{1,0:T(8,128)(2,1)S(1)}, bf16[32,128]{1,0:T(8,128)(2,1)S(1)}, u32[]{:S(2)}, u32[]{:S(2)}) collective-permute-start(bf16[32,128]{1,0:T(8,128)(2,1)S(1)} %get-tuple-element.70), channel_id=1, source_target_pairs={{0,60},{4,8},{8,4},{12,16},{16,12},{20,24},{24,20},{28,32},{32,28}... | collective-permute-start | bytes 24584 | tf_op jit(solution)/shard_map/ppermute | solution.py:445
  93.5 4.0 %collective-permute-start.20 = (bf16[32,128]{1,0:T(8,128)(2,1)S(1)}, bf16[32,128]{1,0:T(8,128)(2,1)S(1)}, u32[]{:S(2)}, u32[]{:S(2)}) collective-permute-start(bf16[32,128]{1,0:T(8,128)(2,1)S(1)} %get-tuple-element.71), channel_id=1, source_target_pairs={{0,8},{4,12},{8,0},{12,4},{16,24},{20,28},{24,16},{28,20},{32,40},... | collective-permute-start | bytes 24584 | tf_op jit(solution)/shard_map/ppermute | solution.py:445
  95.8 2.5 %collective-permute-start.21 = (bf16[32,128]{1,0:T(8,128)(2,1)S(1)}, bf16[32,128]{1,0:T(8,128)(2,1)S(1)}, u32[]{:S(2)}, u32[]{:S(2)}) collective-permute-start(bf16[32,128]{1,0:T(8,128)(2,1)S(1)} %get-tuple-element.72), channel_id=1, source_target_pairs={{0,4},{4,0},{8,12},{12,8},{16,20},{20,16},{24,28},{28,24},{32,36},... | collective-permute-start | bytes 24584 | tf_op jit(solution)/shard_map/ppermute | solution.py:445

commit v6 on v5

--- a/solution.py
+++ b/solution.py
@@ -410,8 +410,16 @@
     nearby_ref[...] = turned[:1, :256]
 
 
-def density_kernel(p0, p1, p2, p3, p4, where_ref, y, phi, out_ref, table):
-    slots, probes = where_ref.shape
+def probe_onehot_kernel(where_ref, onehot_ref):
+    def step(k, carry):
+        onehot_ref[k] = onehot_of(where_ref[pl.ds(k, 1), :], onehot_ref.shape[1])
+        return carry
+
+    lax.fori_loop(0, where_ref.shape[0], step, 0, unroll=2)
+
+
+def density_kernel(p0, p1, p2, p3, p4, onehot_ref, y, phi, out_ref, table):
+    slots, _, probes = onehot_ref.shape
     table[160:, :] = jnp.zeros((96, 128), F32)
     table[64:96, :] = p4[...].astype(F32)
     for swap, piece in zip(SWAPS, (p0, p1, p2, p3)):
@@ -420,7 +428,7 @@
     rows_t = table[...].T[:, :160].astype(BF16)
 
     def slot(k, total):
-        picked = dot(rows_t, onehot_of(where_ref[pl.ds(k, 1), :], 160))
+        picked = dot(rows_t, onehot_ref[k])
         part = jnp.zeros((8, probes), F32)
         for m in range(16):
             part = part + spread(y, m * slots + k) * picked[m * 8 : (m + 1) * 8]
@@ -597,11 +605,19 @@
                 ),
                 after=(begin,),
             ),
-            None,
+            lambda made, begin: (
+                call(
+                    probe_onehot_kernel,
+                    shape((slots, 160, probes), BF16),
+                    (made[0][2],),
+                    limit=12,
+                    after=(begin,),
+                ),
+            ),
             None,
         ),
     )
-    probe_y, probe_phi, probe_where, nearby = made[0]
+    probe_y, probe_phi, _, nearby = made[0]
     sent = call(
         brick_kernel,
         [shape((32, 128), BF16)] * 5,
@@ -612,8 +628,9 @@
     density = call(
         density_kernel,
         shape((1, probes), F32),
-        (*pieces, probe_where, probe_y, probe_phi),
+        (*pieces, made[1][0], probe_y, probe_phi),
         [pltpu.VMEM((256, 128), F32)],
+        limit=16,
     )
     return density.reshape(1, 1, 1, probes)
 

time: 102 us -> 102 us (level)
    pallas_call x18 -> x19, Pallas kernels: 31.2 us -> 32 us  [call(): pl.pallas_call(body, out_shape=out_shape, in_specs=[HBM] * first + [VMEM]...]
  transfers between devices with their start and end apart: 22 -> 22, of which waited for: 10 -> 10; matrix products, arithmetic and copies ran while one was open for 0% -> 0% of each run, Pallas kernels for 11% -> 12%
where the time goes in v6:
time: 102 us
  starting transfers between devices  48.6 us (48%)
  Pallas kernels  32 us (31%)
  waiting for transfers between devices  20.7 us (20%)
    ppermute x18, starting transfers between devices, shifted(): lax.ppermute(block, axis, [(i, (i + step) % size) for i in range(size)])  40.5 us
    pallas_call x19, Pallas kernels, call(): pl.pallas_call(body, out_shape=out_shape, in_specs=[HBM] * first + [VMEM]...  32 us
    ppermute x18, waiting for transfers between devices, shifted(): lax.ppermute(block, axis, [(i, (i + step) % size) for i in range(size)])  18.2 us
    ppermute x4, starting transfers between devices, swapped_with(): return lax.ppermute(block, 'gy', sorted(pairs))  8.18 us
    ppermute x4, waiting for transfers between devices, swapped_with(): return lax.ppermute(block, 'gy', sorted(pairs))  2.5 us
  transfers between devices with their start and end apart: 22, of which 10 were waited for; matrix products, arithmetic and copies ran while one was open for 0% of the time, Pallas kernels for 12%

profile of v6, /device:TPU:1, one launch (start us, length us, event | category | flops | bytes accessed | tf_op | source)
XLA Modules:
  0.0 101.7 jit_solution(13991169331445032024)
XLA Ops:
  0.0 0.8 shard_map.181
  0.9 2.1 %collective-permute-start = (f32[8,128]{1,0:T(8,128)S(1)}, f32[8,128]{1,0:T(8,128)S(1)}, u32[]{:S(2)}, u32[]{:S(2)}) collective-permute-start(f32[8,128]{1,0:T(8,128)S(1)} %get-tuple-element.42.refs_3_), channel_id=1, source_target_pairs={{0,64},{64,128},{128,192},{192,0},{1,65},{65,129},{129,193},{193,1... | collective-permute-start | bytes 12296 | tf_op jit(solution)/shard_map/ppermute | solution.py:443
  3.0 1.4 %collective-permute-start.1 = (f32[8,128]{1,0:T(8,128)S(1)}, f32[8,128]{1,0:T(8,128)S(1)}, u32[]{:S(2)}, u32[]{:S(2)}) collective-permute-start(f32[8,128]{1,0:T(8,128)S(1)} %get-tuple-element.42.refs_3_), channel_id=1, source_target_pairs={{0,192},{64,0},{128,64},{192,128},{1,193},{65,1},{129,65},{193,129... | collective-permute-start | bytes 12296 | tf_op jit(solution)/shard_map/ppermute | solution.py:443
  4.3 1.7 %shard_map.182 = (f32[2,1024,128]{2,1,0:T(8,128)S(1)}, f32[2,256,128]{2,1,0:T(8,128)S(1)}, s32[32,256]{1,0:T(8,128)S(1)}) custom-call(f32[3,32,256]{2,1,0:T(8,128)} %bitcast.16, s32[1,256]{1,0:T(1,128)} %bitcast.19, s32[32,256]{1,0:T(8,128)} %bitcast.17, f32[8,128]{1,0:T(8,128)S(1)} %get-tuple-element.42.refs_3_), custom_call_target="tpu_custom_call" | custom-call | bytes 1048576 | tf_op jit(solution)/shard_map/pallas_call | solution.py:40
  6.0 0.0 collective-permute-done.refs_2_.refs_1_
  6.1 0.0 collective-permute-done.1.refs_3_.refs_2_
  6.1 0.1 shard_map.183.refs_7_
  6.2 1.4 %collective-permute-start.2 = (f32[8,128]{1,0:T(8,128)S(1)}, f32[8,128]{1,0:T(8,128)S(1)}, u32[]{:S(2)}, u32[]{:S(2)}) collective-permute-start(f32[8,128]{1,0:T(8,128)S(1)} %shard_map.183.refs_7_), channel_id=1, source_target_pairs={{0,4},{4,8},{8,12},{12,16},{16,20},{20,24},{24,28},{28,32},{32,36}... | collective-permute-start | bytes 12296 | tf_op jit(solution)/shard_map/ppermute | solution.py:443
  7.6 5.6 %collective-permute-start.3 = (f32[8,128]{1,0:T(8,128)S(1)}, f32[8,128]{1,0:T(8,128)S(1)}, u32[]{:S(2)}, u32[]{:S(2)}) collective-permute-start(f32[8,128]{1,0:T(8,128)S(1)} %shard_map.183.refs_7_), channel_id=1, source_target_pairs={{0,60},{4,0},{8,4},{12,8},{16,12},{20,16},{24,20},{28,24},{32,28},... | collective-permute-start | bytes 12296 | tf_op jit(solution)/shard_map/ppermute | solution.py:443
  13.2 3.1 %shard_map.184 = (bf16[32,256,128]{2,1,0:T(8,128)(2,1)S(1)}, bf16[8,128]{1,0:T(8,128)(2,1)S(1)}, bf16[128,512]{1,0:T(8,128)(2,1)S(1)}, bf16[128,512]{1,0:T(8,128)(2,1)S(1)}, f32[8,256,512]{2,1,0:T(8,128)S(1)}) custom-call(bf16[8,64]{1,0:T(8,128)(2,1)} %refs_0_.1, bf16[8,64]{1,0:T(8,128)(2,1)} %refs_1_.1, bf16[64,512]{1,0:T(8,128)(2,1)} %refs_2_.1, ...), custom_call_target="tpu_custom_call" | custom-call | bytes 1048576 | tf_op jit(solution)/shard_map/pallas_call | solution.py:40
  16.3 0.0 collective-permute-done.2.refs_4_.refs_3_
  16.3 0.0 collective-permute-done.3.refs_5_.refs_4_
  16.4 0.1 shard_map.185.refs_2_
  16.5 7.2 %collective-permute-start.4 = (f32[8,128]{1,0:T(8,128)S(1)}, f32[8,128]{1,0:T(8,128)S(1)}, u32[]{:S(2)}, u32[]{:S(2)}) collective-permute-start(f32[8,128]{1,0:T(8,128)S(1)} %shard_map.185.refs_2_), channel_id=1, source_target_pairs={{0,1},{1,2},{2,3},{3,0},{4,5},{5,6},{6,7},{7,4},{8,9},{9,10},{10,1... | collective-permute-start | bytes 12296 | tf_op jit(solution)/shard_map/ppermute | solution.py:443
  23.7 0.0 collective-permute-start.5
  23.7 0.0 copy-start.6
  23.7 2.5 %shard_map.186.refs_10_ = f32[24,256,512]{2,1,0:T(8,128)S(1)} custom-call(bf16[32,256,128]{2,1,0:T(8,128)(2,1)S(1)} %get-tuple-element.48.refs_0_, bf16[128,512]{1,0:T(8,128)(2,1)S(1)} %get-tuple-element.49.refs_1_, f32[8,128]{1,0:T(8,128)S(1)} %shard_map.185.refs_2_), custom_call_target="tpu_custom_call" | custom-call | bytes 1048576 | tf_op jit(solution)/shard_map/pallas_call | solution.py:40
  26.3 0.0 collective-permute-done.4.refs_5_
  26.3 4.4 %collective-permute-done.5.refs_6_ = f32[8,128]{1,0:T(8,128)S(1)} collective-permute-done((f32[8,128]{1,0:T(8,128)S(1)}, f32[8,128]{1,0:T(8,128)S(1)}, u32[]{:S(2)}, u32[]{:S(2)}) %collective-permute-start.5) | collective-permute-done | bytes 4128 | tf_op jit(solution)/shard_map/ppermute | solution.py:443
  30.7 5.7 %shard_map.187 = (bf16[256,128]{1,0:T(8,128)(2,1)S(1)}, bf16[64,128]{1,0:T(8,128)(2,1)S(1)}, bf16[64,128]{1,0:T(8,128)(2,1)S(1)}) custom-call(s32[1,256]{1,0:T(1,128)S(1)} %get-tuple-element.41.refs_0_, f32[8,128]{1,0:T(8,128)S(1)} %collective-permute-done.refs_2_.refs_1_, f32[8,128]{1,0:T(8,128)S(1)} %collective-permute-done.1.refs_3_.refs_2_, ...), custom_call_target="tpu_custom_call" | custom-call | bytes 1048576 | tf_op jit(solution)/shard_map/pallas_call | solution.py:40
  36.4 1.3 %collective-permute-start.6 = (bf16[64,128]{1,0:T(8,128)(2,1)S(1)}, bf16[64,128]{1,0:T(8,128)(2,1)S(1)}, u32[]{:S(2)}, u32[]{:S(2)}) collective-permute-start(bf16[64,128]{1,0:T(8,128)(2,1)S(1)} %get-tuple-element.52), channel_id=1, source_target_pairs={{0,64},{64,128},{128,192},{192,0},{1,65},{65,129},{129,193},{193,1... | collective-permute-start | bytes 49160 | tf_op jit(solution)/shard_map/ppermute | solution.py:443
  37.7 1.6 %collective-permute-start.7 = (bf16[64,128]{1,0:T(8,128)(2,1)S(1)}, bf16[64,128]{1,0:T(8,128)(2,1)S(1)}, u32[]{:S(2)}, u32[]{:S(2)}) collective-permute-start(bf16[64,128]{1,0:T(8,128)(2,1)S(1)} %get-tuple-element.53), channel_id=1, source_target_pairs={{0,192},{64,0},{128,64},{192,128},{1,193},{65,1},{129,65},{193,129... | collective-permute-start | bytes 49160 | tf_op jit(solution)/shard_map/ppermute | solution.py:443
  39.2 0.8 shard_map.188.refs_4_.refs_9_
  40.1 0.2 collective-permute-done.6.refs_2_.refs_1_
  40.3 0.0 collective-permute-done.7.refs_3_.refs_2_
  40.3 0.2 shard_map.189
  40.5 0.3 collective-permute-start.8
  40.7 5.4 %collective-permute-start.9 = (bf16[64,128]{1,0:T(8,128)(2,1)S(1)}, bf16[64,128]{1,0:T(8,128)(2,1)S(1)}, u32[]{:S(2)}, u32[]{:S(2)}) collective-permute-start(bf16[64,128]{1,0:T(8,128)(2,1)S(1)} %get-tuple-element.56), channel_id=1, source_target_pairs={{0,60},{4,0},{8,4},{12,8},{16,12},{20,16},{24,20},{28,24},{32,28},... | collective-permute-start | bytes 49160 | tf_op jit(solution)/shard_map/ppermute | solution.py:443
  46.1 1.7 %shard_map.190.refs_6_.refs_10_ = f32[16,256,512]{2,1,0:T(8,128)S(1)} custom-call(bf16[32,256,128]{2,1,0:T(8,128)(2,1)S(1)} %get-tuple-element.48.refs_0_, bf16[128,512]{1,0:T(8,128)(2,1)S(1)} %get-tuple-element.54.refs_1_, bf16[64,128]{1,0:T(8,128)(2,1)S(1)} %get-tuple-element.55.refs_2_), custom_call_target="tpu_custom_call" | custom-call | bytes 1048576 | tf_op jit(solution)/shard_map/pallas_call | solution.py:40
  47.8 0.0 copy-start.5
  47.8 0.0 collective-permute-done.8.refs_4_.refs_3_
  47.8 0.0 collective-permute-done.9.refs_5_.refs_4_
  47.8 0.2 shard_map.191
  48.1 3.3 %collective-permute-start.10 = (bf16[64,128]{1,0:T(8,128)(2,1)S(1)}, bf16[64,128]{1,0:T(8,128)(2,1)S(1)}, u32[]{:S(2)}, u32[]{:S(2)}) collective-permute-start(bf16[64,128]{1,0:T(8,128)(2,1)S(1)} %get-tuple-element.57.refs_3_), channel_id=1, source_target_pairs={{0,1},{1,2},{2,3},{3,0},{4,5},{5,6},{6,7},{7,4},{8,9},{9,10},{10,1... | collective-permute-start | bytes 49160 | tf_op jit(solution)/shard_map/ppermute | solution.py:443
  51.4 0.0 collective-permute-start.11
  51.4 1.1 %shard_map.192 = (f32[8,256,512]{2,1,0:T(8,128)S(1)}, bf16[2048,128]{1,0:T(8,128)(2,1)S(1)}) custom-call(bf16[32,256,128]{2,1,0:T(8,128)(2,1)S(1)} %get-tuple-element.48.refs_0_, bf16[128,512]{1,0:T(8,128)(2,1)S(1)} %get-tuple-element.54.refs_1_, bf16[4,8,128]{2,1,0:T(8,128)(2,1)S(1)} %bitcast.13, bf16[64,128]{1,0:T(8,128)(2,1)S(1)} %get-tuple-element.57.refs_3_), custom_call_target="tpu_custom_call" | custom-call | bytes 1048576 | tf_op jit(solution)/shard_map/pallas_call | solution.py:40
  52.5 0.0 collective-permute-done.10.refs_5_
  52.5 6.0 %collective-permute-done.11.refs_6_ = bf16[64,128]{1,0:T(8,128)(2,1)S(1)} collective-permute-done((bf16[64,128]{1,0:T(8,128)(2,1)S(1)}, bf16[64,128]{1,0:T(8,128)(2,1)S(1)}, u32[]{:S(2)}, u32[]{:S(2)}) %collective-permute-start.11) | collective-permute-done | bytes 16416 | tf_op jit(solution)/shard_map/ppermute | solution.py:443
  58.5 8.2 %shard_map.193 = (bf16[256,128]{1,0:T(8,128)(2,1)S(1)}, bf16[64,128]{1,0:T(8,128)(2,1)S(1)}, bf16[64,128]{1,0:T(8,128)(2,1)S(1)}) custom-call(bf16[256,128]{1,0:T(8,128)(2,1)S(1)} %get-tuple-element.51.refs_2_.refs_1_.refs_0_, bf16[64,128]{1,0:T(8,128)(2,1)S(1)} %collective-permute-done.6.refs_2_.refs_1_, ...), custom_call_target="tpu_custom_call" | custom-call | bytes 1048576 | tf_op jit(solution)/shard_map/pallas_call | solution.py:40
  66.7 1.0 collective-permute-start.12
  67.7 1.9 %collective-permute-start.13 = (bf16[64,128]{1,0:T(8,128)(2,1)S(1)}, bf16[64,128]{1,0:T(8,128)(2,1)S(1)}, u32[]{:S(2)}, u32[]{:S(2)}) collective-permute-start(bf16[64,128]{1,0:T(8,128)(2,1)S(1)} %get-tuple-element.64), channel_id=1, source_target_pairs={{0,192},{64,0},{128,64},{192,128},{1,193},{65,1},{129,65},{193,129... | collective-permute-start | bytes 49160 | tf_op jit(solution)/shard_map/ppermute | solution.py:443
  69.6 0.6 shard_map.194
  70.2 0.4 collective-permute-done.12.refs_2_
  70.6 0.0 collective-permute-done.13.refs_3_
  70.6 0.2 shard_map.195
  70.8 0.1 collective-permute-start.14
  70.9 5.7 %collective-permute-start.15 = (bf16[64,128]{1,0:T(8,128)(2,1)S(1)}, bf16[64,128]{1,0:T(8,128)(2,1)S(1)}, u32[]{:S(2)}, u32[]{:S(2)}) collective-permute-start(bf16[64,128]{1,0:T(8,128)(2,1)S(1)} %get-tuple-element.66), channel_id=1, source_target_pairs={{0,60},{4,0},{8,4},{12,8},{16,12},{20,16},{24,20},{28,24},{32,28},... | collective-permute-start | bytes 49160 | tf_op jit(solution)/shard_map/ppermute | solution.py:443
  76.6 0.9 shard_map.196.refs_6_.refs_5_
  77.5 0.1 collective-permute-done.14.refs_4_
  77.6 0.2 shard_map.197
  77.9 2.4 %collective-permute-start.16 = (bf16[64,128]{1,0:T(8,128)(2,1)S(1)}, bf16[64,128]{1,0:T(8,128)(2,1)S(1)}, u32[]{:S(2)}, u32[]{:S(2)}) collective-permute-start(bf16[64,128]{1,0:T(8,128)(2,1)S(1)} %get-tuple-element.68), channel_id=1, source_target_pairs={{0,1},{1,2},{2,3},{3,0},{4,5},{5,6},{6,7},{7,4},{8,9},{9,10},{10,1... | collective-permute-start | bytes 49160 | tf_op jit(solution)/shard_map/ppermute | solution.py:443
  80.2 0.0 collective-permute-start.17
  80.2 0.9 collective-permute-done.16.refs_6_
  81.1 6.2 %collective-permute-done.17.refs_7_ = bf16[64,128]{1,0:T(8,128)(2,1)S(1)} collective-permute-done((bf16[64,128]{1,0:T(8,128)(2,1)S(1)}, bf16[64,128]{1,0:T(8,128)(2,1)S(1)}, u32[]{:S(2)}, u32[]{:S(2)}) %collective-permute-start.17) | collective-permute-done | bytes 16416 | tf_op jit(solution)/shard_map/ppermute | solution.py:443
  87.3 0.3 shard_map.198
  87.6 3.3 %collective-permute-start.18 = (bf16[32,128]{1,0:T(8,128)(2,1)S(1)}, bf16[32,128]{1,0:T(8,128)(2,1)S(1)}, u32[]{:S(2)}, u32[]{:S(2)}) collective-permute-start(bf16[32,128]{1,0:T(8,128)(2,1)S(1)} %get-tuple-element.70), channel_id=1, source_target_pairs={{0,56},{4,60},{8,16},{12,20},{16,8},{20,12},{24,32},{28,36},{32,24... | collective-permute-start | bytes 24584 | tf_op jit(solution)/shard_map/ppermute | solution.py:453
  90.9 2.6 %collective-permute-start.19 = (bf16[32,128]{1,0:T(8,128)(2,1)S(1)}, bf16[32,128]{1,0:T(8,128)(2,1)S(1)}, u32[]{:S(2)}, u32[]{:S(2)}) collective-permute-start(bf16[32,128]{1,0:T(8,128)(2,1)S(1)} %get-tuple-element.71), channel_id=1, source_target_pairs={{0,60},{4,8},{8,4},{12,16},{16,12},{20,24},{24,20},{28,32},{32,28}... | collective-permute-start | bytes 24584 | tf_op jit(solution)/shard_map/ppermute | solution.py:453
  93.5 2.3 %collective-permute-start.20 = (bf16[32,128]{1,0:T(8,128)(2,1)S(1)}, bf16[32,128]{1,0:T(8,128)(2,1)S(1)}, u32[]{:S(2)}, u32[]{:S(2)}) collective-permute-start(bf16[32,128]{1,0:T(8,128)(2,1)S(1)} %get-tuple-element.72), channel_id=1, source_target_pairs={{0,8},{4,12},{8,0},{12,4},{16,24},{20,28},{24,16},{28,20},{32,40},... | collective-permute-start | bytes 24584 | tf_op jit(solution)/shard_map/ppermute | solution.py:453
  95.8 0.0 collective-permute-start.21
  95.8 0.0 collective-permute-done.18.refs_0_
  95.8 1.5 %collective-permute-done.19.refs_1_ = bf16[32,128]{1,0:T(8,128)(2,1)S(1)} collective-permute-done((bf16[32,128]{1,0:T(8,128)(2,1)S(1)}, bf16[32,128]{1,0:T(8,128)(2,1)S(1)}, u32[]{:S(2)}, u32[]{:S(2)}) %collective-permute-start.19) | collective-permute-done | bytes 8224 | tf_op jit(solution)/shard_map/ppermute | solution.py:453
  97.3 0.2 collective-permute-done.20.refs_2_
  97.5 0.8 collective-permute-done.21.refs_3_
  98.3 3.4 %shard_map.199 = f32[1,512]{1,0:T(1,128)} custom-call(bf16[32,128]{1,0:T(8,128)(2,1)S(1)} %collective-permute-done.18.refs_0_, bf16[32,128]{1,0:T(8,128)(2,1)S(1)} %collective-permute-done.19.refs_1_, bf16[32,128]{1,0:T(8,128)(2,1)S(1)} %collective-permute-done.20.refs_2_, bf16[32,128]{1,0:T(8,128)(2,1)S(1)} %collective-permute-done.21.refs_3_, ...), custom_call_target="tpu_custom_call" | custom-call | bytes 1048576 | tf_op jit(solution)/shard_map/pallas_call | solution.py:40
  (17 shorter events, 0.0 us)
Async XLA Ops:
  0.9 5.2 %collective-permute-start = (f32[8,128]{1,0:T(8,128)S(1)}, f32[8,128]{1,0:T(8,128)S(1)}, u32[]{:S(2)}, u32[]{:S(2)}) collective-permute-start(f32[8,128]{1,0:T(8,128)S(1)} %get-tuple-element.42.refs_3_), channel_id=1, source_target_pairs={{0,64},{64,128},{128,192},{192,0},{1,65},{65,129},{129,193},{193,1... | collective-permute-start | bytes 12296 | tf_op jit(solution)/shard_map/ppermute | solution.py:443
  3.0 3.1 %collective-permute-start.1 = (f32[8,128]{1,0:T(8,128)S(1)}, f32[8,128]{1,0:T(8,128)S(1)}, u32[]{:S(2)}, u32[]{:S(2)}) collective-permute-start(f32[8,128]{1,0:T(8,128)S(1)} %get-tuple-element.42.refs_3_), channel_id=1, source_target_pairs={{0,192},{64,0},{128,64},{192,128},{1,193},{65,1},{129,65},{193,129... | collective-permute-start | bytes 12296 | tf_op jit(solution)/shard_map/ppermute | solution.py:443
  6.2 10.1 %collective-permute-start.2 = (f32[8,128]{1,0:T(8,128)S(1)}, f32[8,128]{1,0:T(8,128)S(1)}, u32[]{:S(2)}, u32[]{:S(2)}) collective-permute-start(f32[8,128]{1,0:T(8,128)S(1)} %shard_map.183.refs_7_), channel_id=1, source_target_pairs={{0,4},{4,8},{8,12},{12,16},{16,20},{20,24},{24,28},{28,32},{32,36}... | collective-permute-start | bytes 12296 | tf_op jit(solution)/shard_map/ppermute | solution.py:443
  7.6 8.7 %collective-permute-start.3 = (f32[8,128]{1,0:T(8,128)S(1)}, f32[8,128]{1,0:T(8,128)S(1)}, u32[]{:S(2)}, u32[]{:S(2)}) collective-permute-start(f32[8,128]{1,0:T(8,128)S(1)} %shard_map.183.refs_7_), channel_id=1, source_target_pairs={{0,60},{4,0},{8,4},{12,8},{16,12},{20,16},{24,20},{28,24},{32,28},... | collective-permute-start | bytes 12296 | tf_op jit(solution)/shard_map/ppermute | solution.py:443
  16.5 9.8 %collective-permute-start.4 = (f32[8,128]{1,0:T(8,128)S(1)}, f32[8,128]{1,0:T(8,128)S(1)}, u32[]{:S(2)}, u32[]{:S(2)}) collective-permute-start(f32[8,128]{1,0:T(8,128)S(1)} %shard_map.185.refs_2_), channel_id=1, source_target_pairs={{0,1},{1,2},{2,3},{3,0},{4,5},{5,6},{6,7},{7,4},{8,9},{9,10},{10,1... | collective-permute-start | bytes 12296 | tf_op jit(solution)/shard_map/ppermute | solution.py:443
  23.7 6.9 %collective-permute-start.5 = (f32[8,128]{1,0:T(8,128)S(1)}, f32[8,128]{1,0:T(8,128)S(1)}, u32[]{:S(2)}, u32[]{:S(2)}) collective-permute-start(f32[8,128]{1,0:T(8,128)S(1)} %shard_map.185.refs_2_), channel_id=1, source_target_pairs={{0,3},{1,0},{2,1},{3,2},{4,7},{5,4},{6,5},{7,6},{8,11},{9,8},{10,9... | collective-permute-start | bytes 12296 | tf_op jit(solution)/shard_map/ppermute | solution.py:443
  23.7 6.9 %copy-start.1 = (bf16[512,128]{1,0:T(8,128)(2,1)S(1)}, bf16[512,128]{1,0:T(8,128)(2,1)}, u32[]{:S(2)}) copy-start(bf16[512,128]{1,0:T(8,128)(2,1)} %refs_14_.1) | copy-start | bytes 393220
  23.7 6.9 %copy-start.3 = (bf16[128,128]{1,0:T(8,128)(2,1)S(1)}, bf16[128,128]{1,0:T(8,128)(2,1)}, u32[]{:S(2)}) copy-start(bf16[128,128]{1,0:T(8,128)(2,1)} %refs_13_.1) | copy-start | bytes 98308
  23.7 6.9 %copy-start.4 = (bf16[128,128]{1,0:T(8,128)(2,1)S(1)}, bf16[128,128]{1,0:T(8,128)(2,1)}, u32[]{:S(2)}) copy-start(bf16[128,128]{1,0:T(8,128)(2,1)} %refs_15_.1) | copy-start | bytes 98308
  23.7 6.9 %copy-start.6 = (bf16[8,128]{1,0:T(8,128)(2,1)S(1)}, bf16[8,128]{1,0:T(8,128)(2,1)}, u32[]{:S(2)}) copy-start(bf16[8,128]{1,0:T(8,128)(2,1)} %refs_12_.1) | copy-start | bytes 6148
  36.4 3.9 %collective-permute-start.6 = (bf16[64,128]{1,0:T(8,128)(2,1)S(1)}, bf16[64,128]{1,0:T(8,128)(2,1)S(1)}, u32[]{:S(2)}, u32[]{:S(2)}) collective-permute-start(bf16[64,128]{1,0:T(8,128)(2,1)S(1)} %get-tuple-element.52), channel_id=1, source_target_pairs={{0,64},{64,128},{128,192},{192,0},{1,65},{65,129},{129,193},{193,1... | collective-permute-start | bytes 49160 | tf_op jit(solution)/shard_map/ppermute | solution.py:443
  37.7 2.6 %collective-permute-start.7 = (bf16[64,128]{1,0:T(8,128)(2,1)S(1)}, bf16[64,128]{1,0:T(8,128)(2,1)S(1)}, u32[]{:S(2)}, u32[]{:S(2)}) collective-permute-start(bf16[64,128]{1,0:T(8,128)(2,1)S(1)} %get-tuple-element.53), channel_id=1, source_target_pairs={{0,192},{64,0},{128,64},{192,128},{1,193},{65,1},{129,65},{193,129... | collective-permute-start | bytes 49160 | tf_op jit(solution)/shard_map/ppermute | solution.py:443
  40.5 7.3 %collective-permute-start.8 = (bf16[64,128]{1,0:T(8,128)(2,1)S(1)}, bf16[64,128]{1,0:T(8,128)(2,1)S(1)}, u32[]{:S(2)}, u32[]{:S(2)}) collective-permute-start(bf16[64,128]{1,0:T(8,128)(2,1)S(1)} %get-tuple-element.55.refs_2_), channel_id=1, source_target_pairs={{0,4},{4,8},{8,12},{12,16},{16,20},{20,24},{24,28},{28,32},{32,36}... | collective-permute-start | bytes 49160 | tf_op jit(solution)/shard_map/ppermute | solution.py:443
  40.7 7.1 %collective-permute-start.9 = (bf16[64,128]{1,0:T(8,128)(2,1)S(1)}, bf16[64,128]{1,0:T(8,128)(2,1)S(1)}, u32[]{:S(2)}, u32[]{:S(2)}) collective-permute-start(bf16[64,128]{1,0:T(8,128)(2,1)S(1)} %get-tuple-element.56), channel_id=1, source_target_pairs={{0,60},{4,0},{8,4},{12,8},{16,12},{20,16},{24,20},{28,24},{32,28},... | collective-permute-start | bytes 49160 | tf_op jit(solution)/shard_map/ppermute | solution.py:443
  47.8 3.6 %copy-start.5 = (bf16[4,128,8]{1,2,0:T(8,128)(2,1)S(1)}, bf16[4,128,8]{1,2,0:T(8,128)(2,1)}, u32[]{:S(2)}) copy-start(bf16[4,128,8]{1,2,0:T(8,128)(2,1)} %param.37) | copy-start | bytes 24580
  48.1 4.4 %collective-permute-start.10 = (bf16[64,128]{1,0:T(8,128)(2,1)S(1)}, bf16[64,128]{1,0:T(8,128)(2,1)S(1)}, u32[]{:S(2)}, u32[]{:S(2)}) collective-permute-start(bf16[64,128]{1,0:T(8,128)(2,1)S(1)} %get-tuple-element.57.refs_3_), channel_id=1, source_target_pairs={{0,1},{1,2},{2,3},{3,0},{4,5},{5,6},{6,7},{7,4},{8,9},{9,10},{10,1... | collective-permute-start | bytes 49160 | tf_op jit(solution)/shard_map/ppermute | solution.py:443
  51.4 7.1 %collective-permute-start.11 = (bf16[64,128]{1,0:T(8,128)(2,1)S(1)}, bf16[64,128]{1,0:T(8,128)(2,1)S(1)}, u32[]{:S(2)}, u32[]{:S(2)}) collective-permute-start(bf16[64,128]{1,0:T(8,128)(2,1)S(1)} %get-tuple-element.58), channel_id=1, source_target_pairs={{0,3},{1,0},{2,1},{3,2},{4,7},{5,4},{6,5},{7,6},{8,11},{9,8},{10,9... | collective-permute-start | bytes 49160 | tf_op jit(solution)/shard_map/ppermute | solution.py:443
  58.5 11.1 %copy-start = (f32[1,1,1,3,32,512]{5,4,3,2,1,0:T(8,128)S(1)}, f32[1,1,1,3,32,512]{5,4,3,2,1,0:T(8,128)}, u32[]{:S(2)}) copy-start(f32[1,1,1,3,32,512]{5,4,3,2,1,0:T(8,128)} %param.27) | copy-start | bytes 589828
  58.5 11.1 %copy-start.2 = (s32[1,1,1,32,512]{4,3,2,1,0:T(8,128)S(1)}, s32[1,1,1,32,512]{4,3,2,1,0:T(8,128)}, u32[]{:S(2)}) copy-start(s32[1,1,1,32,512]{4,3,2,1,0:T(8,128)} %param.25) | copy-start | bytes 196612
  58.5 11.1 %copy-start.7 = (s32[1,1,1,512]{3,2,1,0:T(1,128)S(1)}, s32[1,1,1,512]{3,2,1,0:T(1,128)}, u32[]{:S(2)}) copy-start(s32[1,1,1,512]{3,2,1,0:T(1,128)} %param.24) | copy-start | bytes 6148
  58.5 11.1 %copy-start.8 = (s32[1,1,1,512]{3,2,1,0:T(1,128)S(1)}, s32[1,1,1,512]{3,2,1,0:T(1,128)}, u32[]{:S(2)}) copy-start(s32[1,1,1,512]{3,2,1,0:T(1,128)} %param.26) | copy-start | bytes 6148
  66.7 3.9 %collective-permute-start.12 = (bf16[64,128]{1,0:T(8,128)(2,1)S(1)}, bf16[64,128]{1,0:T(8,128)(2,1)S(1)}, u32[]{:S(2)}, u32[]{:S(2)}) collective-permute-start(bf16[64,128]{1,0:T(8,128)(2,1)S(1)} %get-tuple-element.63), channel_id=1, source_target_pairs={{0,64},{64,128},{128,192},{192,0},{1,65},{65,129},{129,193},{193,1... | collective-permute-start | bytes 49160 | tf_op jit(solution)/shard_map/ppermute | solution.py:443
  67.7 2.9 %collective-permute-start.13 = (bf16[64,128]{1,0:T(8,128)(2,1)S(1)}, bf16[64,128]{1,0:T(8,128)(2,1)S(1)}, u32[]{:S(2)}, u32[]{:S(2)}) collective-permute-start(bf16[64,128]{1,0:T(8,128)(2,1)S(1)} %get-tuple-element.64), channel_id=1, source_target_pairs={{0,192},{64,0},{128,64},{192,128},{1,193},{65,1},{129,65},{193,129... | collective-permute-start | bytes 49160 | tf_op jit(solution)/shard_map/ppermute | solution.py:443
  70.8 6.8 %collective-permute-start.14 = (bf16[64,128]{1,0:T(8,128)(2,1)S(1)}, bf16[64,128]{1,0:T(8,128)(2,1)S(1)}, u32[]{:S(2)}, u32[]{:S(2)}) collective-permute-start(bf16[64,128]{1,0:T(8,128)(2,1)S(1)} %get-tuple-element.65.refs_1_), channel_id=1, source_target_pairs={{0,4},{4,8},{8,12},{12,16},{16,20},{20,24},{24,28},{28,32},{32,36}... | collective-permute-start | bytes 49160 | tf_op jit(solution)/shard_map/ppermute | solution.py:443
  70.9 6.7 %collective-permute-start.15 = (bf16[64,128]{1,0:T(8,128)(2,1)S(1)}, bf16[64,128]{1,0:T(8,128)(2,1)S(1)}, u32[]{:S(2)}, u32[]{:S(2)}) collective-permute-start(bf16[64,128]{1,0:T(8,128)(2,1)S(1)} %get-tuple-element.66), channel_id=1, source_target_pairs={{0,60},{4,0},{8,4},{12,8},{16,12},{20,16},{24,20},{28,24},{32,28},... | collective-permute-start | bytes 49160 | tf_op jit(solution)/shard_map/ppermute | solution.py:443
  77.9 3.2 %collective-permute-start.16 = (bf16[64,128]{1,0:T(8,128)(2,1)S(1)}, bf16[64,128]{1,0:T(8,128)(2,1)S(1)}, u32[]{:S(2)}, u32[]{:S(2)}) collective-permute-start(bf16[64,128]{1,0:T(8,128)(2,1)S(1)} %get-tuple-element.68), channel_id=1, source_target_pairs={{0,1},{1,2},{2,3},{3,0},{4,5},{5,6},{6,7},{7,4},{8,9},{9,10},{10,1... | collective-permute-start | bytes 49160 | tf_op jit(solution)/shard_map/ppermute | solution.py:443
  80.2 7.1 %collective-permute-start.17 = (bf16[64,128]{1,0:T(8,128)(2,1)S(1)}, bf16[64,128]{1,0:T(8,128)(2,1)S(1)}, u32[]{:S(2)}, u32[]{:S(2)}) collective-permute-start(bf16[64,128]{1,0:T(8,128)(2,1)S(1)} %get-tuple-element.69), channel_id=1, source_target_pairs={{0,3},{1,0},{2,1},{3,2},{4,7},{5,4},{6,5},{7,6},{8,11},{9,8},{10,9... | collective-permute-start | bytes 49160 | tf_op jit(solution)/shard_map/ppermute | solution.py:443
  87.6 8.2 %collective-permute-start.18 = (bf16[32,128]{1,0:T(8,128)(2,1)S(1)}, bf16[32,128]{1,0:T(8,128)(2,1)S(1)}, u32[]{:S(2)}, u32[]{:S(2)}) collective-permute-start(bf16[32,128]{1,0:T(8,128)(2,1)S(1)} %get-tuple-element.70), channel_id=1, source_target_pairs={{0,56},{4,60},{8,16},{12,20},{16,8},{20,12},{24,32},{28,36},{32,24... | collective-permute-start | bytes 24584 | tf_op jit(solution)/shard_map/ppermute | solution.py:453
  90.9 6.4 %collective-permute-start.19 = (bf16[32,128]{1,0:T(8,128)(2,1)S(1)}, bf16[32,128]{1,0:T(8,128)(2,1)S(1)}, u32[]{:S(2)}, u32[]{:S(2)}) collective-permute-start(bf16[32,128]{1,0:T(8,128)(2,1)S(1)} %get-tuple-element.71), channel_id=1, source_target_pairs={{0,60},{4,8},{8,4},{12,16},{16,12},{20,24},{24,20},{28,32},{32,28}... | collective-permute-start | bytes 24584 | tf_op jit(solution)/shard_map/ppermute | solution.py:453
  93.5 4.0 %collective-permute-start.20 = (bf16[32,128]{1,0:T(8,128)(2,1)S(1)}, bf16[32,128]{1,0:T(8,128)(2,1)S(1)}, u32[]{:S(2)}, u32[]{:S(2)}) collective-permute-start(bf16[32,128]{1,0:T(8,128)(2,1)S(1)} %get-tuple-element.72), channel_id=1, source_target_pairs={{0,8},{4,12},{8,0},{12,4},{16,24},{20,28},{24,16},{28,20},{32,40},... | collective-permute-start | bytes 24584 | tf_op jit(solution)/shard_map/ppermute | solution.py:453
  95.8 2.5 %collective-permute-start.21 = (bf16[32,128]{1,0:T(8,128)(2,1)S(1)}, bf16[32,128]{1,0:T(8,128)(2,1)S(1)}, u32[]{:S(2)}, u32[]{:S(2)}) collective-permute-start(bf16[32,128]{1,0:T(8,128)(2,1)S(1)} %get-tuple-element.73), channel_id=1, source_target_pairs={{0,4},{4,0},{8,12},{12,8},{16,20},{20,16},{24,28},{28,24},{32,36},... | collective-permute-start | bytes 24584 | tf_op jit(solution)/shard_map/ppermute | solution.py:453
